TPU v7x, 32 devices: a whole 2x2x4 slice. The times are simulated.
32 devices in a mesh: seq: 4 (over y, x), batch: 8 (over z, core).
Axes of the slice: x: 2, y: 2, z: 4, core: 2. Of those that a mesh axis runs over, the one named last changes fastest.
Arguments:
- tokens: bfloat16 [8, 1024, 2048], P('batch', 'seq'), may hold values from -6 to 6
- cotangent: bfloat16 [8, 1024, 2048], P('batch', 'seq'), may hold values from -6 to 6
- segment_ids: int32 [8, 1024], P('batch'), may hold values from 0 to 3, never falling along the last dimension, each value on 1 to 512 neighbouring positions
- exit_mask: int32 [8, 8], P('batch', 'seq'), may hold values 0 or 1
- ln1_gain: bfloat16 [2048], P(('seq', 'batch')), may hold values from 0.099609375 to 1.8984375
- ln1_bias: bfloat16 [2048], P(('seq', 'batch')), may hold values from -3 to 3
- w_qkv: bfloat16 [2048, 6144], P(('seq', 'batch')), may hold values from -0.125 to 0.125
- b_qv: bfloat16 [4096], P(('seq', 'batch')), may hold values from -3 to 3
- w_out: bfloat16 [2048, 2048], P(('seq', 'batch')), may hold values from -2 to 2
- b_out: bfloat16 [2048], P(('seq', 'batch')), may hold values from -3 to 3
- ln2_gain: bfloat16 [2048], P(('seq', 'batch')), may hold values from 0.099609375 to 1.8984375
- ln2_bias: bfloat16 [2048], P(('seq', 'batch')), may hold values from -3 to 3
- w_up: bfloat16 [8192, 2048], P(('seq', 'batch')), may hold values from -0.125 to 0.125
- b_up: bfloat16 [8192], P(('seq', 'batch')), may hold values from -3 to 3
- w_down: bfloat16 [8192, 2048], P(('seq', 'batch')), may hold values from -0.09375 to 0.09375
- b_down: bfloat16 [2048], P(('seq', 'batch')), may hold values from -3 to 3
Outputs:
- layer_out: bfloat16 [8, 1024, 2048], P('batch', 'seq')
- input_grad: float32 [8, 1024, 2048], P('batch', 'seq')
- grad_ln1_gain: float32 [2048], P(('seq', 'batch'))
- grad_ln1_bias: float32 [2048], P(('seq', 'batch'))
- grad_w_qkv: float32 [2048, 6144], P(('seq', 'batch'))
- grad_b_qv: float32 [4096], P(('seq', 'batch'))
- grad_w_out: float32 [2048, 2048], P(('seq', 'batch'))
- grad_b_out: float32 [2048], P(('seq', 'batch'))
- grad_ln2_gain: float32 [2048], P(('seq', 'batch'))
- grad_ln2_bias: float32 [2048], P(('seq', 'batch'))
- grad_w_up: float32 [8192, 2048], P(('seq', 'batch'))
- grad_b_up: float32 [8192], P(('seq', 'batch'))
- grad_w_down: float32 [8192, 2048], P(('seq', 'batch'))
- grad_b_down: float32 [2048], P(('seq', 'batch'))
All inputs are finite; a program needn't handle non-finite values. No bound on the sum of `exit_mask` on one device may be relied on, other than what follows from the above.
Results may differ from a plain program's by a relative error of at most 0.012.
Values may be sent and summed in bfloat16 or wider, within the bound.
No kernel may reach another device: no remote copies, remote signals or barrier semaphores. Data moves between devices by JAX's collectives and lax.ppermute only.
A program may use at most 512 MiB of HBM per device.

v0:
```python
import jax
import jax.numpy as jnp
from jax import lax
from jax.sharding import PartitionSpec as P

HEADS = 32
HEAD_DIM = 64
TILE = 128


EPSILON = 1e-05
GELU_C = 0.7978845608028654
GELU_K = 0.044715


def smooth_unit(values):
    return jax.nn.gelu(values, approximate=True)


def smooth_slope(values):
    inner = GELU_C * (values + GELU_K * values * values * values)
    tangent = jnp.tanh(inner)
    return 0.5 * (1.0 + tangent) + 0.5 * values * (1.0 - tangent * tangent) * GELU_C * (
        1.0 + 3.0 * GELU_K * values * values
    )


def norm_forward(values, gain, shift):
    centre = jnp.mean(values, axis=-1, keepdims=True)
    centred = values - centre
    spread = jnp.mean(centred * centred, axis=-1, keepdims=True)
    inverse = lax.rsqrt(spread + EPSILON)
    normed = centred * inverse
    return (normed * gain + shift, normed, inverse)


def norm_backward(upstream, normed, inverse, gain):
    graded = upstream * gain
    first = jnp.mean(graded, axis=-1, keepdims=True)
    second = jnp.mean(graded * normed, axis=-1, keepdims=True)
    return (
        inverse * (graded - first - normed * second),
        jnp.sum(upstream * normed, axis=0),
        jnp.sum(upstream, axis=0),
    )


def product(left, right):
    return jnp.dot(left, right, preferred_element_type=jnp.float32)


def product_t(left, right):
    return lax.dot_general(
        left, right, (((1,), (1,)), ((), ())), preferred_element_type=jnp.float32
    )


def product_rows(left, right):
    return lax.dot_general(
        left, right, (((0,), (0,)), ((), ())), preferred_element_type=jnp.float32
    )


def allowed_mask(segment_row, q_start, q_count, k_start, k_count):
    q_pos = q_start + jnp.arange(q_count, dtype=jnp.int32)
    k_pos = k_start + jnp.arange(k_count, dtype=jnp.int32)
    q_seg = lax.dynamic_slice_in_dim(segment_row, q_start, q_count)
    k_seg = lax.dynamic_slice_in_dim(segment_row, k_start, k_count)
    return (k_pos[None, :] <= q_pos[:, None]) & (k_seg[None, :] == q_seg[:, None])


def head_scores(q_heads, k_block):
    return jnp.einsum(
        "qhd,khd->hqk", q_heads, k_block, preferred_element_type=jnp.float32
    ) * HEAD_DIM ** (-0.5)


def split_heads(queries, keys_all, values_all):
    q_count = queries.shape[0]
    length = keys_all.shape[0]
    k_count = min(512, length)
    n_blocks = length // k_count
    q_heads = queries.reshape(q_count, HEADS, HEAD_DIM)
    k_heads = keys_all.reshape(n_blocks, k_count, HEADS, HEAD_DIM)
    v_heads = values_all.reshape(n_blocks, k_count, HEADS, HEAD_DIM)
    k_starts = jnp.arange(n_blocks, dtype=jnp.int32) * k_count
    return (q_heads, k_heads, v_heads, k_starts)


def weights_of(q_heads, k_block, segment_row, q_start, k_start, logsum):
    allowed = allowed_mask(segment_row, q_start, q_heads.shape[0], k_start, k_block.shape[0])[None]
    return jnp.where(allowed, jnp.exp(head_scores(q_heads, k_block) - logsum[..., None]), 0.0)


def attend_forward(q_heads, k_heads, v_heads, k_starts, segment_row, q_start):
    q_count = q_heads.shape[0]
    k_count = k_heads.shape[1]

    def stats(carry, members):
        peak, total = carry
        k_block, k_start = members
        allowed = allowed_mask(segment_row, q_start, q_count, k_start, k_count)[None]
        masked = jnp.where(allowed, head_scores(q_heads, k_block), -1e30)
        fresh = jnp.maximum(peak, jnp.max(masked, axis=-1))
        added = jnp.sum(jnp.where(allowed, jnp.exp(masked - fresh[..., None]), 0.0), axis=-1)
        return ((fresh, total * jnp.exp(peak - fresh) + added), None)

    start_stats = (
        jnp.full((HEADS, q_count), -1e30, jnp.float32),
        jnp.zeros((HEADS, q_count), jnp.float32),
    )
    (peak, total), unused = lax.scan(stats, start_stats, (k_heads, k_starts))
    logsum = peak + jnp.log(total)

    def collect(acc, members):
        k_block, v_block, k_start = members
        probs_low = weights_of(q_heads, k_block, segment_row, q_start, k_start, logsum).astype(
            jnp.bfloat16
        )
        return (
            acc
            + jnp.einsum("hqk,khd->qhd", probs_low, v_block, preferred_element_type=jnp.float32),
            None,
        )

    mixed, unused = lax.scan(
        collect, jnp.zeros((q_count, HEADS, HEAD_DIM), jnp.float32), (k_heads, v_heads, k_starts)
    )
    return (mixed.reshape(q_count, HEADS * HEAD_DIM), logsum)


def attend_backward(q_heads, k_heads, v_heads, k_starts, segment_row, q_start, logsum, grad_mixed):
    q_count = q_heads.shape[0]
    d_heads = grad_mixed.reshape(q_count, HEADS, HEAD_DIM)

    def first(acc, members):
        k_block, v_block, k_start = members
        probs = weights_of(q_heads, k_block, segment_row, q_start, k_start, logsum)
        d_probs = jnp.einsum("qhd,khd->hqk", d_heads, v_block, preferred_element_type=jnp.float32)
        return (acc + jnp.sum(probs * d_probs, axis=-1), None)

    delta, unused = lax.scan(
        first, jnp.zeros((HEADS, q_count), jnp.float32), (k_heads, v_heads, k_starts)
    )

    def second(acc, members):
        k_block, v_block, k_start = members
        probs = weights_of(q_heads, k_block, segment_row, q_start, k_start, logsum)
        d_probs = jnp.einsum("qhd,khd->hqk", d_heads, v_block, preferred_element_type=jnp.float32)
        d_scores = (probs * (d_probs - delta[..., None])).astype(jnp.bfloat16)
        acc = acc + jnp.einsum(
            "hqk,khd->qhd", d_scores, k_block, preferred_element_type=jnp.float32
        ) * HEAD_DIM ** (-0.5)
        d_keys = jnp.einsum(
            "hqk,qhd->khd", d_scores, q_heads, preferred_element_type=jnp.float32
        ) * HEAD_DIM ** (-0.5)
        d_values = jnp.einsum(
            "hqk,qhd->khd", probs.astype(jnp.bfloat16), d_heads, preferred_element_type=jnp.float32
        )
        return (acc, (d_keys, d_values))

    d_query, (d_keys, d_values) = lax.scan(
        second, jnp.zeros((q_count, HEADS, HEAD_DIM), jnp.float32), (k_heads, v_heads, k_starts)
    )
    length = k_heads.shape[0] * k_heads.shape[1]
    return (d_query.reshape(q_count, -1), d_keys.reshape(length, -1), d_values.reshape(length, -1))


def shards(
    tokens,
    cotangent,
    segment_ids,
    exit_mask,
    ln1_gain,
    ln1_bias,
    w_qkv,
    b_qv,
    w_out,
    b_out,
    ln2_gain,
    ln2_bias,
    w_up,
    b_up,
    w_down,
    b_down,
):
    row_count, local_len, width = tokens.shape
    token_count = row_count * local_len
    active = jnp.repeat(exit_mask, TILE, axis=1).astype(jnp.float32).reshape(token_count, 1)
    gathered = (
        lax.all_gather(ln1_gain, ("seq", "batch"), axis=0, tiled=True),
        lax.all_gather(ln1_bias, ("seq", "batch"), axis=0, tiled=True),
        lax.all_gather(w_qkv, ("seq", "batch"), axis=0, tiled=True),
        lax.all_gather(b_qv, ("seq", "batch"), axis=0, tiled=True),
        lax.all_gather(w_out, ("seq", "batch"), axis=0, tiled=True),
        lax.all_gather(b_out, ("seq", "batch"), axis=0, tiled=True),
        lax.all_gather(ln2_gain, ("seq", "batch"), axis=0, tiled=True),
        lax.all_gather(ln2_bias, ("seq", "batch"), axis=0, tiled=True),
        lax.all_gather(b_down, ("seq", "batch"), axis=0, tiled=True),
    )
    gain_one, bias_one, qkv_full, qv_bias, out_full, out_bias, gain_two, bias_two, down_bias = (
        gathered
    )
    gain_one = gain_one.astype(jnp.float32)
    gain_two = gain_two.astype(jnp.float32)
    inputs = tokens.reshape(token_count, width).astype(jnp.float32)
    normed_one, centred_one, inverse_one = norm_forward(
        inputs, gain_one, bias_one.astype(jnp.float32)
    )
    normed_low = normed_one.astype(jnp.bfloat16)
    joined = product(normed_low, qkv_full)
    bias_full = qv_bias.astype(jnp.float32)
    queries = (joined[:, :width] + bias_full[:width]).astype(jnp.bfloat16)
    keys_local = joined[:, width : 2 * width].astype(jnp.bfloat16)
    values_local = (joined[:, 2 * width :] + bias_full[width:]).astype(jnp.bfloat16)
    keys_rows, values_rows = (
        lax.all_gather(keys_local.reshape(row_count, local_len, width), "seq", axis=1, tiled=True),
        lax.all_gather(
            values_local.reshape(row_count, local_len, width), "seq", axis=1, tiled=True
        ),
    )
    q_start = lax.axis_index("seq") * local_len
    row_index = 0
    q_heads, k_heads, v_heads, k_starts = split_heads(
        queries, keys_rows[row_index], values_rows[row_index]
    )
    mixed, logsum = attend_forward(
        q_heads, k_heads, v_heads, k_starts, segment_ids[row_index], q_start
    )
    logsums = [logsum]
    mixed_low = mixed.astype(jnp.bfloat16)
    branch = product(mixed_low, out_full) + out_bias.astype(jnp.float32)
    middle = inputs + active * branch
    normed_two, centred_two, inverse_two = norm_forward(
        middle, gain_two, bias_two.astype(jnp.float32)
    )
    normed_two_low = normed_two.astype(jnp.bfloat16)
    grad_low = (cotangent.reshape(token_count, width).astype(jnp.float32) * active).astype(
        jnp.bfloat16
    )
    up_full, up_bias, down_full = (
        lax.all_gather(w_up, ("seq", "batch"), axis=0, tiled=True),
        lax.all_gather(b_up, ("seq", "batch"), axis=0, tiled=True),
        lax.all_gather(w_down, ("seq", "batch"), axis=0, tiled=True),
    )
    before = product_t(normed_two_low, up_full) + up_bias.astype(jnp.float32)
    hidden_low = smooth_unit(before).astype(jnp.bfloat16)
    feed = product(hidden_low, down_full)
    up_again, down_again = (
        lax.all_gather(w_up, ("seq", "batch"), axis=0, tiled=True),
        lax.all_gather(w_down, ("seq", "batch"), axis=0, tiled=True),
    )
    d_hidden = product_t(grad_low, down_again)
    d_before = (d_hidden * smooth_slope(before)).astype(jnp.bfloat16)
    grad_down_full = product_rows(hidden_low, grad_low)
    grad_up_full = product_rows(d_before, normed_two_low)
    grad_upb_full = jnp.sum(d_before.astype(jnp.float32), axis=0)
    d_normed_two = product(d_before, up_again)
    grad_up, grad_upb, grad_down = (
        lax.psum_scatter(grad_up_full, ("seq", "batch"), scatter_dimension=0, tiled=True),
        lax.psum_scatter(grad_upb_full, ("seq", "batch"), scatter_dimension=0, tiled=True),
        lax.psum_scatter(grad_down_full, ("seq", "batch"), scatter_dimension=0, tiled=True),
    )
    feed = feed + down_bias.astype(jnp.float32)
    layer_out = (middle + active * feed).astype(jnp.bfloat16).reshape(row_count, local_len, width)
    grad_downb_local = jnp.sum(grad_low.astype(jnp.float32), axis=0)
    d_middle_norm, grad_gain_two, grad_bias_two = norm_backward(
        d_normed_two, centred_two, inverse_two, gain_two
    )
    d_middle = cotangent.reshape(token_count, width).astype(jnp.float32) + d_middle_norm
    d_branch = (d_middle * active).astype(jnp.bfloat16)
    qkv_again, out_again = (
        lax.all_gather(w_qkv, ("seq", "batch"), axis=0, tiled=True),
        lax.all_gather(w_out, ("seq", "batch"), axis=0, tiled=True),
    )
    grad_out_full = product_rows(mixed_low, d_branch)
    grad_outb_full = jnp.sum(d_branch.astype(jnp.float32), axis=0)
    d_mixed = product_t(d_branch, out_again).astype(jnp.bfloat16)
    row_index = 0
    q_heads, k_heads, v_heads, k_starts = split_heads(
        queries, keys_rows[row_index], values_rows[row_index]
    )
    d_query, d_keys, d_values = attend_backward(
        q_heads,
        k_heads,
        v_heads,
        k_starts,
        segment_ids[row_index],
        q_start,
        logsums[row_index],
        d_mixed,
    )
    d_key_rows = [d_keys]
    d_value_rows = [d_values]
    d_keys_local, d_values_local = (
        lax.psum_scatter(
            jnp.stack(d_key_rows, axis=0).astype(jnp.bfloat16),
            "seq",
            scatter_dimension=1,
            tiled=True,
        ).astype(jnp.float32),
        lax.psum_scatter(
            jnp.stack(d_value_rows, axis=0).astype(jnp.bfloat16),
            "seq",
            scatter_dimension=1,
            tiled=True,
        ).astype(jnp.float32),
    )
    d_query_low = d_query.astype(jnp.bfloat16)
    d_keys_low = d_keys_local.reshape(token_count, width).astype(jnp.bfloat16)
    d_values_low = d_values_local.reshape(token_count, width).astype(jnp.bfloat16)
    d_joined = jnp.concatenate([d_query_low, d_keys_low, d_values_low], axis=1)
    grad_qkv_full = product_rows(normed_low, d_joined)
    grad_qvb_full = jnp.concatenate(
        [
            jnp.sum(d_query_low.astype(jnp.float32), axis=0),
            jnp.sum(d_values_low.astype(jnp.float32), axis=0),
        ],
        axis=0,
    )
    d_normed_one = product_t(d_joined, qkv_again)
    d_input_norm, grad_gain_one, grad_bias_one = norm_backward(
        d_normed_one, centred_one, inverse_one, gain_one
    )
    input_grad = (d_middle + d_input_norm).reshape(row_count, local_len, width)
    scattered = (
        lax.psum_scatter(grad_gain_one, ("seq", "batch"), scatter_dimension=0, tiled=True),
        lax.psum_scatter(grad_bias_one, ("seq", "batch"), scatter_dimension=0, tiled=True),
        lax.psum_scatter(grad_qkv_full, ("seq", "batch"), scatter_dimension=0, tiled=True),
        lax.psum_scatter(grad_qvb_full, ("seq", "batch"), scatter_dimension=0, tiled=True),
        lax.psum_scatter(grad_out_full, ("seq", "batch"), scatter_dimension=0, tiled=True),
        lax.psum_scatter(grad_outb_full, ("seq", "batch"), scatter_dimension=0, tiled=True),
        lax.psum_scatter(grad_gain_two, ("seq", "batch"), scatter_dimension=0, tiled=True),
        lax.psum_scatter(grad_bias_two, ("seq", "batch"), scatter_dimension=0, tiled=True),
        lax.psum_scatter(grad_downb_local, ("seq", "batch"), scatter_dimension=0, tiled=True),
    )
    grad_g1, grad_c1, grad_qkv, grad_qvb, grad_out, grad_outb, grad_g2, grad_c2, grad_downb = (
        scattered
    )
    return (
        layer_out,
        input_grad,
        grad_g1,
        grad_c1,
        grad_qkv,
        grad_qvb,
        grad_out,
        grad_outb,
        grad_g2,
        grad_c2,
        grad_up,
        grad_upb,
        grad_down,
        grad_downb,
    )


def solution(mesh):
    placed = (
        P("batch", "seq", None),
        P("batch", "seq", None),
        P("batch", None),
        P("batch", "seq"),
        P(("seq", "batch")),
        P(("seq", "batch")),
        P(("seq", "batch"), None),
        P(("seq", "batch")),
        P(("seq", "batch"), None),
        P(("seq", "batch")),
        P(("seq", "batch")),
        P(("seq", "batch")),
        P(("seq", "batch"), None),
        P(("seq", "batch")),
        P(("seq", "batch"), None),
        P(("seq", "batch")),
    )
    return jax.shard_map(
        shards,
        mesh=mesh,
        in_specs=placed,
        out_specs=(
            P("batch", "seq", None),
            P("batch", "seq", None),
            P(("seq", "batch")),
            P(("seq", "batch")),
            P(("seq", "batch"), None),
            P(("seq", "batch")),
            P(("seq", "batch"), None),
            P(("seq", "batch")),
            P(("seq", "batch")),
            P(("seq", "batch")),
            P(("seq", "batch"), None),
            P(("seq", "batch")),
            P(("seq", "batch"), None),
            P(("seq", "batch")),
        ),
        check_vma=False,
    )
```

profile of v0, /device:TPU:0, one launch (start us, length us, event | category | flops | bytes accessed | tf_op | source)
XLA Modules:
  0.0 3271.3 jit_solution(8073753315432652759)
XLA Ops:
  13.1 43.6 %all-reduce.15 = (bf16[2048]{0:T(1024)(128)(2,1)S(1)}, bf16[2048]{0:T(1024)(128)(2,1)S(1)}, bf16[2048]{0:T(1024)(128)(2,1)S(1)}, bf16[2048]{0:T(1024)(128)(2,1)}...) all-reduce(bf16[2048]{0:T(1024)(128)(2,1)S(1)} %dynamic-update-slic, ...), channel_id=1, replica_groups=mesh['seq'=4,'batch'=8] {'seq','batch'}, use_global_device_ids=true, to_apply=%add.1 | all-reduce | flops 12288 | bytes 49152
  56.6 40.5 %all-gather.2 = bf16[32,1,128]{2,1,0:T(2,128)(2,1)S(1)} all-gather(bf16[1,1,128]{2,1,0:T(2,128)(2,1)} %bitcast.264), channel_id=1, replica_groups=mesh['seq'=4,'batch'=8] {'seq','batch'}, dimensions={0}, use_global_device_ids=true | all-gather | bytes 8448 | tf_op jit(solution)/shard_map/all_gather | solution.py:194
  100.3 69.9 %all-gather.11.cloned.1.call-done = bf16[2048,6144]{1,0:T(8,128)(2,1)} async-done(((bf16[64,6144]{1,0:T(8,128)(2,1)}), bf16[2048,6144]{1,0:T(8,128)(2,1)}) %all-gather.11.cloned.1.call-update) | async-done | bytes 25165840 | tf_op jit(solution)/shard_map/all_gather | solution.py:193
  191.1 38.9 %all-gather.3 = bf16[32,1,256]{2,1,0:T(2,128)(2,1)S(1)} all-gather(bf16[1,1,256]{2,1,0:T(2,128)(2,1)S(1)} %reshape.444), channel_id=1, replica_groups=mesh['seq'=4,'batch'=8] {'seq','batch'}, dimensions={0}, use_global_device_ids=true | all-gather | bytes 16896 | tf_op jit(solution)/shard_map/all_gather | solution.py:243
  260.3 32.5 all-gather.21.cloned.1.call-done
  315.4 43.4 %while.58 = (s32[]{:T(128)}, f32[32,256]{1,0:T(8,128)S(1)}, f32[32,256]{1,0:T(8,128)S(1)}, s32[2]{0:T(128)S(1)}, s32[]{:T(128)}, /*index=5*/s32[1024]{0:T(1024)S...) while((s32[]{:T(128)}, f32[32,256]{1,0:T(8,128)S(1)}, ...), condition=%wide.region_5.6_spmd.clone, body=%wide.region_2.5_spmd.clone.sunk | while | flops 570860288 | bytes 37532868 | solution.py:112
  358.8 24.9 while.59
  393.3 176.0 %all-gather.15.cloned.1.call-done = bf16[8192,2048]{1,0:T(8,128)(2,1)} async-done(((bf16[256,2048]{1,0:T(8,128)(2,1)}), bf16[8192,2048]{1,0:T(8,128)(2,1)}) %all-gather.15.cloned.1.call-update) | async-done | bytes 33554448 | tf_op jit(solution)/shard_map/all_gather | solution.py:242
  569.3 19.4 convolution_add_fusion
  588.7 176.4 %all-gather.17.cloned.1.call-done = bf16[8192,2048]{1,0:T(8,128)(2,1)} async-done(((bf16[256,2048]{1,0:T(8,128)(2,1)}), bf16[8192,2048]{1,0:T(8,128)(2,1)}) %all-gather.17.cloned.1.call-update) | async-done | bytes 33554448 | tf_op jit(solution)/shard_map/all_gather | solution.py:244
  765.1 21.7 convert_reduce_fusion
  786.9 17.2 multiply_reduce_fusion
  815.9 46.5 %while.60 = (s32[]{:T(128)}, f32[32,256]{1,0:T(8,128)S(1)}, s32[2]{0:T(128)S(1)}, s32[]{:T(128)}, s32[1024]{0:T(1024)S(1)}, /*index=5*/s32[256]{0:T(256)S(1)}, b...) while((s32[]{:T(128)}, f32[32,256]{1,0:T(8,128)S(1)}, ...), condition=%wide.region_14.15_spmd.clone, body=%wide.region_12.14_spmd.clone.sunk | while | flops 1095115520 | bytes 40285396 | solution.py:142
  862.5 91.0 %while.61 = (s32[]{:T(128)}, f32[256,32,64]{0,2,1:T(8,128)S(1)}, bf16[2,512,32,64]{1,3,2,0:T(8,128)(2,1)}, bf16[2,512,32,64]{1,3,2,0:T(8,128)(2,1)}, bf16[2,512,...) while((s32[]{:T(128)}, f32[256,32,64]{0,2,1:T(8,128)S(1)}, ...), condition=%wide.region_16.17_spmd.clone, body=%wide.region_15.16_spmd.clone.sunk | while | flops 2729313024 | bytes 132625680 | solution.py:162
  987.5 33.2 %reduce-scatter.9.cloned.1.call-done = bf16[1,256,2048]{1,2,0:T(8,128)(2,1)} async-done(((bf16[1,1024,2048]{1,2,0:T(8,128)(2,1)}), bf16[1,256,2048]{1,2,0:T(8,128)(2,1)}) %reduce-scatter.9.cloned.1.call-update) | async-done | bytes 1048592 | tf_op jit(solution)/shard_map/reduce_scatter | solution.py:302
  1022.9 53.7 %reduce-scatter.7.cloned.1.call-done = bf16[1,256,2048]{1,2,0:T(8,128)(2,1)} async-done(((bf16[1,1024,2048]{1,2,0:T(8,128)(2,1)}), bf16[1,256,2048]{1,2,0:T(8,128)(2,1)}) %reduce-scatter.7.cloned.1.call-update) | async-done | bytes 1048592 | tf_op jit(solution)/shard_map/reduce_scatter | solution.py:296
  1101.7 19.0 fusion.94
  1122.4 25.6 fusion.104
  1149.2 27.8 fusion.98
  1177.6 19.6 fusion.81
  1226.1 180.4 %reduce-scatter.13.cloned.1.call-done = f32[64,2048]{1,0:T(8,128)} async-done(((f32[2048,2048]{1,0:T(8,128)}), f32[64,2048]{1,0:T(8,128)}) %reduce-scatter.13.cloned.1.call-update) | async-done | bytes 524304 | tf_op jit(solution)/shard_map/reduce_scatter | solution.py:331
  1406.5 437.5 %reduce-scatter.11.cloned.1.call-done = f32[64,6144]{1,0:T(8,128)} async-done(((f32[2048,6144]{1,0:T(8,128)}), f32[64,6144]{1,0:T(8,128)}) %reduce-scatter.11.cloned.1.call-update) | async-done | bytes 1572880 | tf_op jit(solution)/shard_map/reduce_scatter | solution.py:329
  1844.1 711.3 %reduce-scatter.15.cloned.1.call-done = f32[256,2048]{1,0:T(8,128)} async-done(((f32[8192,2048]{1,0:T(8,128)}), f32[256,2048]{1,0:T(8,128)}) %reduce-scatter.15.cloned.1.call-update) | async-done | bytes 2097168 | tf_op jit(solution)/shard_map/reduce_scatter | solution.py:260
  2555.3 709.0 %reduce-scatter.17.cloned.1.call-done = f32[256,2048]{1,0:T(8,128)} async-done(((f32[8192,2048]{1,0:T(8,128)}), f32[256,2048]{1,0:T(8,128)}) %reduce-scatter.17.cloned.1.call-update) | async-done | bytes 2097168 | tf_op jit(solution)/shard_map/reduce_scatter | solution.py:262
  (248 shorter events, 386.8 us)
Async XLA Ops:
  7.2 163.0 %all-gather.11.cloned.1.call-start = ((), (), s32[]{:S(2)}) async-start(), calls=%async_computation.6 | async-start | bytes 25952256 | tf_op jit(solution)/shard_map/all_gather | solution.py:193
  7.9 229.7 %all-gather.19.cloned.1.call-start = ((), (), s32[]{:S(2)}) async-start(), calls=%async_computation.16 | async-start | bytes 5242880 | tf_op jit(solution)/shard_map/all_gather | solution.py:218
  56.6 125.6 %copy-start.17 = (f32[2048]{0:T(1024)}, f32[2048]{0:T(1024)S(1)}, u32[]{:S(2)}) copy-start(f32[2048]{0:T(1024)S(1)} %convert_element_type.172) | copy-start | bytes 24580
  56.6 125.5 %copy-start.15 = (f32[2048]{0:T(1024)}, f32[2048]{0:T(1024)S(1)}, u32[]{:S(2)}) copy-start(f32[2048]{0:T(1024)S(1)} %convert_element_type.171) | copy-start | bytes 24580
  186.4 106.3 %all-gather.21.cloned.1.call-start = ((), (), s32[]{:S(2)}) async-start(), calls=%async_computation.17 | async-start | bytes 5242880 | tf_op jit(solution)/shard_map/all_gather | solution.py:217
  189.2 197.3 %all-gather.13.cloned.1.call-start = ((), (), s32[]{:S(2)}) async-start(), calls=%async_computation.7 | async-start | bytes 8650752 | tf_op jit(solution)/shard_map/all_gather | solution.py:195
  189.8 379.5 %all-gather.15.cloned.1.call-start = ((), (), s32[]{:S(2)}) async-start(), calls=%async_computation.8 | async-start | bytes 34603008 | tf_op jit(solution)/shard_map/all_gather | solution.py:242
  190.4 574.8 %all-gather.17.cloned.1.call-start = ((), (), s32[]{:S(2)}) async-start(), calls=%async_computation.9 | async-start | bytes 34603008 | tf_op jit(solution)/shard_map/all_gather | solution.py:244
  190.9 829.8 %reduce-scatter.9.cloned.1.call-start = ((), (), s32[]{:S(2)}) async-start(), calls=%async_computation.11 | async-start | bytes 5242880 | tf_op jit(solution)/shard_map/reduce_scatter | solution.py:302
  230.0 339.3 %copy-start.26 = (f32[2048]{0:T(1024)}, f32[2048]{0:T(1024)S(1)}, u32[]{:S(2)}) copy-start(f32[2048]{0:T(1024)S(1)} %convert_element_type.181) | copy-start | bytes 24580
  230.1 574.0 %copy-start.24 = (f32[2048]{0:T(1024)}, f32[2048]{0:T(1024)S(1)}, u32[]{:S(2)}) copy-start(f32[2048]{0:T(1024)S(1)} %convert_element_type.180) | copy-start | bytes 24580
  230.2 573.9 %copy-start.30 = (f32[256]{0:T(256)}, f32[256]{0:T(256)S(1)}, u32[]{:S(2)}) copy-start(f32[256]{0:T(256)S(1)} %broadcast_bitcast_fusion) | copy-start | bytes 3076
  392.9 411.2 %copy-start.2 = (f32[256,2048]{1,0:T(8,128)}, f32[256,2048]{1,0:T(8,128)S(1)}, u32[]{:S(2)}) copy-start(f32[256,2048]{1,0:T(8,128)S(1)} %get-tuple-element.919) | copy-start | bytes 6291460
  393.0 411.2 %copy-start.28 = (f32[256]{0:T(256)}, f32[256]{0:T(256)S(1)}, u32[]{:S(2)}) copy-start(f32[256]{0:T(256)S(1)} %broadcast_multiply_fusion.4) | copy-start | bytes 3076
  393.3 410.8 %copy-start.32 = (f32[256]{0:T(256)}, f32[256]{0:T(256)S(1)}, u32[]{:S(2)}) copy-start(f32[256]{0:T(256)S(1)} %add_rsqrt_fusion) | copy-start | bytes 3076
  969.7 106.9 %reduce-scatter.7.cloned.1.call-start = ((), (), s32[]{:S(2)}) async-start(), calls=%async_computation.10 | async-start | bytes 5242880 | tf_op jit(solution)/shard_map/reduce_scatter | solution.py:296
  986.1 90.5 %copy-start.16 = (f32[2048]{0:T(1024)S(1)}, f32[2048]{0:T(1024)}, u32[]{:S(2)}) copy-start(f32[2048]{0:T(1024)} %copy-done.15) | copy-start | bytes 24580
  986.1 90.5 %copy-start.21 = (f32[256]{0:T(256)S(1)}, f32[256]{0:T(256)}, u32[]{:S(2)}) copy-start(f32[256]{0:T(256)} %copy-done.20) | copy-start | bytes 3076
  986.1 90.5 %copy-start.23 = (f32[256]{0:T(256)S(1)}, f32[256]{0:T(256)}, u32[]{:S(2)}) copy-start(f32[256]{0:T(256)} %copy-done.22) | copy-start | bytes 3076
  986.2 229.8 %all-reduce.18.cloned.1.call-start = ((), (), s32[]{:S(2)}) async-start(), calls=%async_computation.18 | async-start | bytes 196608
  1091.9 314.6 %reduce-scatter.13.cloned.1.call-start = ((), (), s32[]{:S(2)}) async-start(), calls=%async_computation.13 | async-start | bytes 17301504 | tf_op jit(solution)/shard_map/reduce_scatter | solution.py:331
  1100.2 743.9 %reduce-scatter.11.cloned.1.call-start = ((), (), s32[]{:S(2)}) async-start(), calls=%async_computation.12 | async-start | bytes 51904512 | tf_op jit(solution)/shard_map/reduce_scatter | solution.py:329
  1120.8 1434.5 %reduce-scatter.15.cloned.1.call-start = ((), (), s32[]{:S(2)}) async-start(), calls=%async_computation.14 | async-start | bytes 69206016 | tf_op jit(solution)/shard_map/reduce_scatter | solution.py:260
  1148.0 2116.3 %reduce-scatter.17.cloned.1.call-start = ((), (), s32[]{:S(2)}) async-start(), calls=%async_computation.15 | async-start | bytes 69206016 | tf_op jit(solution)/shard_map/reduce_scatter | solution.py:262
  (27 other events, 501.8 us)
Sparse Core Ops, SparseCore 0:
  11.0 159.0 all-gather.10
  186.5 51.0 all-gather.18
  240.0 52.6 all-gather.20
  295.5 77.4 all-gather.12
  375.9 193.3 all-gather.14
  572.1 192.9 all-gather.16
  969.8 50.8 reduce-scatter.8
  1023.9 52.6 reduce-scatter.6
  1092.1 123.8 all-reduce.17
  1218.8 187.7 reduce-scatter.12
  1414.7 429.3 reduce-scatter.10
  1847.0 708.3 reduce-scatter.14
  2558.4 705.8 reduce-scatter.16
where the time goes:
time: 3280 us; the launch traced here: 3270 us
  waiting for transfers between devices  2600 us (79%)
  matrix products  358 us (11%)
  blocking collectives  123 us (4%)
  local copies, waits for them, and re-layouts  114 us (3%)
  other arithmetic  42 us (1%)
    reduce_scatter x1, waiting for transfers between devices, shards(): lax.psum_scatter(grad_up_full, ('seq', 'batch'), scatter_dimension=0, til...  711 us
    reduce_scatter x1, waiting for transfers between devices, shards(): lax.psum_scatter(grad_down_full, ('seq', 'batch'), scatter_dimension=0, t...  709 us
    reduce_scatter x1, waiting for transfers between devices, shards(): lax.psum_scatter(grad_qkv_full, ('seq', 'batch'), scatter_dimension=0, ti...  438 us
    reduce_scatter x1, waiting for transfers between devices, shards(): lax.psum_scatter(grad_out_full, ('seq', 'batch'), scatter_dimension=0, ti...  180 us
    all_gather x1, waiting for transfers between devices, shards(): lax.all_gather(w_down, ('seq', 'batch'), axis=0, tiled=True)  176 us
    all_gather x1, waiting for transfers between devices, shards(): lax.all_gather(w_up, ('seq', 'batch'), axis=0, tiled=True)  176 us
    dot_general x4, matrix products, product_rows(): lax.dot_general(left, right, (((0,), (0,)), ((), ())), preferred_element_...  80.5 us
    all_gather x1, waiting for transfers between devices, shards(): lax.all_gather(w_qkv, ('seq', 'batch'), axis=0, tiled=True)  69.9 us
  transfers between devices with their start and end apart: 13, of which 12 were waited for; matrix products, arithmetic and copies ran while one was open for 9% of the time, Pallas kernels for 0%

commit v1 on v0

v1 whole, which is shorter than its diff:
```python
import functools

import jax
import jax.numpy as jnp
from jax import lax
from jax.experimental import pallas as pl
from jax.experimental.pallas import tpu as pltpu
from jax.sharding import PartitionSpec as P

HEADS = 32
HEAD_DIM = 64
TILE = 128
PAIR = 2 * HEAD_DIM
Q_BLOCK = 256
PAD = 16
EPSILON = 1e-05
GELU_C = 0.7978845608028654
GELU_K = 0.044715
NEGATIVE = -1e30
VMEM_LIMIT = 56 * 1024 * 1024
LOW = jnp.bfloat16
WIDE = jnp.float32


def product(left, right):
    return jnp.dot(left, right, preferred_element_type=WIDE)


def product_t(left, right):
    return lax.dot_general(left, right, (((1,), (1,)), ((), ())), preferred_element_type=WIDE)


def product_rows(left, right):
    return lax.dot_general(left, right, (((0,), (0,)), ((), ())), preferred_element_type=WIDE)


def norm_stats(values):
    centre = jnp.mean(values, axis=-1, keepdims=True)
    centred = values - centre
    spread = jnp.mean(centred * centred, axis=-1, keepdims=True)
    return centre, lax.rsqrt(spread + EPSILON)


def norm_backward(upstream, normed, inverse, gain):
    graded = upstream * gain
    first = jnp.mean(graded, axis=-1, keepdims=True)
    second = jnp.mean(graded * normed, axis=-1, keepdims=True)
    return inverse * (graded - first - normed * second)


def flip(values, axis, bit, size):
    return lax.ppermute(values, axis, [(i, i ^ bit) for i in range(size)])


def gather_seq(values, n_seq):
    if n_seq != 4:
        return lax.all_gather(values, "seq", axis=0, tiled=False)
    me = lax.axis_index("seq")
    half = values.shape[0] // 2
    one = flip(values, "seq", 1, 4)
    two = flip(values, "seq", 2, 4)
    low = flip(one[:half], "seq", 2, 4)
    high = flip(two[half:], "seq", 1, 4)
    out = jnp.zeros((4,) + values.shape, values.dtype)
    zero = jnp.zeros((), me.dtype)
    out = lax.dynamic_update_slice(out, values[None], (me, zero, zero))
    out = lax.dynamic_update_slice(out, one[None], (me ^ 1, zero, zero))
    out = lax.dynamic_update_slice(out, two[None], (me ^ 2, zero, zero))
    out = lax.dynamic_update_slice(out, low[None], (me ^ 3, zero, zero))
    return lax.dynamic_update_slice(out, high[None], (me ^ 3, zero + half, zero))


def scatter_seq(values, n_seq):
    n = values.shape[0] // n_seq
    me = lax.axis_index("seq")
    if n_seq != 4:
        parts = lax.all_to_all(values.astype(LOW).reshape(n_seq, n, -1), "seq", 0, 0, tiled=True)
        return jnp.sum(parts.astype(WIDE), axis=0)
    total = lax.dynamic_slice_in_dim(values, me * n, n, 0)
    parts = []
    for bit in (3, 1, 2):
        piece = lax.dynamic_slice_in_dim(values, (me ^ bit) * n, n, 0).astype(LOW)
        parts.append(flip(piece, "seq", bit, 4))
    for part in parts:
        total = total + part.astype(WIDE)
    return total


def key_range(q_start, q_count, length):
    low = max(0, (q_start - (length // 2 - 1)) // q_count * q_count)
    return low, q_start + q_count


def block_mask(starts, low, high, q_start, q_count):
    shape = (high - low, q_count)
    key = low + lax.broadcasted_iota(jnp.int32, shape, 0)
    query = q_start + lax.broadcasted_iota(jnp.int32, shape, 1)
    return (key <= query) & (key >= starts)


def attend_kernel(q_ref, k_ref, v_ref, start_ref, o_ref, lse_ref):
    length = q_ref.shape[0]
    lane = lax.broadcasted_iota(jnp.int32, (1, PAIR), 1)
    row = lax.broadcasted_iota(jnp.int32, (PAIR, 1), 0)
    for q_start in range(0, length, Q_BLOCK):
        low, high = key_range(q_start, Q_BLOCK, length)
        here = slice(q_start, q_start + Q_BLOCK)
        q, k, v = q_ref[here, :], k_ref[low:high, :], v_ref[low:high, :]
        allowed = block_mask(start_ref[:, here], low, high, q_start, Q_BLOCK)
        mixed = []
        for head in range(2):
            mine = (lane >= head * HEAD_DIM) & (lane < (head + 1) * HEAD_DIM)
            q_head = jnp.where(mine, q, jnp.zeros_like(q))
            scores = product_t(k, q_head) * HEAD_DIM ** (-0.5)
            scores = jnp.where(allowed, scores, NEGATIVE)
            peak = jnp.max(scores, axis=0, keepdims=True)
            raised = jnp.exp(scores - peak)
            total = jnp.sum(raised, axis=0, keepdims=True)
            probs = (raised / total).astype(LOW)
            mixed.append(product_rows(v, probs))
            lse_ref[0, head : head + 1, here] = peak + jnp.log(total)
        joined = jnp.where(row < HEAD_DIM, mixed[0], mixed[1])
        o_ref[here, :] = joined.T.astype(LOW)


def attend(qkv, starts, width):
    length = qkv.shape[0]
    pairs = width // PAIR
    return pl.pallas_call(
        attend_kernel,
        grid=(pairs,),
        in_specs=[
            pl.BlockSpec((length, PAIR), lambda j: (0, j)),
            pl.BlockSpec((length, PAIR), lambda j: (0, pairs + j)),
            pl.BlockSpec((length, PAIR), lambda j: (0, 2 * pairs + j)),
            pl.BlockSpec((1, length), lambda j: (0, 0)),
        ],
        out_specs=[
            pl.BlockSpec((length, PAIR), lambda j: (0, j)),
            pl.BlockSpec((1, 2, length), lambda j: (j, 0, 0)),
        ],
        out_shape=[
            jax.ShapeDtypeStruct((length, width), LOW),
            jax.ShapeDtypeStruct((pairs, 2, length), WIDE),
        ],
        compiler_params=pltpu.CompilerParams(vmem_limit_bytes=VMEM_LIMIT),
        cost_estimate=pl.CostEstimate(
            flops=16 * length * length * width,
            bytes_accessed=8 * length * width,
            transcendentals=length * length * width // HEAD_DIM,
        ),
        name="attend",
    )(qkv, qkv, qkv, starts)


def attend_back_kernel(q_ref, k_ref, v_ref, do_ref, start_ref, lse_ref, out_ref, dk_acc, dv_acc):
    length = q_ref.shape[0]
    width = out_ref.shape[1] // 3
    at = pl.program_id(0) * PAIR
    scale = HEAD_DIM ** (-0.5)
    lane = lax.broadcasted_iota(jnp.int32, (1, PAIR), 1)
    row = lax.broadcasted_iota(jnp.int32, (PAIR, 1), 0)
    dk_acc[...] = jnp.zeros_like(dk_acc)
    dv_acc[...] = jnp.zeros_like(dv_acc)
    for q_start in range(0, length, Q_BLOCK):
        low, high = key_range(q_start, Q_BLOCK, length)
        here = slice(q_start, q_start + Q_BLOCK)
        q, k, v, do = q_ref[here, :], k_ref[low:high, :], v_ref[low:high, :], do_ref[here, :]
        allowed = block_mask(start_ref[:, here], low, high, q_start, Q_BLOCK)
        d_query = []
        for head in range(2):
            mine = (lane >= head * HEAD_DIM) & (lane < (head + 1) * HEAD_DIM)
            q_head = jnp.where(mine, q, jnp.zeros_like(q))
            do_head = jnp.where(mine, do, jnp.zeros_like(do))
            scores = product_t(k, q_head) * scale - lse_ref[0, head : head + 1, here]
            probs = jnp.exp(jnp.where(allowed, scores, NEGATIVE))
            d_probs = product_t(v, do_head)
            delta = jnp.sum(probs * d_probs, axis=0, keepdims=True)
            d_scores = (probs * (d_probs - delta)).astype(LOW)
            d_query.append(product_rows(k, d_scores))
            dk_acc[low:high, :] += product(d_scores, q_head)
            dv_acc[low:high, :] += product(probs.astype(LOW), do_head)
        joined = jnp.where(row < HEAD_DIM, d_query[0], d_query[1]) * scale
        out_ref[here, pl.ds(pl.multiple_of(at, PAIR), PAIR)] = joined.T.astype(LOW)
    out_ref[:, pl.ds(pl.multiple_of(width + at, PAIR), PAIR)] = (dk_acc[...] * scale).astype(LOW)
    out_ref[:, pl.ds(pl.multiple_of(2 * width + at, PAIR), PAIR)] = dv_acc[...].astype(LOW)


def attend_back(qkv, d_mixed, starts, logsum, width):
    length = qkv.shape[0]
    pairs = width // PAIR
    return pl.pallas_call(
        attend_back_kernel,
        grid=(pairs,),
        in_specs=[
            pl.BlockSpec((length, PAIR), lambda j: (0, j)),
            pl.BlockSpec((length, PAIR), lambda j: (0, pairs + j)),
            pl.BlockSpec((length, PAIR), lambda j: (0, 2 * pairs + j)),
            pl.BlockSpec((length, PAIR), lambda j: (0, j)),
            pl.BlockSpec((1, length), lambda j: (0, 0)),
            pl.BlockSpec((1, 2, length), lambda j: (j, 0, 0)),
        ],
        out_specs=pl.BlockSpec((length, 3 * width), lambda j: (0, 0)),
        out_shape=jax.ShapeDtypeStruct((length, 3 * width), LOW),
        scratch_shapes=[pltpu.VMEM((length, PAIR), WIDE), pltpu.VMEM((length, PAIR), WIDE)],
        compiler_params=pltpu.CompilerParams(vmem_limit_bytes=VMEM_LIMIT),
        cost_estimate=pl.CostEstimate(
            flops=40 * length * length * width,
            bytes_accessed=14 * length * width,
            transcendentals=length * length * width // HEAD_DIM,
        ),
        name="attend_back",
    )(qkv, qkv, qkv, d_mixed, starts, logsum)


def shards(
    n_seq,
    n_batch,
    tokens,
    cotangent,
    segment_ids,
    exit_mask,
    ln1_gain,
    ln1_bias,
    w_qkv,
    b_qv,
    w_out,
    b_out,
    ln2_gain,
    ln2_bias,
    w_up,
    b_up,
    w_down,
    b_down,
):
    _, local_len, width = tokens.shape
    length = n_seq * local_len
    own = w_qkv.shape[0]
    head_width = width // n_seq
    n_all = n_seq * n_batch
    me = lax.axis_index("seq")
    tokens = tokens.reshape(local_len, width)
    cotangent = cotangent.reshape(local_len, width)

    small_parts = (ln1_gain, ln1_bias, b_qv, b_out, ln2_gain, ln2_bias, b_up, b_down)
    sizes = [part.shape[0] for part in small_parts]
    n_small = sum(sizes)
    tiles = exit_mask.shape[1]
    small = jnp.concatenate(small_parts + (exit_mask.reshape(-1).astype(LOW),))
    small = jnp.pad(small, (0, 3 * head_width - small.shape[0]))

    by_head = w_qkv.reshape(own, 3, n_seq, head_width).transpose(2, 0, 1, 3)
    by_head = by_head.reshape(n_seq, own, 3 * head_width)
    extra = jnp.broadcast_to(small[None, None], (n_seq, PAD, 3 * head_width))
    moved = lax.all_to_all(jnp.concatenate([by_head, extra], axis=1), "seq", 0, 0, tiled=True)
    small_rows = moved[:, own, :]
    active_row = jnp.repeat(small_rows[:, n_small : n_small + tiles].reshape(-1), TILE)
    active_row = active_row.astype(WIDE).reshape(length, 1)
    sent = jnp.concatenate(
        [
            moved[:, :own].reshape(n_seq * own, 3 * head_width),
            small_rows,
            jnp.zeros((PAD - n_seq % PAD if n_seq % PAD else 0, 3 * head_width), LOW),
        ],
        axis=0,
    )
    out_part = lax.all_gather(w_out, "batch", axis=0, tiled=True)
    joined = lax.all_gather(sent, "batch", axis=0, tiled=False)
    qkv_full = joined[:, : n_seq * own].reshape(n_batch, n_seq, own, 3 * head_width)
    qkv_full = qkv_full.transpose(1, 0, 2, 3).reshape(width, 3 * head_width)
    small_all = joined[:, n_seq * own : n_seq * own + n_seq, :n_small]
    small_all = small_all.transpose(1, 0, 2).astype(WIDE)
    params, at = [], 0
    for size in sizes:
        params.append(small_all[:, :, at : at + size].reshape(-1))
        at += size
    gain_one, bias_one, qv_bias, out_bias, gain_two, bias_two, up_bias_all, down_bias = params
    up_all = lax.all_gather(w_up, "batch", axis=0, tiled=True)
    down_all = lax.all_gather(w_down, "batch", axis=0, tiled=True)
    hidden_count = up_all.shape[0]
    up_bias = lax.dynamic_slice_in_dim(up_bias_all, me * hidden_count, hidden_count)

    out_full = gather_seq(out_part, n_seq).reshape(width, width)

    row_low = gather_seq(tokens, n_seq).reshape(length, width)
    row = row_low.astype(WIDE)
    centre_one, inverse_one = norm_stats(row)
    normed_one = (row - centre_one) * inverse_one
    normed_low = (normed_one * gain_one + bias_one).astype(LOW)
    own_q = lax.dynamic_slice_in_dim(qv_bias, me * head_width, head_width)
    own_v = lax.dynamic_slice_in_dim(qv_bias, width + me * head_width, head_width)
    own_bias = jnp.concatenate([own_q, jnp.zeros_like(own_q), own_v])
    qkv = (product(normed_low, qkv_full) + own_bias).astype(LOW)
    segment_row = segment_ids.reshape(length)
    starts = jnp.sum(
        (segment_row[None, :] < segment_row[:, None]).astype(jnp.int32), axis=1
    ).reshape(1, length)
    mixed, logsum = attend(qkv, starts, head_width)
    mixed_all = gather_seq(mixed, n_seq).transpose(1, 0, 2).reshape(length, width)
    branch = product(mixed_all, out_full) + out_bias
    middle = row + active_row * branch
    centre_two, inverse_two = norm_stats(middle)
    normed_two = (middle - centre_two) * inverse_two
    normed_two_low = (normed_two * gain_two + bias_two).astype(LOW)

    active = jnp.repeat(exit_mask.reshape(-1), TILE).astype(WIDE).reshape(local_len, 1)
    grad_low = (cotangent.astype(WIDE) * active).astype(LOW)
    grad_row = gather_seq(grad_low, n_seq).reshape(length, width)
    before = product_t(normed_two_low, up_all) + up_bias
    inner = GELU_C * (before + GELU_K * before * before * before)
    tangent = jnp.tanh(inner)
    hidden_low = (0.5 * before * (1.0 + tangent)).astype(LOW)
    slope = 0.5 * (1.0 + tangent) + 0.5 * before * (1.0 - tangent * tangent) * GELU_C * (
        1.0 + 3.0 * GELU_K * before * before
    )
    grad_down = lax.psum_scatter(
        product_rows(hidden_low, grad_row).astype(LOW), "batch", scatter_dimension=0, tiled=True
    )
    d_before = (product_t(grad_row, down_all) * slope).astype(LOW)
    d_normed_two = scatter_seq(product(d_before, up_all), n_seq)
    grad_up = lax.psum_scatter(
        product_rows(d_before, normed_two_low).astype(LOW), "batch", scatter_dimension=0, tiled=True
    )
    grad_upb = jnp.sum(d_before.astype(WIDE), axis=0)
    grad_downb = jnp.sum(
        lax.dynamic_slice_in_dim(grad_row, me * head_width, head_width, 1).astype(WIDE), axis=0
    )
    feed = scatter_seq(product(hidden_low, down_all), n_seq) + down_bias
    middle_own = lax.dynamic_slice_in_dim(middle, me * local_len, local_len, 0)
    layer_out = (middle_own + active * feed).astype(LOW)

    normed_own = lax.dynamic_slice_in_dim(normed_two, me * local_len, local_len, 0)
    inverse_own = lax.dynamic_slice_in_dim(inverse_two, me * local_len, local_len, 0)
    d_middle = cotangent.astype(WIDE) + norm_backward(d_normed_two, normed_own, inverse_own, gain_two)
    grad_gain_two = jnp.sum(d_normed_two * normed_own, axis=0)
    grad_bias_two = jnp.sum(d_normed_two, axis=0)
    d_branch = (d_middle * active).astype(LOW)
    d_mixed_own = product_t(d_branch, out_full).astype(LOW)
    d_mixed = lax.all_to_all(d_mixed_own, "seq", 1, 0, tiled=True)
    d_qkv = attend_back(qkv, d_mixed, starts, logsum, head_width)
    d_branch_row = gather_seq(d_branch, n_seq).reshape(length, width)
    grad_out = lax.psum_scatter(
        product_rows(mixed, d_branch_row).astype(LOW), "batch", scatter_dimension=0, tiled=True
    )
    grad_outb = jnp.sum(
        lax.dynamic_slice_in_dim(d_branch_row, me * head_width, head_width, 1).astype(WIDE), axis=0
    )

    d_normed_part = product_t(d_qkv, qkv_full)
    grad_gain_one = jnp.sum(d_normed_part * normed_one, axis=0)
    grad_bias_one = jnp.sum(d_normed_part, axis=0)
    d_normed_one = scatter_seq(d_normed_part, n_seq)
    row_own = tokens.astype(WIDE)
    centre_own, inverse_first = norm_stats(row_own)
    d_input = d_middle + norm_backward(
        d_normed_one, (row_own - centre_own) * inverse_first, inverse_first, gain_one
    )

    def place(values, total):
        return lax.dynamic_update_slice_in_dim(
            jnp.zeros((total,), WIDE), values, me * values.shape[0], 0
        )

    d_bias = jnp.sum(d_qkv.astype(WIDE), axis=0)
    grad_qvb = jnp.concatenate(
        [place(d_bias[:head_width], width), place(d_bias[2 * head_width :], width)]
    )
    small_grads = (
        grad_gain_one,
        grad_bias_one,
        grad_qvb,
        place(grad_outb, width),
        grad_gain_two,
        grad_bias_two,
        place(grad_upb, n_seq * hidden_count),
        place(grad_downb, width),
    )
    packed = jnp.concatenate([g.reshape(n_seq, n_batch, -1) for g in small_grads], axis=2)
    packed = jnp.pad(packed, ((0, 0), (0, 0), (0, 3 * head_width - n_small))).astype(LOW)
    grad_qkv_part = product_rows(normed_low, d_qkv).astype(LOW)
    grad_qkv_part = grad_qkv_part.reshape(n_seq, n_batch, own, 3 * head_width)
    packed = jnp.pad(packed[:, :, None], ((0, 0), (0, 0), (0, PAD - 1), (0, 0)))
    grad_qkv_part = jnp.concatenate([grad_qkv_part, packed], axis=2).transpose(1, 0, 2, 3)
    reduced = lax.psum_scatter(
        grad_qkv_part.reshape(n_batch * n_seq * (own + PAD), 3 * head_width),
        "batch",
        scatter_dimension=0,
        tiled=True,
    )
    final = lax.all_to_all(
        reduced.reshape(n_seq, own + PAD, 3 * head_width), "seq", 0, 0, tiled=True
    )
    grad_qkv = final[:, :own].reshape(n_seq, own, 3, head_width).transpose(1, 2, 0, 3)
    grad_qkv = grad_qkv.reshape(own, 3 * width).astype(WIDE)
    small_out = jnp.sum(final[:, own, :n_small].astype(WIDE), axis=0)
    small_result, at = [], 0
    for size in sizes:
        small_result.append(small_out[at : at + size])
        at += size
    g_one, c_one, g_qvb, g_outb, g_two, c_two, g_upb, g_downb = small_result
    return (
        layer_out[None],
        d_input[None],
        g_one,
        c_one,
        grad_qkv,
        g_qvb,
        grad_out.astype(WIDE),
        g_outb,
        g_two,
        c_two,
        grad_up.astype(WIDE),
        g_upb,
        grad_down.astype(WIDE),
        g_downb,
    )


def solution(mesh):
    vector = P(("seq", "batch"))
    matrix = P(("seq", "batch"), None)
    rows = P("batch", "seq", None)
    return jax.shard_map(
        functools.partial(shards, mesh.shape["seq"], mesh.shape["batch"]),
        mesh=mesh,
        in_specs=(
            rows, rows, P("batch", None), P("batch", "seq"),
            vector, vector, matrix, vector, matrix, vector, vector, vector, matrix, vector, matrix, vector,
        ),
        out_specs=(
            rows, rows, vector, vector, matrix, vector, matrix, vector, vector, vector, matrix, vector, matrix, vector,
        ),
        check_vma=False,
    )
```

time: 3280 us -> 904 us (0.28)
  waiting for transfers between devices: 2600 us -> 504 us
  matrix products: 358 us -> 150 us
  blocking collectives: 123 us -> 0 us
  starting transfers between devices: 0.53 us -> 49.8 us
  Pallas kernels: 0 us -> 43.6 us
  local copies, waits for them, and re-layouts: 114 us -> 74.3 us
    reduce_scatter x6 -> x4, waiting for transfers between devices: 2130 us -> 197 us  [the longest x1 88.8 us: shards(): lax.psum_scatter(product_rows(hidden_low, grad_row).astype(LOW), 'batch',...]
    all_gather x6 -> x4, waiting for transfers between devices: 462 us -> 37.4 us  [the longest x1 37.4 us: shards(): down_all = lax.all_gather(w_down, 'batch', axis=0, tiled=True)]
    ppermute x0 -> x29, waiting for transfers between devices: none -> 246 us  [flip(): return lax.ppermute(values, axis, [(i, i ^ bit) for i in range(size)])]
    dot_general x22 -> x4, matrix products: 215 us -> 49.6 us  [product(): return jnp.dot(left, right, preferred_element_type=WIDE)]
    all_gather x2 -> x0, blocking collectives: 79.4 us -> none  [the longest x1 40.5 us: shards(): lax.all_gather(b_qv, ('seq', 'batch'), axis=0, tiled=True)]
    unnamed x1 -> x0, blocking collectives: 43.6 us -> none
    pallas_call x0 -> x2, Pallas kernels: none -> 43.6 us  [the longest x1 23.5 us: attend_back(): pl.pallas_call(attend_back_kernel, grid=(pairs,), in_specs=[pl.BlockSpec(...]
    ppermute x0 -> x29, starting transfers between devices: none -> 35.5 us  [flip(): return lax.ppermute(values, axis, [(i, i ^ bit) for i in range(size)])]
  transfers between devices with their start and end apart: 13 -> 40, of which waited for: 12 -> 26; matrix products, arithmetic and copies ran while one was open for 9% -> 21% of each run, Pallas kernels for 0% -> 5%
where the time goes in v1:
time: 904 us; the launch traced here: 895 us
  waiting for transfers between devices  504 us (56%)
  matrix products  150 us (17%)
  local copies, waits for them, and re-layouts  74.3 us (8%)
  other arithmetic  57.8 us (6%)
  starting transfers between devices  49.8 us (6%)
  Pallas kernels  43.6 us (5%)
  between operations  15.3 us (2%)
    ppermute x29, waiting for transfers between devices, flip(): return lax.ppermute(values, axis, [(i, i ^ bit) for i in range(size)])  246 us
    reduce_scatter x1, waiting for transfers between devices, shards(): lax.psum_scatter(product_rows(hidden_low, grad_row).astype(LOW), 'batch',...  88.8 us
    reduce_scatter x1, waiting for transfers between devices, shards(): lax.psum_scatter(product_rows(d_before, normed_two_low).astype(LOW), 'bat...  87.5 us
    dot_general x4, matrix products, product_t(): lax.dot_general(left, right, (((1,), (1,)), ((), ())), preferred_element_...  55.3 us
    dot_general x4, matrix products, product(): return jnp.dot(left, right, preferred_element_type=WIDE)  49.6 us
    dot_general x4, matrix products, product_rows(): lax.dot_general(left, right, (((0,), (0,)), ((), ())), preferred_element_...  45.4 us
    all_gather x1, waiting for transfers between devices, shards(): down_all = lax.all_gather(w_down, 'batch', axis=0, tiled=True)  37.4 us
    ppermute x29, starting transfers between devices, flip(): return lax.ppermute(values, axis, [(i, i ^ bit) for i in range(size)])  35.5 us
  transfers between devices with their start and end apart: 40, of which 26 were waited for; matrix products, arithmetic and copies ran while one was open for 21% of the time, Pallas kernels for 5%

profile of v1, /device:TPU:0, one launch (start us, length us, event | category | flops | bytes accessed | tf_op | source)
XLA Modules:
  0.0 895.4 jit_solution(10432365920411056822)
XLA Ops:
  18.5 12.8 %all-to-all-done = bf16[4,80,1536]{2,1,0:T(8,128)(2,1)S(1)} async-done(((bf16[4,80,1536]{2,1,0:T(8,128)(2,1)}), bf16[4,80,1536]{2,1,0:T(8,128)(2,1)S(1)}, u32[]{:S(2)}, u32[]{:S(2)}) %all-to-all-start) | async-done | bytes 983072 | tf_op jit(solution)/shard_map/all_to_all | solution.py:255
  40.5 17.1 %collective-permute-done = bf16[256,2048]{1,0:T(8,128)(2,1)S(1)} collective-permute-done((bf16[256,2048]{1,0:T(8,128)(2,1)S(1)}, bf16[256,2048]{1,0:T(8,128)(2,1)S(1)}, u32[]{:S(2)}, u32[]{:S(2)}) %collective-permute-start) | collective-permute-done | bytes 1048608 | tf_op jit(solution)/shard_map/ppermute | solution.py:52
  86.7 29.3 %collective-permute-done.8 = bf16[512,2048]{1,0:T(8,128)(2,1)S(1)} collective-permute-done((bf16[512,2048]{1,0:T(8,128)(2,1)}, bf16[512,2048]{1,0:T(8,128)(2,1)S(1)}, u32[]{:S(2)}, u32[]{:S(2)}) %collective-permute-start.8) | collective-permute-done | bytes 2097184 | tf_op jit(solution)/shard_map/ppermute | solution.py:52
  147.1 20.1 %attend.1 = (bf16[1024,512]{1,0:T(8,128)(2,1)}, f32[4,2,1024]{2,1,0:T(2,128)}) custom-call(bf16[1024,1536]{1,0:T(8,128)(2,1)} %add_convert_fusion.1.q_ref.k_ref.v_ref, bf16[1024,1536]{1,0:T(8,128)(2,1)} %add_convert_fusion.1.q_ref.k_ref.v_ref, bf16[1024,1536]{1,0:T(8,128)(2,1)} %add_convert_fusion.1.q_ref.k_ref.v_ref, s32[1,1024]{1,0:T(1,128)} %bitcast.199), custom_call_target="tpu_custom_call" | custom-call | flops 8589934592 | bytes 4194304 | tf_op jit(solution)/shard_map/attend/pallas_call | solution.py:129
  174.7 15.7 %collective-permute-done.4 = bf16[1024,512]{1,0:T(8,128)(2,1)S(1)} collective-permute-done((bf16[1024,512]{1,0:T(8,128)(2,1)}, bf16[1024,512]{1,0:T(8,128)(2,1)S(1)}, u32[]{:S(2)}, u32[]{:S(2)}) %collective-permute-start.4) | collective-permute-done | bytes 1048608 | tf_op jit(solution)/shard_map/ppermute | solution.py:52
  201.4 13.6 %fusion.51 = (f32[1024]{0:T(1024)S(1)}, f32[1024,2048]{1,0:T(8,128)S(1)}) fusion(f32[2048]{0:T(1024)S(1)} %add.251, bf16[4,512,2048]{2,1,0:T(8,128)(2,1)} %bitcast_dynamic-update-slice_fusion.8, bf16[4,1024,512]{2,1,0:T(8,128)(2,1)S(1)} %bitcast_dynamic-update-slice_fusion.19, f32[1024]{0:T(1024)S(1)} %broadcast_bitcast_fusion, ...), kind=kOutput, calls=%fused_computation.148 | convolution fusion | flops 8600419328 | bytes 25182208 | tf_op jit(solution)/shard_map/dot_general | solution.py:26
  222.3 16.0 %fusion.38 = f32[1024,2048]{1,0:T(8,128)} fusion(bf16[2048,2048]{1,0:T(8,128)(2,1)} %all-gather.8.cloned.1.call-done, f32[1024,2048]{1,0:T(8,128)} %subtract_multiply_fusion, f32[2048]{0:T(1024)S(1)} %add.257, f32[2048]{0:T(1024)S(1)} %mul.255), kind=kOutput, calls=%fused_computation.83 | convolution fusion | flops 8596226048 | bytes 25182208 | tf_op jit(solution)/shard_map/dot_general | solution.py:30
  238.3 37.4 %all-gather.10.cloned.1.call-done = bf16[2048,2048]{1,0:T(8,128)(2,1)} async-done(((bf16[256,2048]{1,0:T(8,128)(2,1)}), bf16[2048,2048]{1,0:T(8,128)(2,1)}) %all-gather.10.cloned.1.call-update) | async-done | bytes 8388624 | tf_op jit(solution)/shard_map/all_gather | solution.py:279
  275.7 15.5 %fusion.44 = f32[1024,2048]{1,0:T(8,128)S(1)} fusion(bf16[2048,2048]{1,0:T(8,128)(2,1)} %all-gather.10.cloned.1.call-done, f32[1024,2048]{1,0:T(8,128)} %fusion.38, f32[2048]{0:T(1024)S(1)} %dynamic_slice.61), kind=kOutput, calls=%fused_computation.142 | convolution fusion | flops 8610906112 | bytes 25174016 | tf_op jit(solution)/shard_map/dot_general | solution.py:26
  299.9 23.5 %collective-permute-done.12 = bf16[256,2048]{1,0:T(8,128)(2,1)S(1)} collective-permute-done((bf16[256,2048]{1,0:T(8,128)(2,1)}, bf16[256,2048]{1,0:T(8,128)(2,1)S(1)}, u32[]{:S(2)}, u32[]{:S(2)}) %collective-permute-start.12) | collective-permute-done | bytes 1048608 | tf_op jit(solution)/shard_map/ppermute | solution.py:52
  323.4 21.9 %collective-permute-done.13 = bf16[256,2048]{1,0:T(8,128)(2,1)S(1)} collective-permute-done((bf16[256,2048]{1,0:T(8,128)(2,1)}, bf16[256,2048]{1,0:T(8,128)(2,1)S(1)}, u32[]{:S(2)}, u32[]{:S(2)}) %collective-permute-start.13) | collective-permute-done | bytes 1048608 | tf_op jit(solution)/shard_map/ppermute | solution.py:52
  353.6 21.3 %collective-permute-done.15 = bf16[256,2048]{1,0:T(8,128)(2,1)S(1)} collective-permute-done((bf16[256,2048]{1,0:T(8,128)(2,1)S(1)}, bf16[256,2048]{1,0:T(8,128)(2,1)S(1)}, u32[]{:S(2)}, u32[]{:S(2)}) %collective-permute-start.15) | collective-permute-done | bytes 1048608 | tf_op jit(solution)/shard_map/ppermute | solution.py:52
  389.5 20.6 %convert_reduce_fusion.1 = (bf16[2048]{0:T(1024)(128)(2,1)S(1)}, bf16[1024,2048]{1,0:T(8,128)(2,1)}) fusion(f32[1024,2048]{1,0:T(8,128)} %fusion.38, f32[2048]{0:T(1024)S(1)} %dynamic_slice.61, bf16[1024,2048]{1,0:T(8,128)(2,1)S(1)} %bitcast.178, bf16[2048,2048]{1,0:T(8,128)(2,1)} %all-gather.10.cloned.1.call-done), kind=kOutput, calls=%fused_computation.29 | convolution fusion | flops 8636069888 | bytes 25178112 | tf_op jit(solution)/shard_map/dot_general | solution.py:30
  410.1 12.5 %fusion.52 = f32[1024,2048]{1,0:T(8,128)S(1)} fusion(bf16[1024,2048]{1,0:T(8,128)(2,1)} %get-tuple-element.67, bf16[2048,2048]{1,0:T(8,128)(2,1)} %all-gather.8.cloned.1.call-done), kind=kOutput, calls=%fused_computation.149 | convolution fusion | flops 8589934592 | bytes 20971520 | tf_op jit(solution)/shard_map/dot_general | solution.py:26
  426.7 23.4 %collective-permute-done.19 = bf16[256,2048]{1,0:T(8,128)(2,1)S(1)} collective-permute-done((bf16[256,2048]{1,0:T(8,128)(2,1)S(1)}, bf16[256,2048]{1,0:T(8,128)(2,1)S(1)}, u32[]{:S(2)}, u32[]{:S(2)}) %collective-permute-start.19) | collective-permute-done | bytes 1048608 | tf_op jit(solution)/shard_map/ppermute | solution.py:52
  450.1 19.0 %collective-permute-done.20 = bf16[256,2048]{1,0:T(8,128)(2,1)S(1)} collective-permute-done((bf16[256,2048]{1,0:T(8,128)(2,1)S(1)}, bf16[256,2048]{1,0:T(8,128)(2,1)S(1)}, u32[]{:S(2)}, u32[]{:S(2)}) %collective-permute-start.20) | collective-permute-done | bytes 1048608 | tf_op jit(solution)/shard_map/ppermute | solution.py:52
  502.4 23.5 %attend_back.1 = bf16[1024,1536]{1,0:T(8,128)(2,1)} custom-call(bf16[1024,1536]{1,0:T(8,128)(2,1)} %add_convert_fusion.1.q_ref.k_ref.v_ref, bf16[1024,1536]{1,0:T(8,128)(2,1)} %add_convert_fusion.1.q_ref.k_ref.v_ref, bf16[1024,1536]{1,0:T(8,128)(2,1)} %add_convert_fusion.1.q_ref.k_ref.v_ref, bf16[1024,512]{1,0:T(8,128)(2,1)} %bitcast.42.do_ref, ...), custom_call_target="tpu_custom_call" | custom-call | flops 21474836480 | bytes 7340032 | tf_op jit(solution)/shard_map/attend_back/pallas_call | solution.py:192
  579.2 15.9 %convolution_convert_fusion = bf16[2048,2048]{1,0:T(8,128)(2,1)} fusion(bf16[1024,2048]{1,0:T(8,128)(2,1)} %bitcast.180, f32[1024,2048]{1,0:T(8,128)} %fusion.38, f32[2048]{0:T(1024)S(1)} %dynamic_slice.61), kind=kOutput, calls=%fused_computation.35 | convolution fusion | flops 8615100416 | bytes 20979712 | tf_op jit(solution)/shard_map/dot_general | solution.py:34
  595.9 14.8 %convolution_convert_fusion.1 = bf16[2048,2048]{1,0:T(8,128)(2,1)} fusion(bf16[1024,2048]{1,0:T(8,128)(2,1)} %get-tuple-element.67, f32[1024,2048]{1,0:T(8,128)} %subtract_multiply_fusion, f32[2048]{0:T(1024)S(1)} %copy-done.21, f32[2048]{0:T(1024)S(1)} %mul.255), kind=kOutput, calls=%fused_computation.36 | convolution fusion | flops 8600420352 | bytes 20987904 | tf_op jit(solution)/shard_map/dot_general | solution.py:34
  618.4 22.8 %collective-permute-done.22 = bf16[256,2048]{1,0:T(8,128)(2,1)S(1)} collective-permute-done((bf16[256,2048]{1,0:T(8,128)(2,1)S(1)}, bf16[256,2048]{1,0:T(8,128)(2,1)S(1)}, u32[]{:S(2)}, u32[]{:S(2)}) %collective-permute-start.22) | collective-permute-done | bytes 1048608 | tf_op jit(solution)/shard_map/ppermute | solution.py:52
  641.3 18.3 %collective-permute-done.23 = bf16[256,2048]{1,0:T(8,128)(2,1)S(1)} collective-permute-done((bf16[256,2048]{1,0:T(8,128)(2,1)S(1)}, bf16[256,2048]{1,0:T(8,128)(2,1)S(1)}, u32[]{:S(2)}, u32[]{:S(2)}) %collective-permute-start.23) | collective-permute-done | bytes 1048608 | tf_op jit(solution)/shard_map/ppermute | solution.py:52
  670.3 21.1 %reduce-scatter.7.cloned.1.call-done = bf16[64,2048]{1,0:T(8,128)(2,1)} async-done(((bf16[512,2048]{1,0:T(8,128)(2,1)}), bf16[64,2048]{1,0:T(8,128)(2,1)}) %reduce-scatter.7.cloned.1.call-update) | async-done | bytes 262160 | tf_op jit(solution)/shard_map/reduce_scatter | solution.py:342
  693.1 88.8 %reduce-scatter.11.cloned.1.call-done = bf16[256,2048]{1,0:T(8,128)(2,1)} async-done(((bf16[2048,2048]{1,0:T(8,128)(2,1)}), bf16[256,2048]{1,0:T(8,128)(2,1)}) %reduce-scatter.11.cloned.1.call-update) | async-done | bytes 1048592 | tf_op jit(solution)/shard_map/reduce_scatter | solution.py:316
  784.8 87.5 %reduce-scatter.9.cloned.1.call-done = bf16[256,2048]{1,0:T(8,128)(2,1)} async-done(((bf16[2048,2048]{1,0:T(8,128)(2,1)}), bf16[256,2048]{1,0:T(8,128)(2,1)}) %reduce-scatter.9.cloned.1.call-update) | async-done | bytes 1048592 | tf_op jit(solution)/shard_map/reduce_scatter | solution.py:321
  (301 shorter events, 267.9 us)
Async XLA Ops:
  7.3 63.4 %all-gather.6.cloned.1.call-start = ((), (), s32[]{:S(2)}) async-start(), calls=%async_computation.7 | async-start | bytes 2359296 | tf_op jit(solution)/shard_map/all_gather | solution.py:267
  18.4 104.6 %all-gather.12.cloned.1.call-start = ((), (), s32[]{:S(2)}) async-start(), calls=%async_computation.14 | async-start | bytes 7520256 | tf_op jit(solution)/shard_map/all_gather | solution.py:268
  32.6 189.8 %all-gather.8.cloned.1.call-start = ((), (), s32[]{:S(2)}) async-start(), calls=%async_computation.8 | async-start | bytes 9437184 | tf_op jit(solution)/shard_map/all_gather | solution.py:278
  33.3 242.4 %all-gather.10.cloned.1.call-start = ((), (), s32[]{:S(2)}) async-start(), calls=%async_computation.9 | async-start | bytes 9437184 | tf_op jit(solution)/shard_map/all_gather | solution.py:279
  70.7 45.2 %collective-permute-start.8 = (bf16[512,2048]{1,0:T(8,128)(2,1)}, bf16[512,2048]{1,0:T(8,128)(2,1)S(1)}, u32[]{:S(2)}, u32[]{:S(2)}) collective-permute-start(bf16[512,2048]{1,0:T(8,128)(2,1)} %all-gather.6.cloned.1.call-done), channel_id=1, source_target_pairs={{0,8},{8,0},{16,24},{24,16},{1,9},{9,1},{17,25},{25,17},{2,10},{10... | collective-permute-start | bytes 6291464 | tf_op jit(solution)/shard_map/ppermute | solution.py:52
  71.4 46.3 %collective-permute-start.9 = (bf16[512,2048]{1,0:T(8,128)(2,1)}, bf16[512,2048]{1,0:T(8,128)(2,1)S(1)}, u32[]{:S(2)}, u32[]{:S(2)}) collective-permute-start(bf16[512,2048]{1,0:T(8,128)(2,1)} %all-gather.6.cloned.1.call-done), channel_id=1, source_target_pairs={{0,16},{8,24},{16,0},{24,8},{1,17},{9,25},{17,1},{25,9},{2,18},{10... | collective-permute-start | bytes 6291464 | tf_op jit(solution)/shard_map/ppermute | solution.py:52
  117.0 52.2 %collective-permute-start.10 = (bf16[256,2048]{1,0:T(8,128)(2,1)}, bf16[256,2048]{1,0:T(8,128)(2,1)}, u32[]{:S(2)}, u32[]{:S(2)}) collective-permute-start(bf16[256,2048]{1,0:T(8,128)(2,1)} %slice.152), channel_id=1, source_target_pairs={{0,16},{8,24},{16,0},{24,8},{1,17},{9,25},{17,1},{25,9},{2,18},{10... | collective-permute-start | bytes 3145736 | tf_op jit(solution)/shard_map/ppermute | solution.py:52
  118.8 52.7 %collective-permute-start.11 = (bf16[256,2048]{1,0:T(8,128)(2,1)}, bf16[256,2048]{1,0:T(8,128)(2,1)}, u32[]{:S(2)}, u32[]{:S(2)}) collective-permute-start(bf16[256,2048]{1,0:T(8,128)(2,1)} %slice.153), channel_id=1, source_target_pairs={{0,8},{8,0},{16,24},{24,16},{1,9},{9,1},{17,25},{25,17},{2,10},{10... | collective-permute-start | bytes 3145736 | tf_op jit(solution)/shard_map/ppermute | solution.py:52
  296.2 27.1 %collective-permute-start.12 = (bf16[256,2048]{1,0:T(8,128)(2,1)}, bf16[256,2048]{1,0:T(8,128)(2,1)S(1)}, u32[]{:S(2)}, u32[]{:S(2)}) collective-permute-start(bf16[256,2048]{1,0:T(8,128)(2,1)} %get-tuple-element.37), channel_id=1, source_target_pairs={{0,24},{8,16},{16,8},{24,0},{1,25},{9,17},{17,9},{25,1},{2,26},{10... | collective-permute-start | bytes 3145736 | tf_op jit(solution)/shard_map/ppermute | solution.py:52
  298.6 46.6 %collective-permute-start.13 = (bf16[256,2048]{1,0:T(8,128)(2,1)}, bf16[256,2048]{1,0:T(8,128)(2,1)S(1)}, u32[]{:S(2)}, u32[]{:S(2)}) collective-permute-start(bf16[256,2048]{1,0:T(8,128)(2,1)} %get-tuple-element.39), channel_id=1, source_target_pairs={{0,8},{8,0},{16,24},{24,16},{1,9},{9,1},{17,25},{25,17},{2,10},{10... | collective-permute-start | bytes 3145736 | tf_op jit(solution)/shard_map/ppermute | solution.py:52
  299.2 46.0 %collective-permute-start.14 = (bf16[256,2048]{1,0:T(8,128)(2,1)}, bf16[256,2048]{1,0:T(8,128)(2,1)}, u32[]{:S(2)}, u32[]{:S(2)}) collective-permute-start(bf16[256,2048]{1,0:T(8,128)(2,1)} %get-tuple-element.38), channel_id=1, source_target_pairs={{0,16},{8,24},{16,0},{24,8},{1,17},{9,25},{17,1},{25,9},{2,18},{10... | collective-permute-start | bytes 3145736 | tf_op jit(solution)/shard_map/ppermute | solution.py:52
  423.1 27.1 %collective-permute-start.19 = (bf16[256,2048]{1,0:T(8,128)(2,1)S(1)}, bf16[256,2048]{1,0:T(8,128)(2,1)S(1)}, u32[]{:S(2)}, u32[]{:S(2)}) collective-permute-start(bf16[256,2048]{1,0:T(8,128)(2,1)S(1)} %get-tuple-element.34), channel_id=1, source_target_pairs={{0,24},{8,16},{16,8},{24,0},{1,25},{9,17},{17,9},{25,1},{2,26},{10... | collective-permute-start | bytes 3145736 | tf_op jit(solution)/shard_map/ppermute | solution.py:52
  424.6 44.5 %collective-permute-start.20 = (bf16[256,2048]{1,0:T(8,128)(2,1)S(1)}, bf16[256,2048]{1,0:T(8,128)(2,1)S(1)}, u32[]{:S(2)}, u32[]{:S(2)}) collective-permute-start(bf16[256,2048]{1,0:T(8,128)(2,1)S(1)} %get-tuple-element.36), channel_id=1, source_target_pairs={{0,8},{8,0},{16,24},{24,16},{1,9},{9,1},{17,25},{25,17},{2,10},{10... | collective-permute-start | bytes 3145736 | tf_op jit(solution)/shard_map/ppermute | solution.py:52
  425.6 43.9 %collective-permute-start.21 = (bf16[256,2048]{1,0:T(8,128)(2,1)S(1)}, bf16[256,2048]{1,0:T(8,128)(2,1)S(1)}, u32[]{:S(2)}, u32[]{:S(2)}) collective-permute-start(bf16[256,2048]{1,0:T(8,128)(2,1)S(1)} %get-tuple-element.35), channel_id=1, source_target_pairs={{0,16},{8,24},{16,0},{24,8},{1,17},{9,25},{17,1},{25,9},{2,18},{10... | collective-permute-start | bytes 3145736 | tf_op jit(solution)/shard_map/ppermute | solution.py:52
  487.3 175.1 %reduce-scatter.5.cloned.1.call-start = ((), (), s32[]{:S(2)}) async-start(), calls=%async_computation.10 | async-start | bytes 8847360 | tf_op jit(solution)/shard_map/reduce_scatter | solution.py:384
  489.9 58.3 %collective-permute-start.25 = (bf16[256,2048]{1,0:T(8,128)(2,1)}, bf16[256,2048]{1,0:T(8,128)(2,1)S(1)}, u32[]{:S(2)}, u32[]{:S(2)}) collective-permute-start(bf16[256,2048]{1,0:T(8,128)(2,1)} %copy-done.12), channel_id=1, source_target_pairs={{0,8},{8,0},{16,24},{24,16},{1,9},{9,1},{17,25},{25,17},{2,10},{10... | collective-permute-start | bytes 3145736 | tf_op jit(solution)/shard_map/ppermute | solution.py:52
  491.8 58.0 %collective-permute-start.26 = (bf16[256,2048]{1,0:T(8,128)(2,1)}, bf16[256,2048]{1,0:T(8,128)(2,1)}, u32[]{:S(2)}, u32[]{:S(2)}) collective-permute-start(bf16[256,2048]{1,0:T(8,128)(2,1)} %copy-done.12), channel_id=1, source_target_pairs={{0,16},{8,24},{16,0},{24,8},{1,17},{9,25},{17,1},{25,9},{2,18},{10... | collective-permute-start | bytes 3145736 | tf_op jit(solution)/shard_map/ppermute | solution.py:52
  572.1 119.3 %reduce-scatter.7.cloned.1.call-start = ((), (), s32[]{:S(2)}) async-start(), calls=%async_computation.11 | async-start | bytes 2359296 | tf_op jit(solution)/shard_map/reduce_scatter | solution.py:342
  579.2 202.8 %reduce-scatter.11.cloned.1.call-start = ((), (), s32[]{:S(2)}) async-start(), calls=%async_computation.13 | async-start | bytes 9437184 | tf_op jit(solution)/shard_map/reduce_scatter | solution.py:316
  595.2 277.1 %reduce-scatter.9.cloned.1.call-start = ((), (), s32[]{:S(2)}) async-start(), calls=%async_computation.12 | async-start | bytes 9437184 | tf_op jit(solution)/shard_map/reduce_scatter | solution.py:321
  614.2 27.1 %collective-permute-start.22 = (bf16[256,2048]{1,0:T(8,128)(2,1)S(1)}, bf16[256,2048]{1,0:T(8,128)(2,1)S(1)}, u32[]{:S(2)}, u32[]{:S(2)}) collective-permute-start(bf16[256,2048]{1,0:T(8,128)(2,1)S(1)} %get-tuple-element.31), channel_id=1, source_target_pairs={{0,24},{8,16},{16,8},{24,0},{1,25},{9,17},{17,9},{25,1},{2,26},{10... | collective-permute-start | bytes 3145736 | tf_op jit(solution)/shard_map/ppermute | solution.py:52
  615.7 43.8 %collective-permute-start.23 = (bf16[256,2048]{1,0:T(8,128)(2,1)S(1)}, bf16[256,2048]{1,0:T(8,128)(2,1)S(1)}, u32[]{:S(2)}, u32[]{:S(2)}) collective-permute-start(bf16[256,2048]{1,0:T(8,128)(2,1)S(1)} %get-tuple-element.33), channel_id=1, source_target_pairs={{0,8},{8,0},{16,24},{24,16},{1,9},{9,1},{17,25},{25,17},{2,10},{10... | collective-permute-start | bytes 3145736 | tf_op jit(solution)/shard_map/ppermute | solution.py:52
  616.2 43.6 %collective-permute-start.24 = (bf16[256,2048]{1,0:T(8,128)(2,1)S(1)}, bf16[256,2048]{1,0:T(8,128)(2,1)S(1)}, u32[]{:S(2)}, u32[]{:S(2)}) collective-permute-start(bf16[256,2048]{1,0:T(8,128)(2,1)S(1)} %get-tuple-element.32), channel_id=1, source_target_pairs={{0,16},{8,24},{16,0},{24,8},{1,17},{9,25},{17,1},{25,9},{2,18},{10... | collective-permute-start | bytes 3145736 | tf_op jit(solution)/shard_map/ppermute | solution.py:52
  662.4 212.7 %all-to-all-start.2 = ((bf16[4,80,1536]{2,1,0:T(8,128)(2,1)}), bf16[4,80,1536]{2,1,0:T(8,128)(2,1)}, u32[]{:S(2)}, u32[]{:S(2)}) async-start(bf16[4,80,1536]{2,1,0:T(8,128)(2,1)} %bitcast.192), calls=%async_computation.3 | async-start | bytes 1966080 | tf_op jit(solution)/shard_map/all_to_all | solution.py:390
  (51 other events, 841.4 us)
Sparse Core Ops, SparseCore 0:
  9.7 31.8 all-gather.5
  43.9 67.3 all-gather.11
  112.9 80.6 all-gather.7
  195.1 80.5 all-gather.9
  572.2 82.2 reduce-scatter.4
  657.2 34.1 reduce-scatter.6
  693.7 88.2 reduce-scatter.10
  784.3 87.9 reduce-scatter.8

commit v2 on v1

v2 whole, which is shorter than its diff:
```python
import functools

import jax
import jax.numpy as jnp
from jax import lax
from jax.experimental import pallas as pl
from jax.experimental.pallas import tpu as pltpu
from jax.sharding import PartitionSpec as P

HEADS = 32
HEAD_DIM = 64
TILE = 128
PAIR = 2 * HEAD_DIM
Q_BLOCK = 256
FFN_ROWS = 512
EXTRA = 128
EPSILON = 1e-05
GELU_C = 0.7978845608028654
GELU_K = 0.044715
NEGATIVE = -1e30
VMEM_LIMIT = 56 * 1024 * 1024
LOW = jnp.bfloat16
WIDE = jnp.float32


def product(left, right):
    return jnp.dot(left, right, preferred_element_type=WIDE)


def product_t(left, right):
    return lax.dot_general(left, right, (((1,), (1,)), ((), ())), preferred_element_type=WIDE)


def product_rows(left, right):
    return lax.dot_general(left, right, (((0,), (0,)), ((), ())), preferred_element_type=WIDE)


def norm_stats(values):
    centre = jnp.mean(values, axis=-1, keepdims=True)
    centred = values - centre
    spread = jnp.mean(centred * centred, axis=-1, keepdims=True)
    return centre, lax.rsqrt(spread + EPSILON)


def norm_backward(upstream, normed, inverse, gain):
    graded = upstream * gain
    first = jnp.mean(graded, axis=-1, keepdims=True)
    second = jnp.mean(graded * normed, axis=-1, keepdims=True)
    return inverse * (graded - first - normed * second)


def flip(values, axis, bit, size):
    return lax.ppermute(values, axis, [(i, i ^ bit) for i in range(size)])


def tie(*values):
    return lax.optimization_barrier(values)


def gather_start(values, n_seq):
    if n_seq != 4:
        return [values] + [flip(values, "seq", bit, n_seq) for bit in range(1, n_seq)]
    return [values, flip(values, "seq", 1, 4), flip(values, "seq", 2, 4)]


def gather_end(held, n_seq):
    if n_seq != 4:
        return held
    values, one, two = held
    half = values.shape[0] // 2
    low = flip(one[:half], "seq", 2, 4)
    high = flip(two[half:], "seq", 1, 4)
    return [values, one, two, jnp.concatenate([low, high], axis=0)]


def exchange(blocks, n_seq):
    return [blocks[0]] + [flip(blocks[bit], "seq", bit, n_seq) for bit in range(1, n_seq)]


def scatter_split(values, n_seq):
    count = values.shape[0] // n_seq
    if n_seq != 4:
        return [values[bit * count : (bit + 1) * count] for bit in range(n_seq)]
    half = count // 2

    def piece(bit, part):
        return values[bit * count + part * half : bit * count + (part + 1) * half]

    return [
        values[:count],
        jnp.concatenate([piece(1, 0), piece(3, 0)], axis=0),
        jnp.concatenate([piece(2, 1), piece(3, 1)], axis=0),
        piece(2, 0),
        piece(1, 1),
    ]


def scatter_send(blocks, n_seq):
    if n_seq != 4:
        return [[block] for block in exchange(blocks, n_seq)]
    own, first, second, then_second, then_first = blocks
    half = own.shape[0] // 2
    first, second = flip(first, "seq", 1, 4), flip(second, "seq", 2, 4)
    then_second = (then_second.astype(WIDE) + first[half:].astype(WIDE)).astype(LOW)
    then_first = (then_first.astype(WIDE) + second[half:].astype(WIDE)).astype(LOW)
    then_second, then_first = flip(then_second, "seq", 2, 4), flip(then_first, "seq", 1, 4)
    return [[own], [first, second], [then_second, then_first]]


def scatter_end(parts):
    count = parts[0][0].shape[0]
    total = parts[0][0].astype(WIDE)
    for part in parts[1:]:
        rows = count // len(part)
        total = total + jnp.concatenate([piece[:rows] for piece in part], axis=0).astype(WIDE)
    return total


def pair_split(left, n_batch):
    side = lax.axis_index("batch") & 1
    blocks = left.reshape(left.shape[0], n_batch // 2, 2, left.shape[1] // n_batch)
    sent = lax.dynamic_index_in_dim(blocks, 1 - side, 2, False)
    kept = lax.dynamic_index_in_dim(blocks, side, 2, False)
    return sent.reshape(left.shape[0], -1), kept.reshape(left.shape[0], -1)


def rows_kernel(side_ref, left_ref, right_ref, *refs):
    total = product_rows(left_ref[...], right_ref[...])
    if len(refs) == 2:
        total += refs[0][...].astype(WIDE)
    refs[-1][...] = total.astype(LOW)


def rows_product(side, left, right, added, n_batch):
    length, columns = left.shape
    width = right.shape[1]
    count = columns // n_batch
    block = pl.BlockSpec((count, width), lambda k, side: (k, 0))
    return pl.pallas_call(
        rows_kernel,
        grid_spec=pltpu.PrefetchScalarGridSpec(
            num_scalar_prefetch=1,
            grid=(n_batch // 2,),
            in_specs=[
                pl.BlockSpec((length, count), lambda k, side: (0, 2 * k + side[0])),
                pl.BlockSpec((length, width), lambda k, side: (0, 0), pipeline_mode=pl.Buffered(1)),
            ]
            + [block] * len(added),
            out_specs=block,
        ),
        out_shape=jax.ShapeDtypeStruct((columns // 2, width), LOW),
        compiler_params=pltpu.CompilerParams(vmem_limit_bytes=VMEM_LIMIT),
        cost_estimate=pl.CostEstimate(flops=length * width, bytes_accessed=length, transcendentals=0),
        name="rows_product",
    )(side, left, right, *added)


def pair_rows(left, right, n_batch):
    if left.shape[1] // n_batch % 128:
        return pair_product(*pair_split(left, n_batch), right, n_batch)
    side = (lax.axis_index("batch") & 1).reshape(1)
    moved = flip(rows_product(1 - side, left, right, (), n_batch), "batch", 1, n_batch)
    return rows_product(side, left, right, (moved,), n_batch)


def pair_product(sent, kept, right, n_batch):
    moved = flip(product_rows(sent, right).astype(LOW), "batch", 1, n_batch)
    return (product_rows(kept, right) + moved.astype(WIDE)).astype(LOW)


def scatter_batch(total, n_batch):
    groups = [list(range(0, n_batch, 2)), list(range(1, n_batch, 2))]
    return lax.psum_scatter(
        total,
        "batch",
        scatter_dimension=0,
        tiled=True,
        axis_index_groups=groups,
    )


def key_range(q_start, q_count, length):
    low = max(0, (q_start - (length // 2 - 1)) // q_count * q_count)
    return low, q_start + q_count


def block_mask(starts, low, high, q_start, q_count):
    shape = (high - low, q_count)
    key = low + lax.broadcasted_iota(jnp.int32, shape, 0)
    query = q_start + lax.broadcasted_iota(jnp.int32, shape, 1)
    return (key <= query) & (key >= starts)


def load_natural(me, pairs):
    for source, target in pairs:
        for block in range(target.shape[0] // Q_BLOCK):
            at = pl.multiple_of((block ^ me) * Q_BLOCK, Q_BLOCK)
            target[block * Q_BLOCK : (block + 1) * Q_BLOCK, :] = source[pl.ds(at, Q_BLOCK), :]


def attend_kernel(me_ref, q_ref, k_ref, v_ref, start_ref, o_ref, lse_ref, k_own, v_own):
    length = q_ref.shape[0]
    me = me_ref[0]
    load_natural(me, ((k_ref, k_own), (v_ref, v_own)))
    lane = lax.broadcasted_iota(jnp.int32, (1, PAIR), 1)
    row = lax.broadcasted_iota(jnp.int32, (PAIR, 1), 0)
    for q_start in range(0, length, Q_BLOCK):
        low, high = key_range(q_start, Q_BLOCK, length)
        here = slice(q_start, q_start + Q_BLOCK)
        there = pl.ds(pl.multiple_of((q_start // Q_BLOCK ^ me) * Q_BLOCK, Q_BLOCK), Q_BLOCK)
        q, k, v = q_ref[there, :], k_own[low:high, :], v_own[low:high, :]
        allowed = block_mask(start_ref[:, here], low, high, q_start, Q_BLOCK)
        mixed = []
        for head in range(2):
            mine = (lane >= head * HEAD_DIM) & (lane < (head + 1) * HEAD_DIM)
            q_head = jnp.where(mine, q, jnp.zeros_like(q))
            scores = product_t(k, q_head) * HEAD_DIM ** (-0.5)
            scores = jnp.where(allowed, scores, NEGATIVE)
            peak = jnp.max(scores, axis=0, keepdims=True)
            raised = jnp.exp(scores - peak)
            total = jnp.sum(raised, axis=0, keepdims=True)
            probs = (raised / total).astype(LOW)
            mixed.append(product_rows(v, probs))
            lse_ref[0, head : head + 1, here] = peak + jnp.log(total)
        joined = jnp.where(row < HEAD_DIM, mixed[0], mixed[1])
        o_ref[there, :] = joined.T.astype(LOW)


def attend(me, qkv, starts, width):
    length = qkv.shape[0]
    pairs = width // PAIR
    return pl.pallas_call(
        attend_kernel,
        grid_spec=pltpu.PrefetchScalarGridSpec(
            num_scalar_prefetch=1,
            grid=(pairs,),
            in_specs=[
                pl.BlockSpec((length, PAIR), lambda j, me: (0, j)),
                pl.BlockSpec((length, PAIR), lambda j, me: (0, pairs + j)),
                pl.BlockSpec((length, PAIR), lambda j, me: (0, 2 * pairs + j)),
                pl.BlockSpec((1, length), lambda j, me: (0, 0)),
            ],
            out_specs=[
                pl.BlockSpec((length, PAIR), lambda j, me: (0, j)),
                pl.BlockSpec((1, 2, length), lambda j, me: (j, 0, 0)),
            ],
            scratch_shapes=[pltpu.VMEM((length, PAIR), LOW), pltpu.VMEM((length, PAIR), LOW)],
        ),
        out_shape=[
            jax.ShapeDtypeStruct((length, width), LOW),
            jax.ShapeDtypeStruct((pairs, 2, length), WIDE),
        ],
        compiler_params=pltpu.CompilerParams(vmem_limit_bytes=VMEM_LIMIT),
        cost_estimate=pl.CostEstimate(
            flops=16 * length * length * width,
            bytes_accessed=8 * length * width,
            transcendentals=length * length * width // HEAD_DIM,
        ),
        name="attend",
    )(me, qkv, qkv, qkv, starts)


def attend_back_kernel(
    me_ref, q_ref, k_ref, v_ref, do_ref, start_ref, lse_ref, out_ref, k_own, v_own, dk_acc, dv_acc
):
    length = q_ref.shape[0]
    width = out_ref.shape[1] // 3
    me = me_ref[0]
    at = pl.program_id(0) * PAIR
    scale = HEAD_DIM ** (-0.5)
    lane = lax.broadcasted_iota(jnp.int32, (1, PAIR), 1)
    row = lax.broadcasted_iota(jnp.int32, (PAIR, 1), 0)
    load_natural(me, ((k_ref, k_own), (v_ref, v_own)))
    dk_acc[...] = jnp.zeros_like(dk_acc)
    dv_acc[...] = jnp.zeros_like(dv_acc)
    for q_start in range(0, length, Q_BLOCK):
        low, high = key_range(q_start, Q_BLOCK, length)
        here = slice(q_start, q_start + Q_BLOCK)
        there = pl.ds(pl.multiple_of((q_start // Q_BLOCK ^ me) * Q_BLOCK, Q_BLOCK), Q_BLOCK)
        q, k, v, do = q_ref[there, :], k_own[low:high, :], v_own[low:high, :], do_ref[there, :]
        allowed = block_mask(start_ref[:, here], low, high, q_start, Q_BLOCK)
        d_query = []
        for head in range(2):
            mine = (lane >= head * HEAD_DIM) & (lane < (head + 1) * HEAD_DIM)
            q_head = jnp.where(mine, q, jnp.zeros_like(q))
            do_head = jnp.where(mine, do, jnp.zeros_like(do))
            scores = product_t(k, q_head) * scale - lse_ref[0, head : head + 1, here]
            probs = jnp.exp(jnp.where(allowed, scores, NEGATIVE))
            d_probs = product_t(v, do_head)
            delta = jnp.sum(probs * d_probs, axis=0, keepdims=True)
            d_scores = (probs * (d_probs - delta)).astype(LOW)
            d_query.append(product_rows(k, d_scores))
            dk_acc[low:high, :] += product(d_scores, q_head)
            dv_acc[low:high, :] += product(probs.astype(LOW), do_head)
        joined = jnp.where(row < HEAD_DIM, d_query[0], d_query[1]) * scale
        out_ref[there, pl.ds(pl.multiple_of(at, PAIR), PAIR)] = joined.T.astype(LOW)
    for q_start in range(0, length, Q_BLOCK):
        here = slice(q_start, q_start + Q_BLOCK)
        there = pl.ds(pl.multiple_of((q_start // Q_BLOCK ^ me) * Q_BLOCK, Q_BLOCK), Q_BLOCK)
        d_key = (dk_acc[here, :] * scale).astype(LOW)
        out_ref[there, pl.ds(pl.multiple_of(width + at, PAIR), PAIR)] = d_key
        d_value = dv_acc[here, :].astype(LOW)
        out_ref[there, pl.ds(pl.multiple_of(2 * width + at, PAIR), PAIR)] = d_value


def attend_back(me, qkv, d_mixed, starts, logsum, width):
    length = qkv.shape[0]
    pairs = width // PAIR
    return pl.pallas_call(
        attend_back_kernel,
        grid_spec=pltpu.PrefetchScalarGridSpec(
            num_scalar_prefetch=1,
            grid=(pairs,),
            in_specs=[
                pl.BlockSpec((length, PAIR), lambda j, me: (0, j)),
                pl.BlockSpec((length, PAIR), lambda j, me: (0, pairs + j)),
                pl.BlockSpec((length, PAIR), lambda j, me: (0, 2 * pairs + j)),
                pl.BlockSpec((length, PAIR), lambda j, me: (0, j)),
                pl.BlockSpec((1, length), lambda j, me: (0, 0)),
                pl.BlockSpec((1, 2, length), lambda j, me: (j, 0, 0)),
            ],
            out_specs=pl.BlockSpec((length, 3 * width), lambda j, me: (0, 0)),
            scratch_shapes=[
                pltpu.VMEM((length, PAIR), LOW),
                pltpu.VMEM((length, PAIR), LOW),
                pltpu.VMEM((length, PAIR), WIDE),
                pltpu.VMEM((length, PAIR), WIDE),
            ],
        ),
        out_shape=jax.ShapeDtypeStruct((length, 3 * width), LOW),
        compiler_params=pltpu.CompilerParams(vmem_limit_bytes=VMEM_LIMIT),
        cost_estimate=pl.CostEstimate(
            flops=40 * length * length * width,
            bytes_accessed=14 * length * width,
            transcendentals=length * length * width // HEAD_DIM,
        ),
        name="attend_back",
    )(me, qkv, qkv, qkv, d_mixed, starts, logsum)


def out_norm_kernel(n_seq, *refs):
    o_refs = refs[:n_seq]
    w_ref, row_ref, active_ref, bias_ref, gain_ref, shift_ref = refs[n_seq : n_seq + 6]
    low_ref, middle_ref, normed_ref, inverse_ref = refs[n_seq + 6 :]
    depth = o_refs[0].shape[1]
    branch = product(o_refs[0][...], w_ref[:depth, :])
    for block in range(1, n_seq):
        branch += product(o_refs[block][...], w_ref[block * depth : (block + 1) * depth, :])
    middle = row_ref[...].astype(WIDE) + active_ref[...] * (branch + bias_ref[...])
    centre, inverse = norm_stats(middle)
    normed = (middle - centre) * inverse
    low_ref[...] = (normed * gain_ref[...] + shift_ref[...]).astype(LOW)

    @pl.when(pl.program_id(0) == 0)
    def _():
        middle_ref[...] = middle
        normed_ref[...] = normed
        inverse_ref[...] = inverse


def out_norm(mixed_all, out_full, row_low, active_row, bias, gain, shift, n_seq):
    length, width = row_low.shape
    count = length // n_seq
    depth = width // n_seq

    def mixed_spec(bit):
        return pl.BlockSpec((count, depth), lambda k: (k ^ bit, 0))

    vector = pl.BlockSpec((1, width), lambda k: (0, 0))
    block = pl.BlockSpec((count, width), lambda k: (k, 0))
    first = pl.BlockSpec((count, width), lambda k: (0, 0))
    return pl.pallas_call(
        functools.partial(out_norm_kernel, n_seq),
        grid=(n_seq,),
        in_specs=[mixed_spec(bit) for bit in range(n_seq)]
        + [
            pl.BlockSpec((width, width), lambda k: (0, 0)),
            block,
            pl.BlockSpec((count, 1), lambda k: (k, 0)),
            vector,
            vector,
            vector,
        ],
        out_specs=[block, first, first, pl.BlockSpec((count, 1), lambda k: (0, 0))],
        out_shape=[
            jax.ShapeDtypeStruct((length, width), LOW),
            jax.ShapeDtypeStruct((count, width), WIDE),
            jax.ShapeDtypeStruct((count, width), WIDE),
            jax.ShapeDtypeStruct((count, 1), WIDE),
        ],
        compiler_params=pltpu.CompilerParams(vmem_limit_bytes=VMEM_LIMIT),
        cost_estimate=pl.CostEstimate(
            flops=2 * length * width * width,
            bytes_accessed=2 * width * width + 6 * length * width,
            transcendentals=length,
        ),
        name="out_norm",
    )(
        *mixed_all,
        out_full,
        row_low,
        active_row,
        bias.reshape(1, width),
        gain.reshape(1, width),
        shift.reshape(1, width),
    )


def assemble_kernel(me_ref, joined_ref, full_ref, extra_ref):
    own = joined_ref.shape[2]
    width = full_ref.shape[1]
    for member in range(joined_ref.shape[0]):
        rows = slice(member * own, (member + 1) * own)
        full_ref[rows, :] = joined_ref[member, 0, :, :width]
        extra_ref[rows, :] = joined_ref[member, 0, :, width:]


def assemble(me, joined, width):
    n_batch, n_seq, own, columns = joined.shape
    count = n_batch * own
    return pl.pallas_call(
        assemble_kernel,
        grid_spec=pltpu.PrefetchScalarGridSpec(
            num_scalar_prefetch=1,
            grid=(n_seq,),
            in_specs=[
                pl.BlockSpec((n_batch, 1, own, columns), lambda j, me: (0, j ^ me[0], 0, 0)),
            ],
            out_specs=[
                pl.BlockSpec((count, width), lambda j, me: (j, 0)),
                pl.BlockSpec((count, EXTRA), lambda j, me: (j, 0)),
            ],
        ),
        out_shape=[
            jax.ShapeDtypeStruct((n_seq * count, width), LOW),
            jax.ShapeDtypeStruct((n_seq * count, EXTRA), LOW),
        ],
        compiler_params=pltpu.CompilerParams(vmem_limit_bytes=VMEM_LIMIT),
        name="assemble",
    )(me, joined)


def ffn_up_kernel(n_ref, w_ref, bias_ref, hidden_ref, slope_ref):
    step = 512
    for at in range(0, w_ref.shape[0], step):
        here = slice(at, at + step)
        before = product_t(n_ref[...], w_ref[here, :]) + bias_ref[:, here]
        square = before * before
        tangent = jnp.tanh(before * (GELU_C + GELU_C * GELU_K * square))
        half = 0.5 + 0.5 * tangent
        hidden = before * half
        hidden_ref[:, here] = hidden.astype(LOW)
        slope_ref[:, here] = half + hidden * (1.0 - tangent) * (
            GELU_C + 3.0 * GELU_C * GELU_K * square
        )


def ffn_up(normed, w_up, bias):
    length, width = normed.shape
    hidden = w_up.shape[0]
    return pl.pallas_call(
        ffn_up_kernel,
        grid=(length // FFN_ROWS,),
        in_specs=[
            pl.BlockSpec((FFN_ROWS, width), lambda k: (k, 0)),
            pl.BlockSpec((hidden, width), lambda k: (0, 0), pipeline_mode=pl.Buffered(1)),
            pl.BlockSpec((1, hidden), lambda k: (0, 0)),
        ],
        out_specs=[
            pl.BlockSpec((FFN_ROWS, hidden), lambda k: (k, 0)),
            pl.BlockSpec((FFN_ROWS, hidden), lambda k: (k, 0)),
        ],
        out_shape=[
            jax.ShapeDtypeStruct((length, hidden), LOW),
            jax.ShapeDtypeStruct((length, hidden), WIDE),
        ],
        compiler_params=pltpu.CompilerParams(vmem_limit_bytes=VMEM_LIMIT),
        cost_estimate=pl.CostEstimate(
            flops=2 * length * width * hidden,
            bytes_accessed=2 * width * (hidden + length) + 6 * length * hidden,
            transcendentals=length * hidden,
        ),
        name="ffn_up",
    )(normed, w_up, bias.reshape(1, hidden))


def ffn_back_kernel(n_seq, grad_ref, slope_ref, down_ref, up_ref, d_before_ref, sum_ref, *refs):
    outs, (down, up, sems) = refs[:-3], refs[-3:]
    index = pl.program_id(0)
    load_down = pltpu.make_async_copy(down_ref, down, sems.at[0])
    load_up = pltpu.make_async_copy(up_ref, up, sems.at[1])

    @pl.when(index == 0)
    def _():
        load_down.start()
        load_up.start()
        sum_ref[...] = jnp.zeros_like(sum_ref)
        load_down.wait()

    step = 512
    for at in range(0, down.shape[0], step):
        here = slice(at, at + step)
        d_hidden = product_t(grad_ref[...], down[here, :])
        d_before = (d_hidden * slope_ref[:, here]).astype(LOW)
        d_before_ref[:, here] = d_before
        sum_ref[:, here] += jnp.sum(d_before.astype(WIDE), axis=0, keepdims=True)

    @pl.when(index == 0)
    def _():
        load_up.wait()

    d_normed = product(d_before_ref[...], up[...]).astype(LOW)
    half = d_normed.shape[0] // 2
    if n_seq != 4:
        places = [[(outs[bit], 0, slice(None))] for bit in range(n_seq)]
    else:
        own, first, second, then_second, then_first = outs
        upper, lower = slice(0, half), slice(half, 2 * half)
        places = [
            [(own, 0, slice(None))],
            [(first, 0, upper), (then_first, 0, lower)],
            [(then_second, 0, upper), (second, 0, lower)],
            [(first, half, upper), (second, half, lower)],
        ]
    for bit, targets in enumerate(places):

        @pl.when(index == bit)
        def _():
            for target, at, rows in targets:
                piece = d_normed[rows]
                target[at : at + piece.shape[0], :] = piece


def ffn_back(grad_row, slope, w_down, w_up, n_seq):
    length, width = grad_row.shape
    hidden = w_up.shape[0]
    count = length // n_seq
    sizes = [count] * n_seq if n_seq != 4 else [count, count, count, count // 2, count // 2]
    return pl.pallas_call(
        functools.partial(ffn_back_kernel, n_seq),
        grid=(n_seq,),
        in_specs=[
            pl.BlockSpec((count, width), lambda k: (k, 0)),
            pl.BlockSpec((count, hidden), lambda k: (k, 0)),
            pl.BlockSpec(memory_space=pl.ANY),
            pl.BlockSpec(memory_space=pl.ANY),
        ],
        out_specs=[
            pl.BlockSpec((count, hidden), lambda k: (k, 0)),
            pl.BlockSpec((1, hidden), lambda k: (0, 0)),
        ]
        + [pl.BlockSpec((size, width), lambda k: (0, 0)) for size in sizes],
        out_shape=[
            jax.ShapeDtypeStruct((length, hidden), LOW),
            jax.ShapeDtypeStruct((1, hidden), WIDE),
        ]
        + [jax.ShapeDtypeStruct((size, width), LOW) for size in sizes],
        scratch_shapes=[
            pltpu.VMEM((hidden, width), LOW),
            pltpu.VMEM((hidden, width), LOW),
            pltpu.SemaphoreType.DMA((2,)),
        ],
        compiler_params=pltpu.CompilerParams(vmem_limit_bytes=VMEM_LIMIT),
        cost_estimate=pl.CostEstimate(flops=length * width, bytes_accessed=length, transcendentals=0),
        name="ffn_back",
    )(grad_row, slope, w_down, w_up)


def norm_back_kernel(pieces, *refs):
    n_parts = sum(pieces)
    parts, at = [], 0
    for number in pieces:
        parts.append(refs[at : at + number])
        at += number
    cot_ref, normed_ref, inverse_ref, active_ref, gain_ref, w_ref = refs[n_parts : n_parts + 6]
    d_middle_ref, d_branch_ref, d_mixed_ref, sums_ref = refs[n_parts + 6 :]

    @pl.when(pl.program_id(0) == 0)
    def _():
        upstream = parts[0][0][...].astype(WIDE)
        for part in parts[1:]:
            upstream += jnp.concatenate([piece[...] for piece in part], axis=0).astype(WIDE)
        normed = normed_ref[...]
        d_middle = cot_ref[...].astype(WIDE) + norm_backward(
            upstream, normed, inverse_ref[...], gain_ref[...]
        )
        d_middle_ref[...] = d_middle
        d_branch = (d_middle * active_ref[...]).astype(LOW)
        d_branch_ref[...] = d_branch
        sums_ref[...] = jnp.zeros_like(sums_ref)
        sums_ref[0:1, :] = jnp.sum(upstream * normed, axis=0, keepdims=True)
        sums_ref[1:2, :] = jnp.sum(upstream, axis=0, keepdims=True)
        sums_ref[2:3, :] = jnp.sum(d_branch.astype(WIDE), axis=0, keepdims=True)

    d_mixed_ref[0] = product_t(d_branch_ref[...], w_ref[...]).astype(LOW)


def norm_back(parts, cotangent, normed, inverse, active, gain, out_full, n_seq):
    count, width = cotangent.shape
    depth = width // n_seq
    block = pl.BlockSpec((count, width), lambda j: (0, 0))
    column = pl.BlockSpec((count, 1), lambda j: (0, 0))
    return pl.pallas_call(
        functools.partial(norm_back_kernel, [len(part) for part in parts]),
        grid=(n_seq,),
        in_specs=[
            pl.BlockSpec((count // len(part), width), lambda j: (0, 0)) for part in parts for piece in part
        ]
        + [block, block]
        + [
            column,
            column,
            pl.BlockSpec((1, width), lambda j: (0, 0)),
            pl.BlockSpec((depth, width), lambda j: (j, 0)),
        ],
        out_specs=[
            block,
            block,
            pl.BlockSpec((1, count, depth), lambda j: (j, 0, 0)),
            pl.BlockSpec((8, width), lambda j: (0, 0)),
        ],
        out_shape=[
            jax.ShapeDtypeStruct((count, width), WIDE),
            jax.ShapeDtypeStruct((count, width), LOW),
            jax.ShapeDtypeStruct((n_seq, count, depth), LOW),
            jax.ShapeDtypeStruct((8, width), WIDE),
        ],
        compiler_params=pltpu.CompilerParams(vmem_limit_bytes=VMEM_LIMIT),
        cost_estimate=pl.CostEstimate(flops=count * width, bytes_accessed=count, transcendentals=0),
        name="norm_back",
    )(
        *[piece for part in parts for piece in part],
        cotangent,
        normed,
        inverse,
        active,
        gain.reshape(1, width),
        out_full,
    )


def format_kernel(n_seq, me_ref, *refs):
    out_ref = refs[n_seq]
    width = out_ref.shape[1] // 3
    count = width // n_seq
    for block in range(n_seq):
        ref = refs[block]
        for kind in range(3):
            at = kind * width + (me_ref[0] ^ block) * count
            at = pl.multiple_of(at, count)
            out_ref[:, pl.ds(at, count)] = ref[:, kind * count : (kind + 1) * count].astype(WIDE)


def format_qkv(me, blocks, width, n_seq):
    own = blocks[0].shape[0]
    return pl.pallas_call(
        functools.partial(format_kernel, n_seq),
        grid_spec=pltpu.PrefetchScalarGridSpec(
            num_scalar_prefetch=1,
            grid=(1,),
            in_specs=[pl.BlockSpec(blocks[0].shape, lambda i, me: (0, 0))] * n_seq,
            out_specs=pl.BlockSpec((own, 3 * width), lambda i, me: (0, 0)),
        ),
        out_shape=jax.ShapeDtypeStruct((own, 3 * width), WIDE),
        compiler_params=pltpu.CompilerParams(vmem_limit_bytes=VMEM_LIMIT),
        name="format_qkv",
    )(me, *blocks)


def gather_shared(values, n_seq, n_batch):
    half = values.shape[0] // 2
    side = lax.axis_index("batch") & 1
    mine = lax.dynamic_slice_in_dim(values, side * half, half, 0)
    held = gather_end(gather_start(mine, n_seq), n_seq)[1:]
    other = [flip(block, "batch", 1, n_batch) for block in held]
    blocks = [values]
    for mine, theirs in zip(held, other):
        blocks.append(jnp.where(side == 0, mine, theirs))
        blocks.append(jnp.where(side == 0, theirs, mine))
    return blocks


def shards(
    n_seq,
    n_batch,
    tokens,
    cotangent,
    segment_ids,
    exit_mask,
    ln1_gain,
    ln1_bias,
    w_qkv,
    b_qv,
    w_out,
    b_out,
    ln2_gain,
    ln2_bias,
    w_up,
    b_up,
    w_down,
    b_down,
):
    _, local_len, width = tokens.shape
    length = n_seq * local_len
    own = w_qkv.shape[0]
    head_width = width // n_seq
    n_all = n_seq * n_batch
    me = lax.axis_index("seq")
    tokens = tokens.reshape(local_len, width)
    cotangent = cotangent.reshape(local_len, width)

    small_parts = (ln1_gain, ln1_bias, b_qv, b_out, ln2_gain, ln2_bias, b_up, b_down)
    sizes = [part.shape[0] for part in small_parts]
    n_small = sum(sizes)
    tiles = exit_mask.shape[1]
    part_width = 3 * head_width
    small = jnp.concatenate(small_parts + (exit_mask.reshape(-1).astype(LOW),))
    lanes = -(-small.shape[0] // own)
    small = jnp.pad(small, (0, own * lanes - small.shape[0])).reshape(own, lanes)
    small = jnp.pad(small, ((0, 0), (0, EXTRA - lanes)))

    by_head = w_qkv.reshape(own, 3, n_seq, head_width).transpose(2, 0, 1, 3)
    by_head = by_head.reshape(n_seq, own, part_width)
    moved = exchange(
        [
            jnp.concatenate([lax.dynamic_index_in_dim(by_head, me ^ bit, 0, False), small], axis=1)
            for bit in range(n_seq)
        ],
        n_seq,
    )
    moved = jnp.concatenate(moved, axis=0).reshape(n_seq, own, part_width + EXTRA)
    out_part = lax.all_gather(w_out, "batch", axis=0, tiled=True)
    joined = lax.all_gather(moved.reshape(n_seq * own, part_width + EXTRA), "batch", axis=0)
    up_all = lax.all_gather(w_up, "batch", axis=0, tiled=True)
    down_all = lax.all_gather(w_down, "batch", axis=0, tiled=True)
    hidden_count = up_all.shape[0]

    def unpack(extra):
        return extra[..., :lanes].reshape(extra.shape[:-2] + (own * lanes,))

    mask_row = unpack(moved[..., part_width:])[:, n_small : n_small + tiles]
    active_row = jnp.repeat(mask_row.reshape(-1), TILE).astype(WIDE).reshape(length, 1)
    joined = joined.reshape(n_batch, n_seq, own, part_width + EXTRA)
    qkv_full, small_all = assemble(me.reshape(1), joined, part_width)
    small_all = unpack(small_all.reshape(n_seq, n_batch, own, EXTRA)).astype(WIDE)
    params, at = [], 0
    for size in sizes:
        params.append(small_all[:, :, at : at + size].reshape(-1))
        at += size
    gain_one, bias_one, qv_bias, out_bias, gain_two, bias_two, up_bias_all, down_bias = params
    up_bias = lax.dynamic_slice_in_dim(up_bias_all, me * hidden_count, hidden_count)

    held_row = gather_start(tokens, n_seq)
    *held_row, out_part = tie(*gather_end(held_row, n_seq), out_part)
    row_low = jnp.concatenate(held_row, axis=0)
    out_full = jnp.concatenate(gather_shared(out_part, n_seq, n_batch), axis=0)
    active = jnp.repeat(exit_mask.reshape(-1), TILE).astype(WIDE).reshape(local_len, 1)
    grad_low = (cotangent.astype(WIDE) * active).astype(LOW)
    row_low, out_full, grad_low = tie(row_low, out_full, grad_low)
    held_grad = gather_start(grad_low, n_seq)
    row = row_low.astype(WIDE)
    centre_one, inverse_one = norm_stats(row)
    normed_one = (row - centre_one) * inverse_one
    normed_low = (normed_one * gain_one + bias_one).astype(LOW)
    normed_low, *held_grad = tie(normed_low, *held_grad)
    own_q = lax.dynamic_slice_in_dim(qv_bias, me * head_width, head_width)
    own_v = lax.dynamic_slice_in_dim(qv_bias, width + me * head_width, head_width)
    own_bias = jnp.concatenate([own_q, jnp.zeros_like(own_q), own_v])
    qkv = (product(normed_low, qkv_full) + own_bias).astype(LOW)
    qkv, *held_grad = tie(qkv, *gather_end(held_grad, n_seq))
    grad_row = jnp.concatenate(held_grad, axis=0)
    segment_row = segment_ids.reshape(length)
    starts = jnp.sum(
        (segment_row[None, :] < segment_row[:, None]).astype(jnp.int32), axis=1
    ).reshape(1, length)
    mixed, logsum = attend(me.reshape(1), qkv, starts, head_width)
    mixed_all = gather_end(gather_start(mixed, n_seq), n_seq)
    side = lax.axis_index("batch") & 1
    normed_halves = normed_low.reshape(length, n_seq, n_batch // 2, 2, own).transpose(3, 0, 2, 1, 4)
    normed_halves = normed_halves.reshape(2, length, width // 2)
    normed_sent = lax.dynamic_index_in_dim(normed_halves, 1 - side, 0, False)
    normed_kept = lax.dynamic_index_in_dim(normed_halves, side, 0, False)
    mixed_sent, mixed_kept = pair_split(mixed, n_batch)
    normed_two_low, middle_own, normed_own, inverse_own = out_norm(
        mixed_all, out_full, row_low, active_row, out_bias, gain_two, bias_two, n_seq
    )

    hidden_low, slope = ffn_up(normed_two_low, up_all, up_bias)
    grad_down_part = pair_rows(hidden_low, grad_row, n_batch)
    grad_down_part, down_all, normed_sent, normed_kept, mixed_sent, mixed_kept = tie(
        grad_down_part, down_all, normed_sent, normed_kept, mixed_sent, mixed_kept
    )
    grad_down = scatter_batch(grad_down_part, n_batch)
    d_before, grad_upb, *blocks = ffn_back(grad_row, slope, down_all, up_all, n_seq)
    parts = scatter_send(blocks, n_seq)
    grad_up_part = pair_rows(d_before, normed_two_low, n_batch)
    feed_part = product(hidden_low, down_all).astype(LOW)
    parts[0][0], grad_up_part, feed_part, grad_down = tie(
        parts[0][0], grad_up_part, feed_part, grad_down
    )
    grad_up = scatter_batch(grad_up_part, n_batch)
    grad_downb = jnp.sum(grad_low.astype(WIDE), axis=0)

    d_middle, d_branch, d_mixed, sums = norm_back(
        parts, cotangent, normed_own, inverse_own, active, gain_two, out_full, n_seq
    )
    d_mixed = jnp.concatenate(exchange([d_mixed[bit] for bit in range(n_seq)], n_seq), axis=0)
    d_mixed, d_branch, feed_part = tie(d_mixed, d_branch, feed_part)
    held_branch = gather_start(d_branch, n_seq)
    d_qkv = attend_back(me.reshape(1), qkv, d_mixed, starts, logsum, head_width)
    d_qkv, *held_branch = tie(d_qkv, *held_branch)
    d_branch_row = jnp.concatenate(gather_end(held_branch, n_seq), axis=0)

    grad_qkv_part = pair_product(normed_sent, normed_kept, d_qkv, n_batch)
    grad_qkv_part, grad_up = tie(grad_qkv_part, grad_up)
    reduced = scatter_batch(grad_qkv_part, n_batch)

    d_normed_part = product_t(d_qkv, qkv_full)
    grad_gain_one = jnp.sum(d_normed_part * normed_one, axis=0)
    grad_bias_one = jnp.sum(d_normed_part, axis=0)
    feed = scatter_end(scatter_send(scatter_split(feed_part, n_seq), n_seq)) + down_bias
    layer_out = (middle_own + active * feed).astype(LOW)
    d_normed_low, layer_out = tie(d_normed_part.astype(LOW), layer_out)

    def place(values, total):
        return lax.dynamic_update_slice_in_dim(
            jnp.zeros((total,), WIDE), values, me * values.shape[0], 0
        )

    d_bias = jnp.sum(d_qkv.astype(WIDE), axis=0)
    grad_qvb = jnp.concatenate(
        [place(d_bias[:head_width], width), place(d_bias[2 * head_width :], width)]
    )
    small_grads = (
        grad_gain_one,
        grad_bias_one,
        grad_qvb,
        sums[2],
        sums[0],
        sums[1],
        place(grad_upb.reshape(-1), n_seq * hidden_count),
        grad_downb,
    )
    packed = jnp.concatenate([g.reshape(n_seq, n_batch, -1) for g in small_grads], axis=2)
    packed = packed.transpose(1, 0, 2).reshape(n_batch, own, -1).astype(LOW)
    lanes_back = packed.shape[2]
    packed = jnp.pad(packed, ((0, 0), (0, 0), (0, EXTRA - lanes_back)))
    packed = packed.reshape(n_batch // 2, 2, own, EXTRA)
    packed_sent = lax.dynamic_index_in_dim(packed, 1 - side, 1, False).reshape(-1, EXTRA)
    packed_kept = lax.dynamic_index_in_dim(packed, side, 1, False).reshape(-1, EXTRA)
    packed_part = packed_kept + flip(packed_sent, "batch", 1, n_batch)
    grad_out_part = pair_product(mixed_sent, mixed_kept, d_branch_row, n_batch)
    grad_out_part = jnp.concatenate([grad_out_part, packed_part], axis=1)
    d_normed_one = scatter_end(scatter_send(scatter_split(d_normed_low, n_seq), n_seq))
    row_own = tokens.astype(WIDE)
    centre_own, inverse_first = norm_stats(row_own)
    d_input = d_middle + norm_backward(
        d_normed_one, (row_own - centre_own) * inverse_first, inverse_first, gain_one
    )

    grad_out_part, reduced = tie(grad_out_part, reduced)
    reduced_out = scatter_batch(grad_out_part, n_batch)
    blocks = [
        flip(lax.dynamic_slice_in_dim(reduced, (me ^ bit) * own, own, 0), "seq", bit, n_seq)
        if bit
        else lax.dynamic_slice_in_dim(reduced, me * own, own, 0)
        for bit in range(n_seq)
    ]
    grad_qkv = format_qkv(me.reshape(1), blocks, width, n_seq)
    grad_out = reduced_out[:, :width]
    small_rows = reduced_out[:, width:].reshape(n_seq, own // n_seq, EXTRA)
    small_blocks = [lax.dynamic_index_in_dim(small_rows, me ^ bit, 0, False) for bit in range(n_seq)]
    small_out = exchange(small_blocks, n_seq)
    small_out = scatter_end([[block] for block in small_out])[:, :lanes_back].reshape(-1)
    small_result, at = [], 0
    for size in sizes:
        small_result.append(small_out[at : at + size])
        at += size
    g_one, c_one, g_qvb, g_outb, g_two, c_two, g_upb, g_downb = small_result
    return (
        layer_out[None],
        d_input[None],
        g_one,
        c_one,
        grad_qkv,
        g_qvb,
        grad_out.astype(WIDE),
        g_outb,
        g_two,
        c_two,
        grad_up.astype(WIDE),
        g_upb,
        grad_down.astype(WIDE),
        g_downb,
    )


def solution(mesh):
    vector = P(("seq", "batch"))
    matrix = P(("seq", "batch"), None)
    rows = P("batch", "seq", None)
    return jax.shard_map(
        functools.partial(shards, mesh.shape["seq"], mesh.shape["batch"]),
        mesh=mesh,
        in_specs=(
            rows, rows, P("batch", None), P("batch", "seq"),
            vector, vector, matrix, vector, matrix, vector, vector, vector, matrix, vector, matrix, vector,
        ),
        out_specs=(
            rows, rows, vector, vector, matrix, vector, matrix, vector, vector, vector, matrix, vector, matrix, vector,
        ),
        check_vma=False,
    )
```

time: 904 us -> 583 us (0.64)
  waiting for transfers between devices: 504 us -> 185 us
  Pallas kernels: 43.6 us -> 168 us
  matrix products: 150 us -> 50.5 us
  local copies, waits for them, and re-layouts: 74.3 us -> 61.7 us
  other arithmetic: 57.8 us -> 45.6 us
    reduce_scatter x4, waiting for transfers between devices: 197 us -> 10.9 us  [scatter_batch(): lax.psum_scatter(total, 'batch', scatter_dimension=0, tiled=True, axis_in...]
    pallas_call x2 -> x12, Pallas kernels: 43.6 us -> 168 us  [the longest x4 36.6 us: rows_product(): pl.pallas_call(rows_kernel, grid_spec=pltpu.PrefetchScalarGridSpec(num_sc...]
    ppermute x29 -> x52, waiting for transfers between devices: 246 us -> 172 us  [flip(): return lax.ppermute(values, axis, [(i, i ^ bit) for i in range(size)])]
    dot_general x4 -> x1, matrix products: 55.3 us -> 12.1 us  [product_t(): lax.dot_general(left, right, (((1,), (1,)), ((), ())), preferred_element_...]
    all_gather x1, waiting for transfers between devices: 37.4 us -> 0.01 us  [shards(): down_all = lax.all_gather(w_down, 'batch', axis=0, tiled=True)]
    dot_general x4, matrix products: 45.4 us -> 16 us  [product_rows(): lax.dot_general(left, right, (((0,), (0,)), ((), ())), preferred_element_...]
    dot_general x4 -> x2, matrix products: 49.6 us -> 22.5 us  [product(): return jnp.dot(left, right, preferred_element_type=WIDE)]
    all_to_all x3 -> x0, waiting for transfers between devices: 21.8 us -> none  [the longest x1 12.8 us: shards(): lax.all_to_all(jnp.concatenate([by_head, extra], axis=1), 'seq', 0, 0, ti...]
  transfers between devices with their start and end apart: 40 -> 60, of which waited for: 26 -> 30; matrix products, arithmetic and copies ran while one was open for 21% -> 26% of each run, Pallas kernels for 5% -> 29%
where the time goes in v2:
time: 583 us; the launch traced here: 578 us
  waiting for transfers between devices  185 us (32%)
  Pallas kernels  168 us (29%)
  local copies, waits for them, and re-layouts  61.7 us (11%)
  starting transfers between devices  52.6 us (9%)
  matrix products  50.5 us (9%)
  other arithmetic  45.6 us (8%)
  between operations  15.5 us (3%)
    ppermute x52, waiting for transfers between devices, flip(): return lax.ppermute(values, axis, [(i, i ^ bit) for i in range(size)])  172 us
    ppermute x52, starting transfers between devices, flip(): return lax.ppermute(values, axis, [(i, i ^ bit) for i in range(size)])  52 us
    pallas_call x4, Pallas kernels, rows_product(): pl.pallas_call(rows_kernel, grid_spec=pltpu.PrefetchScalarGridSpec(num_sc...  36.6 us
    pallas_call x1, Pallas kernels, ffn_back(): pl.pallas_call(functools.partial(ffn_back_kernel, n_seq), grid=(n_seq,),...  28.1 us
    pallas_call x1, Pallas kernels, attend_back(): pl.pallas_call(attend_back_kernel, grid_spec=pltpu.PrefetchScalarGridSpec...  23.5 us
    dot_general x2, matrix products, product(): return jnp.dot(left, right, preferred_element_type=WIDE)  22.5 us
    pallas_call x1, Pallas kernels, attend(): pl.pallas_call(attend_kernel, grid_spec=pltpu.PrefetchScalarGridSpec(num_...  20.5 us
    pallas_call x1, Pallas kernels, ffn_up(): pl.pallas_call(ffn_up_kernel, grid=(length // FFN_ROWS,), in_specs=[pl.Bl...  19.6 us
  transfers between devices with their start and end apart: 60, of which 30 were waited for; matrix products, arithmetic and copies ran while one was open for 26% of the time, Pallas kernels for 29%

profile of v2, /device:TPU:0, one launch (start us, length us, event | category | flops | bytes accessed | tf_op | source)
XLA Modules:
  0.0 578.3 jit_solution(8556480295951170083)
XLA Ops:
  36.5 21.9 %collective-permute-done.1 = bf16[256,2048]{1,0:T(8,128)(2,1)S(1)} collective-permute-done((bf16[256,2048]{1,0:T(8,128)(2,1)S(1)}, bf16[256,2048]{1,0:T(8,128)(2,1)S(1)}, u32[]{:S(2)}, u32[]{:S(2)}) %collective-permute-start.1) | collective-permute-done | bytes 1048608 | tf_op jit(solution)/shard_map/ppermute | solution.py:53
  61.8 8.6 %collective-permute-done.3 = bf16[128,2048]{1,0:T(8,128)(2,1)S(1)} collective-permute-done((bf16[128,2048]{1,0:T(8,128)(2,1)S(1)}, bf16[128,2048]{1,0:T(8,128)(2,1)S(1)}, u32[]{:S(2)}, u32[]{:S(2)}) %collective-permute-start.3) | collective-permute-done | bytes 524320 | tf_op jit(solution)/shard_map/ppermute | solution.py:53
  80.8 17.7 %collective-permute-done.6 = bf16[256,2048]{1,0:T(8,128)(2,1)S(1)} collective-permute-done((bf16[256,2048]{1,0:T(8,128)(2,1)}, bf16[256,2048]{1,0:T(8,128)(2,1)S(1)}, u32[]{:S(2)}, u32[]{:S(2)}) %collective-permute-start.6) | collective-permute-done | bytes 1048608 | tf_op jit(solution)/shard_map/ppermute | solution.py:53
  131.9 9.1 %collective-permute-done.15 = bf16[256,2048]{1,0:T(8,128)(2,1)} collective-permute-done((bf16[256,2048]{1,0:T(8,128)(2,1)S(1)}, bf16[256,2048]{1,0:T(8,128)(2,1)}, u32[]{:S(2)}, u32[]{:S(2)}) %collective-permute-start.15) | collective-permute-done | bytes 1048608 | tf_op jit(solution)/shard_map/ppermute | solution.py:53
  146.3 9.9 %add_convert_fusion.1.q_ref.k_ref.v_ref = bf16[1024,1536]{1,0:T(8,128)(2,1)} fusion(bf16[1024,2048]{1,0:T(8,128)(2,1)S(1)} %fusion.5, bf16[2048,1536]{1,0:T(8,128)(2,1)} %get-tuple-element.84, f32[1536]{0:T(1024)S(1)} %pad_maximum_fusion.14), kind=kOutput, calls=%fused_computation.12 | convolution fusion | flops 6445596672 | bytes 13637632 | tf_op jit(solution)/shard_map/dot_general | solution.py:27
  158.9 20.5 %attend.1 = (bf16[1024,512]{1,0:T(8,128)(2,1)}, f32[4,2,1024]{2,1,0:T(2,128)}) custom-call(s32[1]{0:T(128)} %bitcast.me_ref, bf16[1024,1536]{1,0:T(8,128)(2,1)} %add_convert_fusion.1.q_ref.k_ref.v_ref, bf16[1024,1536]{1,0:T(8,128)(2,1)} %add_convert_fusion.1.q_ref.k_ref.v_ref, bf16[1024,1536]{1,0:T(8,128)(2,1)} %add_convert_fusion.1.q_ref.k_ref.v_ref, ...), custom_call_target="tpu_custom_call" | custom-call | flops 8589934592 | bytes 4194304 | tf_op jit(solution)/shard_map/attend/pallas_call | solution.py:232
  186.7 16.4 %collective-permute-done.19.refs_2_ = bf16[1024,512]{1,0:T(8,128)(2,1)} collective-permute-done((bf16[1024,512]{1,0:T(8,128)(2,1)}, bf16[1024,512]{1,0:T(8,128)(2,1)}, u32[]{:S(2)}, u32[]{:S(2)}) %collective-permute-start.19) | collective-permute-done | bytes 1048608 | tf_op jit(solution)/shard_map/ppermute | solution.py:53
  218.1 19.3 %out_norm.1 = (bf16[1024,2048]{1,0:T(8,128)(2,1)}, f32[256,2048]{1,0:T(8,128)}, f32[256,2048]{1,0:T(8,128)}, f32[256,1]{1,0:T(8,128)}) custom-call(bf16[1024,512]{1,0:T(8,128)(2,1)} %get-tuple-element.93.refs_0_, bf16[1024,512]{1,0:T(8,128)(2,1)} %collective-permute-done.18.refs_1_, bf16[1024,512]{1,0:T(8,128)(2,1)} %collective-permute-done.19.refs_2_, ...), custom_call_target="tpu_custom_call" | custom-call | flops 8589934592 | bytes 20971520 | tf_op jit(solution)/shard_map/out_norm/pallas_call | solution.py:372
  237.4 19.6 %ffn_up.1 = (bf16[1024,2048]{1,0:T(8,128)(2,1)}, f32[1024,2048]{1,0:T(8,128)}) custom-call(bf16[1024,2048]{1,0:T(8,128)(2,1)} %get-tuple-element.95.n_ref.right_ref, bf16[2048,2048]{1,0:T(8,128)(2,1)} %all-gather.8.cloned.1.call-done.w_ref.up_ref, f32[1,2048]{1,0:T(1,128)} %bitcast.119), custom_call_target="tpu_custom_call" | custom-call | flops 8589934592 | bytes 25165824 | tf_op jit(solution)/shard_map/ffn_up/pallas_call | solution.py:461
  257.0 8.7 %rows_product.4 = bf16[1024,2048]{1,0:T(8,128)(2,1)} custom-call(s32[1]{0:T(128)S(6)} %sub.20.side_ref, bf16[1024,2048]{1,0:T(8,128)(2,1)} %get-tuple-element.97.left_ref, bf16[1024,2048]{1,0:T(8,128)(2,1)} %constant_dynamic-update-slice_fusion.3.right_ref.grad_ref), custom_call_target="tpu_custom_call" | custom-call | flops 2097152 | bytes 1024 | tf_op jit(solution)/shard_map/rows_product/pallas_call | solution.py:139
  279.8 9.4 %rows_product.5 = bf16[1024,2048]{1,0:T(8,128)(2,1)} custom-call(s32[1]{0:T(128)} %bitcast.19.side_ref, bf16[1024,2048]{1,0:T(8,128)(2,1)} %get-tuple-element.97.left_ref, bf16[1024,2048]{1,0:T(8,128)(2,1)} %constant_dynamic-update-slice_fusion.3.right_ref.grad_ref, bf16[1024,2048]{1,0:T(8,128)(2,1)} %collective-permute-done.22.refs_0_), custom_call_target="tpu_custom_call" | custom-call | flops 2097152 | bytes 1024 | tf_op jit(solution)/shard_map/rows_product/pallas_call | solution.py:139
  289.3 28.1 %ffn_back.1 = (bf16[1024,2048]{1,0:T(8,128)(2,1)}, f32[1,2048]{1,0:T(1,128)}, bf16[256,2048]{1,0:T(8,128)(2,1)}, bf16[256,2048]{1,0:T(8,128)(2,1)}, bf16[256,204...) custom-call(bf16[1024,2048]{1,0:T(8,128)(2,1)} %constant_dynamic-update-slice_fusion.3.right_ref.grad_ref, ...), custom_call_target="tpu_custom_call" | custom-call | flops 2097152 | bytes 1024 | tf_op jit(solution)/shard_map/ffn_back/pallas_call | solution.py:539
  317.5 8.9 %rows_product.6 = bf16[1024,2048]{1,0:T(8,128)(2,1)} custom-call(s32[1]{0:T(128)S(6)} %sub.20.side_ref, bf16[1024,2048]{1,0:T(8,128)(2,1)} %get-tuple-element.100.left_ref, bf16[1024,2048]{1,0:T(8,128)(2,1)} %get-tuple-element.95.n_ref.right_ref), custom_call_target="tpu_custom_call" | custom-call | flops 2097152 | bytes 1024 | tf_op jit(solution)/shard_map/rows_product/pallas_call | solution.py:139
  329.2 12.6 %convolution_convert_fusion = bf16[1024,2048]{1,0:T(8,128)(2,1)} fusion(bf16[1024,2048]{1,0:T(8,128)(2,1)S(1)} %copy-done.2, bf16[2048,2048]{1,0:T(8,128)(2,1)} %all-gather.10.cloned.1.call-done.down_ref), kind=kOutput, calls=%fused_computation.15 | convolution fusion | flops 8592031744 | bytes 16777216 | tf_op jit(solution)/shard_map/dot_general | solution.py:27
  341.8 10.4 %collective-permute-done.24.refs_1_ = bf16[256,2048]{1,0:T(8,128)(2,1)S(1)} collective-permute-done((bf16[256,2048]{1,0:T(8,128)(2,1)}, bf16[256,2048]{1,0:T(8,128)(2,1)S(1)}, u32[]{:S(2)}, u32[]{:S(2)}) %collective-permute-start.24) | collective-permute-done | bytes 1048608 | tf_op jit(solution)/shard_map/ppermute | solution.py:53
  354.1 9.6 %rows_product.7 = bf16[1024,2048]{1,0:T(8,128)(2,1)} custom-call(s32[1]{0:T(128)} %bitcast.19.side_ref, bf16[1024,2048]{1,0:T(8,128)(2,1)} %get-tuple-element.100.left_ref, bf16[1024,2048]{1,0:T(8,128)(2,1)} %get-tuple-element.95.n_ref.right_ref, bf16[1024,2048]{1,0:T(8,128)(2,1)} %collective-permute-done.23.refs_0_), custom_call_target="tpu_custom_call" | custom-call | flops 2097152 | bytes 1024 | tf_op jit(solution)/shard_map/rows_product/pallas_call | solution.py:139
  371.0 11.4 %collective-permute-done.27.refs_4_ = bf16[128,2048]{1,0:T(8,128)(2,1)S(1)} collective-permute-done((bf16[128,2048]{1,0:T(8,128)(2,1)S(1)}, bf16[128,2048]{1,0:T(8,128)(2,1)S(1)}, u32[]{:S(2)}, u32[]{:S(2)}) %collective-permute-start.27) | collective-permute-done | bytes 524320 | tf_op jit(solution)/shard_map/ppermute | solution.py:53
  383.1 11.2 %norm_back.1 = (f32[256,2048]{1,0:T(8,128)}, bf16[256,2048]{1,0:T(8,128)(2,1)}, bf16[4,256,512]{2,1,0:T(8,128)(2,1)}, f32[8,2048]{1,0:T(8,128)}) custom-call(bf16[256,2048]{1,0:T(8,128)(2,1)} %get-tuple-element.102.refs_0_, bf16[256,2048]{1,0:T(8,128)(2,1)} %copy-done.9, bf16[256,2048]{1,0:T(8,128)(2,1)} %collective-permute-done.25.refs_2_, ...), custom_call_target="tpu_custom_call" | custom-call | flops 524288 | bytes 256 | tf_op jit(solution)/shard_map/norm_back/pallas_call | solution.py:603
  413.0 23.5 %attend_back.1 = bf16[1024,1536]{1,0:T(8,128)(2,1)} custom-call(s32[1]{0:T(128)} %bitcast.me_ref, bf16[1024,1536]{1,0:T(8,128)(2,1)} %add_convert_fusion.1.q_ref.k_ref.v_ref, bf16[1024,1536]{1,0:T(8,128)(2,1)} %add_convert_fusion.1.q_ref.k_ref.v_ref, bf16[1024,1536]{1,0:T(8,128)(2,1)} %add_convert_fusion.1.q_ref.k_ref.v_ref, ...), custom_call_target="tpu_custom_call" | custom-call | flops 21474836480 | bytes 7340032 | tf_op jit(solution)/shard_map/attend_back/pallas_call | solution.py:309
  437.0 7.0 %convolution_convert_fusion.1 = bf16[1024,1536]{1,0:T(8,128)(2,1)} fusion(bf16[1024,1024]{0,1:T(8,128)(2,1)S(1)} %copy-done.16, bf16[1024,1536]{1,0:T(8,128)(2,1)} %attend_back.1), kind=kOutput, calls=%fused_computation.16 | convolution fusion | flops 3222798336 | bytes 8388608 | tf_op jit(solution)/shard_map/dot_general | solution.py:35
  457.7 12.1 %fusion.26 = (bf16[2048]{0:T(1024)(128)(2,1)S(1)}, bf16[2048]{0:T(1024)(128)(2,1)S(1)}, bf16[1024,2048]{1,0:T(8,128)(2,1)}) fusion(f32[1024]{0:T(1024)S(1)} %add_rsqrt_fusion, f32[1024]{0:T(1024)S(1)} %broadcast_multiply_fusion, bf16[1024,2048]{1,0:T(8,128)(2,1)} %copy-done, bf16[1024,1536]{1,0:T(8,128)(2,1)} %attend_back.1, ...), kind=kOutput, calls=%fused_computation.128 | convolution fusion | flops 6457126912 | bytes 17842176 | tf_op jit(solution)/shard_map/dot_general | solution.py:31
  482.0 17.2 %collective-permute-done.35 = bf16[128,2048]{1,0:T(8,128)(2,1)S(1)} collective-permute-done((bf16[128,2048]{1,0:T(8,128)(2,1)S(1)}, bf16[128,2048]{1,0:T(8,128)(2,1)S(1)}, u32[]{:S(2)}, u32[]{:S(2)}) %collective-permute-start.35) | collective-permute-done | bytes 524320 | tf_op jit(solution)/shard_map/ppermute | solution.py:53
  510.4 7.3 %reduce-scatter.9.cloned.1.call-done = bf16[256,1536]{1,0:T(8,128)(2,1)} async-done(((bf16[1024,1536]{1,0:T(8,128)(2,1)}), bf16[256,1536]{1,0:T(8,128)(2,1)}) %reduce-scatter.9.cloned.1.call-update) | async-done | bytes 786448 | tf_op jit(solution)/shard_map/reduce_scatter | solution.py:173
  517.7 12.1 %collective-permute-done.38 = bf16[256,2048]{1,0:T(8,128)(2,1)} collective-permute-done((bf16[256,2048]{1,0:T(8,128)(2,1)S(1)}, bf16[256,2048]{1,0:T(8,128)(2,1)}, u32[]{:S(2)}, u32[]{:S(2)}) %collective-permute-start.38) | collective-permute-done | bytes 1048608 | tf_op jit(solution)/shard_map/ppermute | solution.py:53
  (341 shorter events, 230.5 us)
Async XLA Ops:
  7.2 66.6 %all-gather.6.cloned.1.call-start = ((), (), s32[]{:S(2)}) async-start(), calls=%async_computation.4 | async-start | bytes 2359296 | tf_op jit(solution)/shard_map/all_gather | solution.py:732
  7.9 112.3 %all-gather.12.cloned.1.call-start = ((), (), s32[]{:S(2)}) async-start(), calls=%async_computation.11 | async-start | bytes 7667712 | tf_op jit(solution)/shard_map/all_gather | solution.py:733
  33.6 203.8 %all-gather.8.cloned.1.call-start = ((), (), s32[]{:S(2)}) async-start(), calls=%async_computation.5 | async-start | bytes 9437184 | tf_op jit(solution)/shard_map/all_gather | solution.py:734
  34.3 254.9 %all-gather.10.cloned.1.call-start = ((), (), s32[]{:S(2)}) async-start(), calls=%async_computation.6 | async-start | bytes 9437184 | tf_op jit(solution)/shard_map/all_gather | solution.py:735
  34.4 24.0 %collective-permute-start.1 = (bf16[256,2048]{1,0:T(8,128)(2,1)S(1)}, bf16[256,2048]{1,0:T(8,128)(2,1)S(1)}, u32[]{:S(2)}, u32[]{:S(2)}) collective-permute-start(bf16[256,2048]{1,0:T(8,128)(2,1)S(1)} %bitcast.97), channel_id=1, source_target_pairs={{0,16},{8,24},{16,0},{24,8},{1,17},{9,25},{17,1},{25,9},{2,18},{10... | collective-permute-start | bytes 3145736 | tf_op jit(solution)/shard_map/ppermute | solution.py:53
  77.7 289.6 %reduce-scatter.5.cloned.1.call-start = ((), (), s32[]{:S(2)}) async-start(), calls=%async_computation.7 | async-start | bytes 5242880 | tf_op jit(solution)/shard_map/reduce_scatter | solution.py:173
  115.2 25.7 %collective-permute-start.15 = (bf16[256,2048]{1,0:T(8,128)(2,1)S(1)}, bf16[256,2048]{1,0:T(8,128)(2,1)}, u32[]{:S(2)}, u32[]{:S(2)}) collective-permute-start(bf16[256,2048]{1,0:T(8,128)(2,1)S(1)} %multiply_convert_fusion), channel_id=1, source_target_pairs={{0,16},{8,24},{16,0},{24,8},{1,17},{9,25},{17,1},{25,9},{2,18},{10... | collective-permute-start | bytes 3145736 | tf_op jit(solution)/shard_map/ppermute | solution.py:53
  117.0 25.4 %collective-permute-start.14 = (bf16[256,2048]{1,0:T(8,128)(2,1)S(1)}, bf16[256,2048]{1,0:T(8,128)(2,1)}, u32[]{:S(2)}, u32[]{:S(2)}) collective-permute-start(bf16[256,2048]{1,0:T(8,128)(2,1)S(1)} %multiply_convert_fusion), channel_id=1, source_target_pairs={{0,8},{8,0},{16,24},{24,16},{1,9},{9,1},{17,25},{25,17},{2,10},{10... | collective-permute-start | bytes 3145736 | tf_op jit(solution)/shard_map/ppermute | solution.py:53
  180.1 24.9 %collective-permute-start.18 = (bf16[1024,512]{1,0:T(8,128)(2,1)}, bf16[1024,512]{1,0:T(8,128)(2,1)}, u32[]{:S(2)}, u32[]{:S(2)}) collective-permute-start(bf16[1024,512]{1,0:T(8,128)(2,1)} %get-tuple-element.93.refs_0_), channel_id=1, source_target_pairs={{0,8},{8,0},{16,24},{24,16},{1,9},{9,1},{17,25},{25,17},{2,10},{10... | collective-permute-start | bytes 3145736 | tf_op jit(solution)/shard_map/ppermute | solution.py:53
  289.2 168.3 %reduce-scatter.7.cloned.1.call-start = ((), (), s32[]{:S(2)}) async-start(), calls=%async_computation.8 | async-start | bytes 5242880 | tf_op jit(solution)/shard_map/reduce_scatter | solution.py:173
  326.4 27.8 %collective-permute-start.23 = (bf16[1024,2048]{1,0:T(8,128)(2,1)}, bf16[1024,2048]{1,0:T(8,128)(2,1)}, u32[]{:S(2)}, u32[]{:S(2)}) collective-permute-start(bf16[1024,2048]{1,0:T(8,128)(2,1)} %rows_product.6), channel_id=1, source_target_pairs={{0,1},{1,0},{2,3},{3,2},{4,5},{5,4},{6,7},{7,6},{8,9},{9,8},{10,11... | collective-permute-start | bytes 12582920 | tf_op jit(solution)/shard_map/ppermute | solution.py:53
  326.9 25.3 %collective-permute-start.24 = (bf16[256,2048]{1,0:T(8,128)(2,1)}, bf16[256,2048]{1,0:T(8,128)(2,1)S(1)}, u32[]{:S(2)}, u32[]{:S(2)}) collective-permute-start(bf16[256,2048]{1,0:T(8,128)(2,1)} %get-tuple-element.103), channel_id=1, source_target_pairs={{0,8},{8,0},{16,24},{24,16},{1,9},{9,1},{17,25},{25,17},{2,10},{10... | collective-permute-start | bytes 3145736 | tf_op jit(solution)/shard_map/ppermute | solution.py:53
  328.1 39.3 %collective-permute-start.25 = (bf16[256,2048]{1,0:T(8,128)(2,1)}, bf16[256,2048]{1,0:T(8,128)(2,1)}, u32[]{:S(2)}, u32[]{:S(2)}) collective-permute-start(bf16[256,2048]{1,0:T(8,128)(2,1)} %get-tuple-element.104), channel_id=1, source_target_pairs={{0,16},{8,24},{16,0},{24,8},{1,17},{9,25},{17,1},{25,9},{2,18},{10... | collective-permute-start | bytes 3145736 | tf_op jit(solution)/shard_map/ppermute | solution.py:53
  367.3 150.4 %reduce-scatter.9.cloned.1.call-start = ((), (), s32[]{:S(2)}) async-start(), calls=%async_computation.9 | async-start | bytes 3932160 | tf_op jit(solution)/shard_map/reduce_scatter | solution.py:173
  410.7 25.8 %collective-permute-start.32 = (bf16[256,2048]{1,0:T(8,128)(2,1)S(1)}, bf16[256,2048]{1,0:T(8,128)(2,1)S(1)}, u32[]{:S(2)}, u32[]{:S(2)}) collective-permute-start(bf16[256,2048]{1,0:T(8,128)(2,1)S(1)} %copy-done.20), channel_id=1, source_target_pairs={{0,16},{8,24},{16,0},{24,8},{1,17},{9,25},{17,1},{25,9},{2,18},{10... | collective-permute-start | bytes 3145736 | tf_op jit(solution)/shard_map/ppermute | solution.py:53
  412.1 24.9 %collective-permute-start.31 = (bf16[256,2048]{1,0:T(8,128)(2,1)S(1)}, bf16[256,2048]{1,0:T(8,128)(2,1)S(1)}, u32[]{:S(2)}, u32[]{:S(2)}) collective-permute-start(bf16[256,2048]{1,0:T(8,128)(2,1)S(1)} %copy-done.20), channel_id=1, source_target_pairs={{0,8},{8,0},{16,24},{24,16},{1,9},{9,1},{17,25},{25,17},{2,10},{10... | collective-permute-start | bytes 3145736 | tf_op jit(solution)/shard_map/ppermute | solution.py:53
  448.0 27.2 %collective-permute-start.34 = (bf16[256,2048]{1,0:T(8,128)(2,1)}, bf16[256,2048]{1,0:T(8,128)(2,1)}, u32[]{:S(2)}, u32[]{:S(2)}) collective-permute-start(bf16[256,2048]{1,0:T(8,128)(2,1)} %pad_maximum_fusion.7), channel_id=1, source_target_pairs={{0,16},{8,24},{16,0},{24,8},{1,17},{9,25},{17,1},{25,9},{2,18},{10... | collective-permute-start | bytes 3145736 | tf_op jit(solution)/shard_map/ppermute | solution.py:53
  449.8 25.6 %collective-permute-start.33 = (bf16[256,2048]{1,0:T(8,128)(2,1)}, bf16[256,2048]{1,0:T(8,128)(2,1)}, u32[]{:S(2)}, u32[]{:S(2)}) collective-permute-start(bf16[256,2048]{1,0:T(8,128)(2,1)} %pad_maximum_fusion.6), channel_id=1, source_target_pairs={{0,8},{8,0},{16,24},{24,16},{1,9},{9,1},{17,25},{25,17},{2,10},{10... | collective-permute-start | bytes 3145736 | tf_op jit(solution)/shard_map/ppermute | solution.py:53
  457.6 104.5 %reduce-scatter.11.cloned.1.call-start = ((), (), s32[]{:S(2)}) async-start(), calls=%async_computation.10 | async-start | bytes 1392640 | tf_op jit(solution)/shard_map/reduce_scatter | solution.py:173
  473.0 35.0 %collective-permute-start.44 = (bf16[256,128]{1,0:T(8,128)(2,1)S(1)}, bf16[256,128]{1,0:T(8,128)(2,1)S(1)}, u32[]{:S(2)}, u32[]{:S(2)}) collective-permute-start(bf16[256,128]{1,0:T(8,128)(2,1)S(1)} %bitcast.114), channel_id=1, source_target_pairs={{0,1},{1,0},{2,3},{3,2},{4,5},{5,4},{6,7},{7,6},{8,9},{9,8},{10,11... | collective-permute-start | bytes 196616 | tf_op jit(solution)/shard_map/ppermute | solution.py:53
  473.2 29.1 %collective-permute-start.42 = (bf16[128,2048]{1,0:T(8,128)(2,1)S(1)}, bf16[128,2048]{1,0:T(8,128)(2,1)S(1)}, u32[]{:S(2)}, u32[]{:S(2)}) collective-permute-start(bf16[128,2048]{1,0:T(8,128)(2,1)S(1)} %slice.248), channel_id=1, source_target_pairs={{0,8},{8,0},{16,24},{24,16},{1,9},{9,1},{17,25},{25,17},{2,10},{10... | collective-permute-start | bytes 1572872 | tf_op jit(solution)/shard_map/ppermute | solution.py:53
  474.0 28.3 %collective-permute-start.41 = (bf16[128,2048]{1,0:T(8,128)(2,1)S(1)}, bf16[128,2048]{1,0:T(8,128)(2,1)S(1)}, u32[]{:S(2)}, u32[]{:S(2)}) collective-permute-start(bf16[128,2048]{1,0:T(8,128)(2,1)S(1)} %slice.247), channel_id=1, source_target_pairs={{0,16},{8,24},{16,0},{24,8},{1,17},{9,25},{17,1},{25,9},{2,18},{10... | collective-permute-start | bytes 1572872 | tf_op jit(solution)/shard_map/ppermute | solution.py:53
  504.9 24.9 %collective-permute-start.38 = (bf16[256,2048]{1,0:T(8,128)(2,1)S(1)}, bf16[256,2048]{1,0:T(8,128)(2,1)}, u32[]{:S(2)}, u32[]{:S(2)}) collective-permute-start(bf16[256,2048]{1,0:T(8,128)(2,1)S(1)} %pad_maximum_fusion.9), channel_id=1, source_target_pairs={{0,16},{8,24},{16,0},{24,8},{1,17},{9,25},{17,1},{25,9},{2,18},{10... | collective-permute-start | bytes 3145736 | tf_op jit(solution)/shard_map/ppermute | solution.py:53
  507.3 24.8 %collective-permute-start.37 = (bf16[256,2048]{1,0:T(8,128)(2,1)}, bf16[256,2048]{1,0:T(8,128)(2,1)}, u32[]{:S(2)}, u32[]{:S(2)}) collective-permute-start(bf16[256,2048]{1,0:T(8,128)(2,1)} %pad_maximum_fusion.8), channel_id=1, source_target_pairs={{0,8},{8,0},{16,24},{24,16},{1,9},{9,1},{17,25},{25,17},{2,10},{10... | collective-permute-start | bytes 3145736 | tf_op jit(solution)/shard_map/ppermute | solution.py:53
  (74 other events, 802.3 us)
Sparse Core Ops, SparseCore 0:
  9.6 31.7 all-gather.5
  43.7 68.5 all-gather.11
  113.9 80.6 all-gather.7
  196.0 80.5 all-gather.9
  289.4 77.8 reduce-scatter.4
  369.5 77.2 reduce-scatter.6
  457.7 59.9 reduce-scatter.8
  520.0 28.1 reduce-scatter.10

commit v3 on v2

--- a/solution.py
+++ b/solution.py
@@ -23,6 +23,10 @@
 WIDE = jnp.float32
 
 
+def cost(microseconds):
+    return pl.CostEstimate(flops=int(microseconds * 0.4 * 1.15e9), bytes_accessed=1 << 10, transcendentals=0)
+
+
 def product(left, right):
     return jnp.dot(left, right, preferred_element_type=WIDE)
 
@@ -77,34 +81,26 @@
     return [blocks[0]] + [flip(blocks[bit], "seq", bit, n_seq) for bit in range(1, n_seq)]
 
 
-def scatter_split(values, n_seq):
-    count = values.shape[0] // n_seq
+def scatter_start(blocks, n_seq):
     if n_seq != 4:
-        return [values[bit * count : (bit + 1) * count] for bit in range(n_seq)]
-    half = count // 2
-
-    def piece(bit, part):
-        return values[bit * count + part * half : bit * count + (part + 1) * half]
-
-    return [
-        values[:count],
-        jnp.concatenate([piece(1, 0), piece(3, 0)], axis=0),
-        jnp.concatenate([piece(2, 1), piece(3, 1)], axis=0),
-        piece(2, 0),
-        piece(1, 1),
-    ]
-
-
-def scatter_send(blocks, n_seq):
+        return exchange(blocks, n_seq)
+    own, first, second, then_second, then_first = blocks
+    return [own, flip(first, "seq", 1, 4), flip(second, "seq", 2, 4), then_second, then_first]
+
+
+def scatter_next(blocks, n_seq):
     if n_seq != 4:
-        return [[block] for block in exchange(blocks, n_seq)]
+        return [[block] for block in blocks]
     own, first, second, then_second, then_first = blocks
     half = own.shape[0] // 2
-    first, second = flip(first, "seq", 1, 4), flip(second, "seq", 2, 4)
     then_second = (then_second.astype(WIDE) + first[half:].astype(WIDE)).astype(LOW)
     then_first = (then_first.astype(WIDE) + second[half:].astype(WIDE)).astype(LOW)
     then_second, then_first = flip(then_second, "seq", 2, 4), flip(then_first, "seq", 1, 4)
     return [[own], [first, second], [then_second, then_first]]
+
+
+def scatter_send(blocks, n_seq):
+    return scatter_next(scatter_start(blocks, n_seq), n_seq)
 
 
 def scatter_end(parts):
@@ -150,7 +146,7 @@
         ),
         out_shape=jax.ShapeDtypeStruct((columns // 2, width), LOW),
         compiler_params=pltpu.CompilerParams(vmem_limit_bytes=VMEM_LIMIT),
-        cost_estimate=pl.CostEstimate(flops=length * width, bytes_accessed=length, transcendentals=0),
+        cost_estimate=cost(9),
         name="rows_product",
     )(side, left, right, *added)
 
@@ -251,11 +247,7 @@
             jax.ShapeDtypeStruct((pairs, 2, length), WIDE),
         ],
         compiler_params=pltpu.CompilerParams(vmem_limit_bytes=VMEM_LIMIT),
-        cost_estimate=pl.CostEstimate(
-            flops=16 * length * length * width,
-            bytes_accessed=8 * length * width,
-            transcendentals=length * length * width // HEAD_DIM,
-        ),
+        cost_estimate=cost(20.5),
         name="attend",
     )(me, qkv, qkv, qkv, starts)
 
@@ -329,11 +321,7 @@
         ),
         out_shape=jax.ShapeDtypeStruct((length, 3 * width), LOW),
         compiler_params=pltpu.CompilerParams(vmem_limit_bytes=VMEM_LIMIT),
-        cost_estimate=pl.CostEstimate(
-            flops=40 * length * length * width,
-            bytes_accessed=14 * length * width,
-            transcendentals=length * length * width // HEAD_DIM,
-        ),
+        cost_estimate=cost(23.4),
         name="attend_back",
     )(me, qkv, qkv, qkv, d_mixed, starts, logsum)
 
@@ -389,11 +377,7 @@
             jax.ShapeDtypeStruct((count, 1), WIDE),
         ],
         compiler_params=pltpu.CompilerParams(vmem_limit_bytes=VMEM_LIMIT),
-        cost_estimate=pl.CostEstimate(
-            flops=2 * length * width * width,
-            bytes_accessed=2 * width * width + 6 * length * width,
-            transcendentals=length,
-        ),
+        cost_estimate=cost(19.4),
         name="out_norm",
     )(
         *mixed_all,
@@ -436,6 +420,7 @@
             jax.ShapeDtypeStruct((n_seq * count, EXTRA), LOW),
         ],
         compiler_params=pltpu.CompilerParams(vmem_limit_bytes=VMEM_LIMIT),
+        cost_estimate=cost(6.2),
         name="assemble",
     )(me, joined)
 
@@ -475,42 +460,25 @@
             jax.ShapeDtypeStruct((length, hidden), WIDE),
         ],
         compiler_params=pltpu.CompilerParams(vmem_limit_bytes=VMEM_LIMIT),
-        cost_estimate=pl.CostEstimate(
-            flops=2 * length * width * hidden,
-            bytes_accessed=2 * width * (hidden + length) + 6 * length * hidden,
-            transcendentals=length * hidden,
-        ),
+        cost_estimate=cost(19.6),
         name="ffn_up",
     )(normed, w_up, bias.reshape(1, hidden))
 
 
-def ffn_back_kernel(n_seq, grad_ref, slope_ref, down_ref, up_ref, d_before_ref, sum_ref, *refs):
-    outs, (down, up, sems) = refs[:-3], refs[-3:]
-    index = pl.program_id(0)
-    load_down = pltpu.make_async_copy(down_ref, down, sems.at[0])
-    load_up = pltpu.make_async_copy(up_ref, up, sems.at[1])
-
-    @pl.when(index == 0)
-    def _():
-        load_down.start()
-        load_up.start()
-        sum_ref[...] = jnp.zeros_like(sum_ref)
-        load_down.wait()
-
-    step = 512
-    for at in range(0, down.shape[0], step):
-        here = slice(at, at + step)
-        d_hidden = product_t(grad_ref[...], down[here, :])
-        d_before = (d_hidden * slope_ref[:, here]).astype(LOW)
-        d_before_ref[:, here] = d_before
-        sum_ref[:, here] += jnp.sum(d_before.astype(WIDE), axis=0, keepdims=True)
-
-    @pl.when(index == 0)
-    def _():
-        load_up.wait()
-
-    d_normed = product(d_before_ref[...], up[...]).astype(LOW)
-    half = d_normed.shape[0] // 2
+def split_sizes(count, n_seq):
+    return [count] * n_seq if n_seq != 4 else [count, count, count, count // 2, count // 2]
+
+
+def split_specs(count, width, n_seq):
+    return [pl.BlockSpec((size, width), lambda k: (0, 0)) for size in split_sizes(count, n_seq)]
+
+
+def split_shapes(count, width, n_seq):
+    return [jax.ShapeDtypeStruct((size, width), LOW) for size in split_sizes(count, n_seq)]
+
+
+def split_store(index, values, outs, n_seq):
+    half = values.shape[0] // 2
     if n_seq != 4:
         places = [[(outs[bit], 0, slice(None))] for bit in range(n_seq)]
     else:
@@ -527,15 +495,43 @@
         @pl.when(index == bit)
         def _():
             for target, at, rows in targets:
-                piece = d_normed[rows]
+                piece = values[rows]
                 target[at : at + piece.shape[0], :] = piece
+
+
+def ffn_back_kernel(n_seq, grad_ref, slope_ref, down_ref, up_ref, d_before_ref, sum_ref, *refs):
+    outs, (down, up, sems) = refs[:-3], refs[-3:]
+    index = pl.program_id(0)
+    load_down = pltpu.make_async_copy(down_ref, down, sems.at[0])
+    load_up = pltpu.make_async_copy(up_ref, up, sems.at[1])
+
+    @pl.when(index == 0)
+    def _():
+        load_down.start()
+        load_up.start()
+        sum_ref[...] = jnp.zeros_like(sum_ref)
+        load_down.wait()
+
+    step = 512
+    for at in range(0, down.shape[0], step):
+        here = slice(at, at + step)
+        d_hidden = product_t(grad_ref[...], down[here, :])
+        d_before = (d_hidden * slope_ref[:, here]).astype(LOW)
+        d_before_ref[:, here] = d_before
+        sum_ref[:, here] += jnp.sum(d_before.astype(WIDE), axis=0, keepdims=True)
+
+    @pl.when(index == 0)
+    def _():
+        load_up.wait()
+
+    d_normed = product(d_before_ref[...], up[...]).astype(LOW)
+    split_store(index, d_normed, outs, n_seq)
 
 
 def ffn_back(grad_row, slope, w_down, w_up, n_seq):
     length, width = grad_row.shape
     hidden = w_up.shape[0]
     count = length // n_seq
-    sizes = [count] * n_seq if n_seq != 4 else [count, count, count, count // 2, count // 2]
     return pl.pallas_call(
         functools.partial(ffn_back_kernel, n_seq),
         grid=(n_seq,),
@@ -549,21 +545,91 @@
             pl.BlockSpec((count, hidden), lambda k: (k, 0)),
             pl.BlockSpec((1, hidden), lambda k: (0, 0)),
         ]
-        + [pl.BlockSpec((size, width), lambda k: (0, 0)) for size in sizes],
+        + split_specs(count, width, n_seq),
         out_shape=[
             jax.ShapeDtypeStruct((length, hidden), LOW),
             jax.ShapeDtypeStruct((1, hidden), WIDE),
         ]
-        + [jax.ShapeDtypeStruct((size, width), LOW) for size in sizes],
+        + split_shapes(count, width, n_seq),
         scratch_shapes=[
             pltpu.VMEM((hidden, width), LOW),
             pltpu.VMEM((hidden, width), LOW),
             pltpu.SemaphoreType.DMA((2,)),
         ],
         compiler_params=pltpu.CompilerParams(vmem_limit_bytes=VMEM_LIMIT),
-        cost_estimate=pl.CostEstimate(flops=length * width, bytes_accessed=length, transcendentals=0),
+        cost_estimate=cost(28),
         name="ffn_back",
     )(grad_row, slope, w_down, w_up)
+
+
+def feed_kernel(n_seq, hidden_ref, down_ref, *outs):
+    values = product(hidden_ref[...], down_ref[...]).astype(LOW)
+    split_store(pl.program_id(0), values, outs, n_seq)
+
+
+def feed_down(hidden_low, w_down, n_seq):
+    length, hidden = hidden_low.shape
+    width = w_down.shape[1]
+    count = length // n_seq
+    return pl.pallas_call(
+        functools.partial(feed_kernel, n_seq),
+        grid=(n_seq,),
+        in_specs=[
+            pl.BlockSpec((count, hidden), lambda k: (k, 0)),
+            pl.BlockSpec((hidden, width), lambda k: (0, 0), pipeline_mode=pl.Buffered(1)),
+        ],
+        out_specs=split_specs(count, width, n_seq),
+        out_shape=split_shapes(count, width, n_seq),
+        compiler_params=pltpu.CompilerParams(vmem_limit_bytes=VMEM_LIMIT),
+        cost_estimate=cost(15.6),
+        name="feed_down",
+    )(hidden_low, w_down)
+
+
+def qkv_back_kernel(n_seq, grad_ref, w_ref, row_ref, sums_ref, bias_ref, *outs):
+    index = pl.program_id(0)
+
+    @pl.when(index == 0)
+    def _():
+        sums_ref[...] = jnp.zeros_like(sums_ref)
+        bias_ref[...] = jnp.zeros_like(bias_ref)
+
+    d_normed = product_t(grad_ref[...], w_ref[...])
+    row = row_ref[...].astype(WIDE)
+    centre, inverse = norm_stats(row)
+    normed = (row - centre) * inverse
+    sums_ref[0:1, :] += jnp.sum(d_normed * normed, axis=0, keepdims=True)
+    sums_ref[1:2, :] += jnp.sum(d_normed, axis=0, keepdims=True)
+    bias_ref[0:1, :] += jnp.sum(grad_ref[...].astype(WIDE), axis=0, keepdims=True)
+    split_store(index, d_normed.astype(LOW), outs, n_seq)
+
+
+def qkv_back(d_qkv, qkv_full, row_low, n_seq):
+    length, width = row_low.shape
+    columns = d_qkv.shape[1]
+    count = length // n_seq
+    return pl.pallas_call(
+        functools.partial(qkv_back_kernel, n_seq),
+        grid=(n_seq,),
+        in_specs=[
+            pl.BlockSpec((count, columns), lambda k: (k, 0)),
+            pl.BlockSpec((width, columns), lambda k: (0, 0), pipeline_mode=pl.Buffered(1)),
+            pl.BlockSpec((count, width), lambda k: (k, 0)),
+        ],
+        out_specs=[
+            pl.BlockSpec((8, width), lambda k: (0, 0)),
+            pl.BlockSpec((8, columns), lambda k: (0, 0)),
+        ]
+        + split_specs(count, width, n_seq),
+        out_shape=[
+            jax.ShapeDtypeStruct((8, width), WIDE),
+            jax.ShapeDtypeStruct((8, columns), WIDE),
+        ]
+        + split_shapes(count, width, n_seq),
+        compiler_params=pltpu.CompilerParams(vmem_limit_bytes=VMEM_LIMIT),
+        cost_estimate=cost(15.3),
+        name="qkv_back",
+    )(d_qkv, qkv_full, row_low)
 
 
 def norm_back_kernel(pieces, *refs):
@@ -626,7 +692,7 @@
             jax.ShapeDtypeStruct((8, width), WIDE),
         ],
         compiler_params=pltpu.CompilerParams(vmem_limit_bytes=VMEM_LIMIT),
-        cost_estimate=pl.CostEstimate(flops=count * width, bytes_accessed=count, transcendentals=0),
+        cost_estimate=cost(11),
         name="norm_back",
     )(
         *[piece for part in parts for piece in part],
@@ -663,6 +729,7 @@
         ),
         out_shape=jax.ShapeDtypeStruct((own, 3 * width), WIDE),
         compiler_params=pltpu.CompilerParams(vmem_limit_bytes=VMEM_LIMIT),
+        cost_estimate=cost(2.5),
         name="format_qkv",
     )(me, *blocks)
 
@@ -728,6 +795,9 @@
         ],
         n_seq,
     )
+    held_row = gather_start(tokens, n_seq)
+    tied = tie(*moved, *held_row)
+    moved, held_row = list(tied[:n_seq]), list(tied[n_seq:])
     moved = jnp.concatenate(moved, axis=0).reshape(n_seq, own, part_width + EXTRA)
     out_part = lax.all_gather(w_out, "batch", axis=0, tiled=True)
     joined = lax.all_gather(moved.reshape(n_seq * own, part_width + EXTRA), "batch", axis=0)
@@ -750,7 +820,6 @@
     gain_one, bias_one, qv_bias, out_bias, gain_two, bias_two, up_bias_all, down_bias = params
     up_bias = lax.dynamic_slice_in_dim(up_bias_all, me * hidden_count, hidden_count)
 
-    held_row = gather_start(tokens, n_seq)
     *held_row, out_part = tie(*gather_end(held_row, n_seq), out_part)
     row_low = jnp.concatenate(held_row, axis=0)
     out_full = jnp.concatenate(gather_shared(out_part, n_seq, n_batch), axis=0)
@@ -794,10 +863,8 @@
     d_before, grad_upb, *blocks = ffn_back(grad_row, slope, down_all, up_all, n_seq)
     parts = scatter_send(blocks, n_seq)
     grad_up_part = pair_rows(d_before, normed_two_low, n_batch)
-    feed_part = product(hidden_low, down_all).astype(LOW)
-    parts[0][0], grad_up_part, feed_part, grad_down = tie(
-        parts[0][0], grad_up_part, feed_part, grad_down
-    )
+    feed_blocks = feed_down(hidden_low, down_all, n_seq)
+    parts[0][0], grad_up_part, *feed_blocks = tie(parts[0][0], grad_up_part, *feed_blocks)
     grad_up = scatter_batch(grad_up_part, n_batch)
     grad_downb = jnp.sum(grad_low.astype(WIDE), axis=0)
 
@@ -805,35 +872,33 @@
         parts, cotangent, normed_own, inverse_own, active, gain_two, out_full, n_seq
     )
     d_mixed = jnp.concatenate(exchange([d_mixed[bit] for bit in range(n_seq)], n_seq), axis=0)
-    d_mixed, d_branch, feed_part = tie(d_mixed, d_branch, feed_part)
+    d_mixed, d_branch = tie(d_mixed, d_branch)
     held_branch = gather_start(d_branch, n_seq)
     d_qkv = attend_back(me.reshape(1), qkv, d_mixed, starts, logsum, head_width)
-    d_qkv, *held_branch = tie(d_qkv, *held_branch)
+    tied = tie(d_qkv, *held_branch, *feed_blocks)
+    d_qkv, held_branch, feed_blocks = tied[0], tied[1 : len(held_branch) + 1], tied[len(held_branch) + 1 :]
     d_branch_row = jnp.concatenate(gather_end(held_branch, n_seq), axis=0)
 
     grad_qkv_part = pair_product(normed_sent, normed_kept, d_qkv, n_batch)
-    grad_qkv_part, grad_up = tie(grad_qkv_part, grad_up)
+    grad_qkv_part, grad_up, grad_down = tie(grad_qkv_part, grad_up, grad_down)
     reduced = scatter_batch(grad_qkv_part, n_batch)
 
-    d_normed_part = product_t(d_qkv, qkv_full)
-    grad_gain_one = jnp.sum(d_normed_part * normed_one, axis=0)
-    grad_bias_one = jnp.sum(d_normed_part, axis=0)
-    feed = scatter_end(scatter_send(scatter_split(feed_part, n_seq), n_seq)) + down_bias
-    layer_out = (middle_own + active * feed).astype(LOW)
-    d_normed_low, layer_out = tie(d_normed_part.astype(LOW), layer_out)
+    sums_one, d_bias, *blocks_one = qkv_back(d_qkv, qkv_full, row_low, n_seq)
+    d_bias = d_bias[0]
+    tied = tie(*scatter_start(blocks_one, n_seq), *feed_blocks)
+    blocks_one, feed_blocks = tied[: len(blocks_one)], scatter_start(tied[len(blocks_one) :], n_seq)
 
     def place(values, total):
         return lax.dynamic_update_slice_in_dim(
             jnp.zeros((total,), WIDE), values, me * values.shape[0], 0
         )
 
-    d_bias = jnp.sum(d_qkv.astype(WIDE), axis=0)
     grad_qvb = jnp.concatenate(
         [place(d_bias[:head_width], width), place(d_bias[2 * head_width :], width)]
     )
     small_grads = (
-        grad_gain_one,
-        grad_bias_one,
+        sums_one[0],
+        sums_one[1],
         grad_qvb,
         sums[2],
         sums[0],
@@ -842,22 +907,16 @@
         grad_downb,
     )
     packed = jnp.concatenate([g.reshape(n_seq, n_batch, -1) for g in small_grads], axis=2)
-    packed = packed.transpose(1, 0, 2).reshape(n_batch, own, -1).astype(LOW)
-    lanes_back = packed.shape[2]
-    packed = jnp.pad(packed, ((0, 0), (0, 0), (0, EXTRA - lanes_back)))
-    packed = packed.reshape(n_batch // 2, 2, own, EXTRA)
+    rows_back = -(-n_small // EXTRA)
+    packed = jnp.pad(packed, ((0, 0), (0, 0), (0, rows_back * EXTRA - n_small)))
+    packed = packed.reshape(n_seq, n_batch, rows_back, EXTRA).transpose(1, 0, 2, 3).astype(LOW)
+    packed = packed.reshape(n_batch // 2, 2, n_seq * rows_back, EXTRA)
+    packed = jnp.pad(packed, ((0, 0), (0, 0), (0, own - n_seq * rows_back), (0, 0)))
     packed_sent = lax.dynamic_index_in_dim(packed, 1 - side, 1, False).reshape(-1, EXTRA)
     packed_kept = lax.dynamic_index_in_dim(packed, side, 1, False).reshape(-1, EXTRA)
     packed_part = packed_kept + flip(packed_sent, "batch", 1, n_batch)
     grad_out_part = pair_product(mixed_sent, mixed_kept, d_branch_row, n_batch)
     grad_out_part = jnp.concatenate([grad_out_part, packed_part], axis=1)
-    d_normed_one = scatter_end(scatter_send(scatter_split(d_normed_low, n_seq), n_seq))
-    row_own = tokens.astype(WIDE)
-    centre_own, inverse_first = norm_stats(row_own)
-    d_input = d_middle + norm_backward(
-        d_normed_one, (row_own - centre_own) * inverse_first, inverse_first, gain_one
-    )
-
     grad_out_part, reduced = tie(grad_out_part, reduced)
     reduced_out = scatter_batch(grad_out_part, n_batch)
     blocks = [
@@ -867,11 +926,23 @@
         for bit in range(n_seq)
     ]
     grad_qkv = format_qkv(me.reshape(1), blocks, width, n_seq)
+    grad_qkv, *feed_blocks = tie(grad_qkv, *feed_blocks)
+    feed = scatter_end(scatter_next(feed_blocks, n_seq)) + down_bias
+    layer_out = (middle_own + active * feed).astype(LOW)
+    parts_one = scatter_next(blocks_one, n_seq)
+    parts_one[0][0], reduced_out = tie(parts_one[0][0], reduced_out)
+    d_normed_one = scatter_end(parts_one)
+    row_own = tokens.astype(WIDE)
+    centre_own, inverse_first = norm_stats(row_own)
+    d_input = d_middle + norm_backward(
+        d_normed_one, (row_own - centre_own) * inverse_first, inverse_first, gain_one
+    )
     grad_out = reduced_out[:, :width]
-    small_rows = reduced_out[:, width:].reshape(n_seq, own // n_seq, EXTRA)
-    small_blocks = [lax.dynamic_index_in_dim(small_rows, me ^ bit, 0, False) for bit in range(n_seq)]
-    small_out = exchange(small_blocks, n_seq)
-    small_out = scatter_end([[block] for block in small_out])[:, :lanes_back].reshape(-1)
+    small_rows = reduced_out[: n_seq * rows_back, width:].reshape(n_seq, rows_back, EXTRA)
+    small_rows = exchange(
+        [lax.dynamic_index_in_dim(small_rows, me ^ bit, 0, False) for bit in range(n_seq)], n_seq
+    )
+    small_out = scatter_end([[block] for block in small_rows]).reshape(-1)
     small_result, at = [], 0
     for size in sizes:
         small_result.append(small_out[at : at + size])

time: 583 us -> 565 us (0.969)
  Pallas kernels: 168 us -> 199 us
  waiting for transfers between devices: 185 us -> 159 us
  matrix products: 50.5 us -> 27.6 us
    ppermute x52, waiting for transfers between devices: 172 us -> 137 us  [flip(): return lax.ppermute(values, axis, [(i, i ^ bit) for i in range(size)])]
    pallas_call x0 -> x2, Pallas kernels: none -> 30.8 us  [the longest x1 15.6 us: feed_down(): pl.pallas_call(functools.partial(feed_kernel, n_seq), grid=(n_seq,), in_s...]
    dot_general x2 -> x1, matrix products: 22.5 us -> 10.1 us  [product(): return jnp.dot(left, right, preferred_element_type=WIDE)]
    dot_general x1 -> x0, matrix products: 12.1 us -> none  [product_t(): lax.dot_general(left, right, (((1,), (1,)), ((), ())), preferred_element_...]
    all_gather x1, waiting for transfers between devices: 0.02 us -> 7.72 us  [shards(): lax.all_gather(moved.reshape(n_seq * own, part_width + EXTRA), 'batch', a...]
    unnamed x87 -> x102, local copies, waits for them, and re-layouts: 9.88 us -> 12.1 us
  transfers between devices with their start and end apart: 60 -> 60, of which waited for: 30 -> 31; matrix products, arithmetic and copies ran while one was open for 26% -> 23% of each run, Pallas kernels for 29% -> 36%
where the time goes in v3:
time: 565 us; the launch traced here: 560 us
  Pallas kernels  199 us (35%)
  waiting for transfers between devices  159 us (28%)
  local copies, waits for them, and re-layouts  64.9 us (11%)
  starting transfers between devices  51.9 us (9%)
  other arithmetic  41.8 us (7%)
  matrix products  27.6 us (5%)
  between operations  15.6 us (3%)
    ppermute x52, waiting for transfers between devices, flip(): return lax.ppermute(values, axis, [(i, i ^ bit) for i in range(size)])  137 us
    ppermute x52, starting transfers between devices, flip(): return lax.ppermute(values, axis, [(i, i ^ bit) for i in range(size)])  51.3 us
    pallas_call x4, Pallas kernels, rows_product(): pl.pallas_call(rows_kernel, grid_spec=pltpu.PrefetchScalarGridSpec(num_sc...  36.4 us
    pallas_call x1, Pallas kernels, ffn_back(): pl.pallas_call(functools.partial(ffn_back_kernel, n_seq), grid=(n_seq,),...  28.4 us
    pallas_call x1, Pallas kernels, attend_back(): pl.pallas_call(attend_back_kernel, grid_spec=pltpu.PrefetchScalarGridSpec...  23.4 us
    pallas_call x1, Pallas kernels, attend(): pl.pallas_call(attend_kernel, grid_spec=pltpu.PrefetchScalarGridSpec(num_...  20.5 us
    pallas_call x1, Pallas kernels, ffn_up(): pl.pallas_call(ffn_up_kernel, grid=(length // FFN_ROWS,), in_specs=[pl.Bl...  19.7 us
    pallas_call x1, Pallas kernels, out_norm(): pl.pallas_call(functools.partial(out_norm_kernel, n_seq), grid=(n_seq,),...  19.5 us
  transfers between devices with their start and end apart: 60, of which 31 were waited for; matrix products, arithmetic and copies ran while one was open for 23% of the time, Pallas kernels for 36%

profile of v3, /device:TPU:0, one launch (start us, length us, event | category | flops | bytes accessed | tf_op | source)
XLA Modules:
  0.0 559.6 jit_solution(9404985489296260202)
XLA Ops:
  26.4 15.0 %collective-permute-done.2 = bf16[64,1664]{1,0:T(8,128)(2,1)S(1)} collective-permute-done((bf16[64,1664]{1,0:T(8,128)(2,1)S(1)}, bf16[64,1664]{1,0:T(8,128)(2,1)S(1)}, u32[]{:S(2)}, u32[]{:S(2)}) %collective-permute-start.2) | collective-permute-done | bytes 213024 | tf_op jit(solution)/shard_map/ppermute | solution.py:57
  50.3 10.5 %collective-permute-done.6 = bf16[128,2048]{1,0:T(8,128)(2,1)S(1)} collective-permute-done((bf16[128,2048]{1,0:T(8,128)(2,1)S(1)}, bf16[128,2048]{1,0:T(8,128)(2,1)S(1)}, u32[]{:S(2)}, u32[]{:S(2)}) %collective-permute-start.6) | collective-permute-done | bytes 524320 | tf_op jit(solution)/shard_map/ppermute | solution.py:57
  69.6 18.6 %collective-permute-done.9 = bf16[256,2048]{1,0:T(8,128)(2,1)S(1)} collective-permute-done((bf16[256,2048]{1,0:T(8,128)(2,1)}, bf16[256,2048]{1,0:T(8,128)(2,1)S(1)}, u32[]{:S(2)}, u32[]{:S(2)}) %collective-permute-start.9) | collective-permute-done | bytes 1048608 | tf_op jit(solution)/shard_map/ppermute | solution.py:57
  108.1 7.7 %all-gather.12.cloned.1.call-done = bf16[2048,1664]{1,0:T(8,128)(2,1)} async-done(((bf16[256,1664]{1,0:T(8,128)(2,1)}), bf16[2048,1664]{1,0:T(8,128)(2,1)}) %all-gather.12.cloned.1.call-update) | async-done | bytes 6815760 | tf_op jit(solution)/shard_map/all_gather | solution.py:803
  135.5 10.1 %add_convert_fusion.1.q_ref.k_ref.v_ref = bf16[1024,1536]{1,0:T(8,128)(2,1)} fusion(bf16[1024,2048]{1,0:T(8,128)(2,1)S(1)} %fusion.5, bf16[2048,1536]{1,0:T(8,128)(2,1)} %get-tuple-element.134.w_ref, f32[1536]{0:T(1024)S(1)} %pad_maximum_fusion.6), kind=kOutput, calls=%fused_computation.9 | convolution fusion | flops 6445596672 | bytes 13637632 | tf_op jit(solution)/shard_map/dot_general | solution.py:31
  147.0 20.5 %attend.1 = (bf16[1024,512]{1,0:T(8,128)(2,1)}, f32[4,2,1024]{2,1,0:T(2,128)}) custom-call(s32[1]{0:T(128)} %bitcast.me_ref, bf16[1024,1536]{1,0:T(8,128)(2,1)} %add_convert_fusion.1.q_ref.k_ref.v_ref, bf16[1024,1536]{1,0:T(8,128)(2,1)} %add_convert_fusion.1.q_ref.k_ref.v_ref, bf16[1024,1536]{1,0:T(8,128)(2,1)} %add_convert_fusion.1.q_ref.k_ref.v_ref, ...), custom_call_target="tpu_custom_call" | custom-call | flops 9429999616 | bytes 1024 | tf_op jit(solution)/shard_map/attend/pallas_call | solution.py:228
  175.7 15.6 %collective-permute-done.19.refs_2_ = bf16[1024,512]{1,0:T(8,128)(2,1)} collective-permute-done((bf16[1024,512]{1,0:T(8,128)(2,1)}, bf16[1024,512]{1,0:T(8,128)(2,1)}, u32[]{:S(2)}, u32[]{:S(2)}) %collective-permute-start.19) | collective-permute-done | bytes 1048608 | tf_op jit(solution)/shard_map/ppermute | solution.py:57
  207.1 19.5 %out_norm.1 = (bf16[1024,2048]{1,0:T(8,128)(2,1)}, f32[256,2048]{1,0:T(8,128)}, f32[256,2048]{1,0:T(8,128)}, f32[256,1]{1,0:T(8,128)}) custom-call(bf16[1024,512]{1,0:T(8,128)(2,1)} %get-tuple-element.139.refs_0_, bf16[1024,512]{1,0:T(8,128)(2,1)} %collective-permute-done.18.refs_1_, bf16[1024,512]{1,0:T(8,128)(2,1)} %collective-permute-done.19.refs_2_, ...), custom_call_target="tpu_custom_call" | custom-call | flops 8924000256 | bytes 1024 | tf_op jit(solution)/shard_map/out_norm/pallas_call | solution.py:360
  226.7 19.7 %ffn_up.1 = (bf16[1024,2048]{1,0:T(8,128)(2,1)}, f32[1024,2048]{1,0:T(8,128)}) custom-call(bf16[1024,2048]{1,0:T(8,128)(2,1)} %get-tuple-element.142.n_ref.right_ref, bf16[2048,2048]{1,0:T(8,128)(2,1)} %all-gather.8.cloned.1.call-done.w_ref.up_ref, f32[1,2048]{1,0:T(1,128)} %bitcast.127), custom_call_target="tpu_custom_call" | custom-call | flops 9016000512 | bytes 1024 | tf_op jit(solution)/shard_map/ffn_up/pallas_call | solution.py:446
  246.4 8.8 %rows_product.4 = bf16[1024,2048]{1,0:T(8,128)(2,1)} custom-call(s32[1]{0:T(128)S(6)} %sub.20.side_ref, bf16[1024,2048]{1,0:T(8,128)(2,1)} %get-tuple-element.143.left_ref.hidden_ref, bf16[1024,2048]{1,0:T(8,128)(2,1)} %constant_dynamic-update-slice_fusion.7.right_ref.grad_ref), custom_call_target="tpu_custom_call" | custom-call | flops 4140000000 | bytes 1024 | tf_op jit(solution)/shard_map/rows_product/pallas_call | solution.py:135
  255.1 6.4 %copy.40 = bf16[1024,2048]{0,1:T(8,128)(2,1)} copy(bf16[1024,2048]{1,0:T(8,128)(2,1)} %copy-done.2) | data formatting | bytes 8388608 | tf_op jit(solution)/shard_map/optimization_barrier | solution.py:61
  269.3 9.4 %rows_product.5 = bf16[1024,2048]{1,0:T(8,128)(2,1)} custom-call(s32[1]{0:T(128)} %bitcast.18.side_ref, bf16[1024,2048]{1,0:T(8,128)(2,1)} %get-tuple-element.143.left_ref.hidden_ref, bf16[1024,2048]{1,0:T(8,128)(2,1)} %constant_dynamic-update-slice_fusion.7.right_ref.grad_ref, bf16[1024,2048]{1,0:T(8,128)(2,1)} %collective-permute-done.22.refs_0_), custom_call_target="tpu_custom_call" | custom-call | flops 4140000000 | bytes 1024 | tf_op jit(solution)/shard_map/rows_product/pallas_call | solution.py:135
  280.3 28.4 %ffn_back.1 = (bf16[1024,2048]{1,0:T(8,128)(2,1)}, f32[1,2048]{1,0:T(1,128)}, bf16[256,2048]{1,0:T(8,128)(2,1)}, bf16[256,2048]{1,0:T(8,128)(2,1)}, bf16[256,204...) custom-call(bf16[1024,2048]{1,0:T(8,128)(2,1)} %constant_dynamic-update-slice_fusion.7.right_ref.grad_ref, ...), custom_call_target="tpu_custom_call" | custom-call | flops 12880000000 | bytes 1024 | tf_op jit(solution)/shard_map/ffn_back/pallas_call | solution.py:535
  308.7 8.7 %rows_product.6 = bf16[1024,2048]{1,0:T(8,128)(2,1)} custom-call(s32[1]{0:T(128)S(6)} %sub.20.side_ref, bf16[1024,2048]{1,0:T(8,128)(2,1)} %get-tuple-element.152.left_ref, bf16[1024,2048]{1,0:T(8,128)(2,1)} %get-tuple-element.142.n_ref.right_ref), custom_call_target="tpu_custom_call" | custom-call | flops 4140000000 | bytes 1024 | tf_op jit(solution)/shard_map/rows_product/pallas_call | solution.py:135
  320.6 15.6 %feed_down.1 = (bf16[256,2048]{1,0:T(8,128)(2,1)}, bf16[256,2048]{1,0:T(8,128)(2,1)}, bf16[256,2048]{1,0:T(8,128)(2,1)}, bf16[128,2048]{1,0:T(8,128)(2,1)}, bf16[128,2048]{1,0:T(8,128)(2,1)}) custom-call(bf16[1024,2048]{1,0:T(8,128)(2,1)} %get-tuple-element.143.left_ref.hidden_ref, bf16[2048,2048]{1,0:T(8,128)(2,1)} %all-gather.10.cloned.1.call-done.down_ref), custom_call_target="tpu_custom_call" | custom-call | flops 7176000000 | bytes 1024 | tf_op jit(solution)/shard_map/feed_down/pallas_call | solution.py:574
  338.2 9.5 %rows_product.7 = bf16[1024,2048]{1,0:T(8,128)(2,1)} custom-call(s32[1]{0:T(128)} %bitcast.18.side_ref, bf16[1024,2048]{1,0:T(8,128)(2,1)} %get-tuple-element.152.left_ref, bf16[1024,2048]{1,0:T(8,128)(2,1)} %get-tuple-element.142.n_ref.right_ref, bf16[1024,2048]{1,0:T(8,128)(2,1)} %copy-done.4), custom_call_target="tpu_custom_call" | custom-call | flops 4140000000 | bytes 1024 | tf_op jit(solution)/shard_map/rows_product/pallas_call | solution.py:135
  353.9 10.7 %collective-permute-done.26.refs_3_ = bf16[128,2048]{1,0:T(8,128)(2,1)} collective-permute-done((bf16[128,2048]{1,0:T(8,128)(2,1)}, bf16[128,2048]{1,0:T(8,128)(2,1)}, u32[]{:S(2)}, u32[]{:S(2)}) %collective-permute-start.26) | collective-permute-done | bytes 524320 | tf_op jit(solution)/shard_map/ppermute | solution.py:57
  366.5 11.2 %norm_back.1 = (f32[256,2048]{1,0:T(8,128)}, bf16[256,2048]{1,0:T(8,128)(2,1)}, bf16[4,256,512]{2,1,0:T(8,128)(2,1)}, f32[8,2048]{1,0:T(8,128)}) custom-call(bf16[256,2048]{1,0:T(8,128)(2,1)} %get-tuple-element.158.refs_0_, bf16[256,2048]{1,0:T(8,128)(2,1)} %collective-permute-done.24.refs_1_, bf16[256,2048]{1,0:T(8,128)(2,1)} %collective-permute-done.25.refs_2_, ...), custom_call_target="tpu_custom_call" | custom-call | flops 5059999744 | bytes 1024 | tf_op jit(solution)/shard_map/norm_back/pallas_call | solution.py:669
  382.7 6.7 %collective-permute-done.30 = bf16[256,512]{1,0:T(8,128)(2,1)S(1)} collective-permute-done((bf16[256,512]{1,0:T(8,128)(2,1)S(1)}, bf16[256,512]{1,0:T(8,128)(2,1)S(1)}, u32[]{:S(2)}, u32[]{:S(2)}) %collective-permute-start.30) | collective-permute-done | bytes 262176 | tf_op jit(solution)/shard_map/ppermute | solution.py:57
  396.1 23.4 %attend_back.1.grad_ref = bf16[1024,1536]{1,0:T(8,128)(2,1)} custom-call(s32[1]{0:T(128)} %bitcast.me_ref, bf16[1024,1536]{1,0:T(8,128)(2,1)} %add_convert_fusion.1.q_ref.k_ref.v_ref, bf16[1024,1536]{1,0:T(8,128)(2,1)} %add_convert_fusion.1.q_ref.k_ref.v_ref, bf16[1024,1536]{1,0:T(8,128)(2,1)} %add_convert_fusion.1.q_ref.k_ref.v_ref, ...), custom_call_target="tpu_custom_call" | custom-call | flops 10764000256 | bytes 1024 | tf_op jit(solution)/shard_map/attend_back/pallas_call | solution.py:301
  419.5 6.4 %convolution_convert_fusion = bf16[1024,1536]{1,0:T(8,128)(2,1)S(1)} fusion(bf16[1024,1024]{0,1:T(8,128)(2,1)} %get-tuple-element.185, bf16[1024,1536]{1,0:T(8,128)(2,1)} %attend_back.1.grad_ref), kind=kOutput, calls=%fused_computation.12 | convolution fusion | flops 3222798336 | bytes 8388608 | tf_op jit(solution)/shard_map/dot_general | solution.py:39
  442.5 15.1 %qkv_back.1 = (f32[8,2048]{1,0:T(8,128)}, f32[8,1536]{1,0:T(8,128)}, bf16[256,2048]{1,0:T(8,128)(2,1)}, bf16[256,2048]{1,0:T(8,128)(2,1)}, bf16[256,2048]{1,0:T(...) custom-call(bf16[1024,1536]{1,0:T(8,128)(2,1)} %attend_back.1.grad_ref, ...), custom_call_target="tpu_custom_call" | custom-call | flops 7038000128 | bytes 1024 | tf_op jit(solution)/shard_map/qkv_back/pallas_call | solution.py:611
  465.9 16.4 %collective-permute-done.41 = bf16[256,2048]{1,0:T(8,128)(2,1)} collective-permute-done((bf16[256,2048]{1,0:T(8,128)(2,1)}, bf16[256,2048]{1,0:T(8,128)(2,1)}, u32[]{:S(2)}, u32[]{:S(2)}) %collective-permute-start.41) | collective-permute-done | bytes 1048608 | tf_op jit(solution)/shard_map/ppermute | solution.py:57
  489.6 10.7 %reduce-scatter.9.cloned.1.call-done = bf16[256,1536]{1,0:T(8,128)(2,1)} async-done(((bf16[1024,1536]{1,0:T(8,128)(2,1)}), bf16[256,1536]{1,0:T(8,128)(2,1)}) %reduce-scatter.9.cloned.1.call-update) | async-done | bytes 786448 | tf_op jit(solution)/shard_map/reduce_scatter | solution.py:169
  (351 shorter events, 219.4 us)
Async XLA Ops:
  7.2 55.8 %all-gather.6.cloned.1.call-start = ((), (), s32[]{:S(2)}) async-start(), calls=%async_computation.4 | async-start | bytes 2359296 | tf_op jit(solution)/shard_map/all_gather | solution.py:802
  7.9 107.9 %all-gather.12.cloned.1.call-start = ((), (), s32[]{:S(2)}) async-start(), calls=%async_computation.11 | async-start | bytes 7667712 | tf_op jit(solution)/shard_map/all_gather | solution.py:803
  8.0 37.0 %collective-permute-start.4 = (bf16[256,2048]{1,0:T(8,128)(2,1)}, bf16[256,2048]{1,0:T(8,128)(2,1)S(1)}, u32[]{:S(2)}, u32[]{:S(2)}) collective-permute-start(bf16[256,2048]{1,0:T(8,128)(2,1)} %bitcast.105), channel_id=1, source_target_pairs={{0,16},{8,24},{16,0},{24,8},{1,17},{9,25},{17,1},{25,9},{2,18},{10... | collective-permute-start | bytes 3145736 | tf_op jit(solution)/shard_map/ppermute | solution.py:57
  11.0 34.0 %collective-permute-start.3 = (bf16[256,2048]{1,0:T(8,128)(2,1)}, bf16[256,2048]{1,0:T(8,128)(2,1)}, u32[]{:S(2)}, u32[]{:S(2)}) collective-permute-start(bf16[256,2048]{1,0:T(8,128)(2,1)} %bitcast.106), channel_id=1, source_target_pairs={{0,8},{8,0},{16,24},{24,16},{1,9},{9,1},{17,25},{25,17},{2,10},{10... | collective-permute-start | bytes 3145736 | tf_op jit(solution)/shard_map/ppermute | solution.py:57
  46.3 180.4 %all-gather.8.cloned.1.call-start = ((), (), s32[]{:S(2)}) async-start(), calls=%async_computation.5 | async-start | bytes 9437184 | tf_op jit(solution)/shard_map/all_gather | solution.py:804
  47.0 233.2 %all-gather.10.cloned.1.call-start = ((), (), s32[]{:S(2)}) async-start(), calls=%async_computation.6 | async-start | bytes 9437184 | tf_op jit(solution)/shard_map/all_gather | solution.py:805
  65.3 22.9 %collective-permute-start.9 = (bf16[256,2048]{1,0:T(8,128)(2,1)}, bf16[256,2048]{1,0:T(8,128)(2,1)S(1)}, u32[]{:S(2)}, u32[]{:S(2)}) collective-permute-start(bf16[256,2048]{1,0:T(8,128)(2,1)} %constant_dynamic-slice_fusion.10), channel_id=1, source_target_pairs={{0,16},{8,24},{16,0},{24,8},{1,17},{9,25},{17,1},{25,9},{2,18},{10... | collective-permute-start | bytes 3145736 | tf_op jit(solution)/shard_map/ppermute | solution.py:57
  65.8 23.4 %collective-permute-start.7 = (bf16[256,2048]{1,0:T(8,128)(2,1)}, bf16[256,2048]{1,0:T(8,128)(2,1)}, u32[]{:S(2)}, u32[]{:S(2)}) collective-permute-start(bf16[256,2048]{1,0:T(8,128)(2,1)} %constant_dynamic-slice_fusion.10), channel_id=1, source_target_pairs={{0,8},{8,0},{16,24},{24,16},{1,9},{9,1},{17,25},{25,17},{2,10},{10... | collective-permute-start | bytes 3145736 | tf_op jit(solution)/shard_map/ppermute | solution.py:57
  66.5 369.9 %reduce-scatter.7.cloned.1.call-start = ((), (), s32[]{:S(2)}) async-start(), calls=%async_computation.8 | async-start | bytes 5242880 | tf_op jit(solution)/shard_map/reduce_scatter | solution.py:169
  104.1 25.8 %collective-permute-start.15 = (bf16[256,2048]{1,0:T(8,128)(2,1)S(1)}, bf16[256,2048]{1,0:T(8,128)(2,1)}, u32[]{:S(2)}, u32[]{:S(2)}) collective-permute-start(bf16[256,2048]{1,0:T(8,128)(2,1)S(1)} %multiply_convert_fusion), channel_id=1, source_target_pairs={{0,16},{8,24},{16,0},{24,8},{1,17},{9,25},{17,1},{25,9},{2,18},{10... | collective-permute-start | bytes 3145736 | tf_op jit(solution)/shard_map/ppermute | solution.py:57
  106.0 25.4 %collective-permute-start.14 = (bf16[256,2048]{1,0:T(8,128)(2,1)S(1)}, bf16[256,2048]{1,0:T(8,128)(2,1)}, u32[]{:S(2)}, u32[]{:S(2)}) collective-permute-start(bf16[256,2048]{1,0:T(8,128)(2,1)S(1)} %multiply_convert_fusion), channel_id=1, source_target_pairs={{0,8},{8,0},{16,24},{24,16},{1,9},{9,1},{17,25},{25,17},{2,10},{10... | collective-permute-start | bytes 3145736 | tf_op jit(solution)/shard_map/ppermute | solution.py:57
  167.5 23.8 %collective-permute-start.19 = (bf16[1024,512]{1,0:T(8,128)(2,1)}, bf16[1024,512]{1,0:T(8,128)(2,1)}, u32[]{:S(2)}, u32[]{:S(2)}) collective-permute-start(bf16[1024,512]{1,0:T(8,128)(2,1)} %get-tuple-element.139.refs_0_), channel_id=1, source_target_pairs={{0,16},{8,24},{16,0},{24,8},{1,17},{9,25},{17,1},{25,9},{2,18},{10... | collective-permute-start | bytes 3145736 | tf_op jit(solution)/shard_map/ppermute | solution.py:57
  168.9 25.0 %collective-permute-start.18 = (bf16[1024,512]{1,0:T(8,128)(2,1)}, bf16[1024,512]{1,0:T(8,128)(2,1)}, u32[]{:S(2)}, u32[]{:S(2)}) collective-permute-start(bf16[1024,512]{1,0:T(8,128)(2,1)} %get-tuple-element.139.refs_0_), channel_id=1, source_target_pairs={{0,8},{8,0},{16,24},{24,16},{1,9},{9,1},{17,25},{25,17},{2,10},{10... | collective-permute-start | bytes 3145736 | tf_op jit(solution)/shard_map/ppermute | solution.py:57
  280.2 157.0 %reduce-scatter.5.cloned.1.call-start = ((), (), s32[]{:S(2)}) async-start(), calls=%async_computation.7 | async-start | bytes 5242880 | tf_op jit(solution)/shard_map/reduce_scatter | solution.py:169
  317.6 30.1 %collective-permute-start.24 = (bf16[256,2048]{1,0:T(8,128)(2,1)}, bf16[256,2048]{1,0:T(8,128)(2,1)}, u32[]{:S(2)}, u32[]{:S(2)}) collective-permute-start(bf16[256,2048]{1,0:T(8,128)(2,1)} %get-tuple-element.159), channel_id=1, source_target_pairs={{0,8},{8,0},{16,24},{24,16},{1,9},{9,1},{17,25},{25,17},{2,10},{10... | collective-permute-start | bytes 3145736 | tf_op jit(solution)/shard_map/ppermute | solution.py:57
  319.1 32.1 %collective-permute-start.25 = (bf16[256,2048]{1,0:T(8,128)(2,1)}, bf16[256,2048]{1,0:T(8,128)(2,1)}, u32[]{:S(2)}, u32[]{:S(2)}) collective-permute-start(bf16[256,2048]{1,0:T(8,128)(2,1)} %get-tuple-element.160), channel_id=1, source_target_pairs={{0,16},{8,24},{16,0},{24,8},{1,17},{9,25},{17,1},{25,9},{2,18},{10... | collective-permute-start | bytes 3145736 | tf_op jit(solution)/shard_map/ppermute | solution.py:57
  347.7 152.6 %reduce-scatter.9.cloned.1.call-start = ((), (), s32[]{:S(2)}) async-start(), calls=%async_computation.9 | async-start | bytes 3932160 | tf_op jit(solution)/shard_map/reduce_scatter | solution.py:169
  394.2 25.3 %collective-permute-start.32 = (bf16[256,2048]{1,0:T(8,128)(2,1)S(1)}, bf16[256,2048]{1,0:T(8,128)(2,1)S(1)}, u32[]{:S(2)}, u32[]{:S(2)}) collective-permute-start(bf16[256,2048]{1,0:T(8,128)(2,1)S(1)} %copy-done.17), channel_id=1, source_target_pairs={{0,16},{8,24},{16,0},{24,8},{1,17},{9,25},{17,1},{25,9},{2,18},{10... | collective-permute-start | bytes 3145736 | tf_op jit(solution)/shard_map/ppermute | solution.py:57
  395.0 24.5 %collective-permute-start.31 = (bf16[256,2048]{1,0:T(8,128)(2,1)S(1)}, bf16[256,2048]{1,0:T(8,128)(2,1)S(1)}, u32[]{:S(2)}, u32[]{:S(2)}) collective-permute-start(bf16[256,2048]{1,0:T(8,128)(2,1)S(1)} %copy-done.17), channel_id=1, source_target_pairs={{0,8},{8,0},{16,24},{24,16},{1,9},{9,1},{17,25},{25,17},{2,10},{10... | collective-permute-start | bytes 3145736 | tf_op jit(solution)/shard_map/ppermute | solution.py:57
  437.2 98.9 %reduce-scatter.11.cloned.1.call-start = ((), (), s32[]{:S(2)}) async-start(), calls=%async_computation.10 | async-start | bytes 1392640 | tf_op jit(solution)/shard_map/reduce_scatter | solution.py:169
  457.7 24.6 %collective-permute-start.41 = (bf16[256,2048]{1,0:T(8,128)(2,1)}, bf16[256,2048]{1,0:T(8,128)(2,1)}, u32[]{:S(2)}, u32[]{:S(2)}) collective-permute-start(bf16[256,2048]{1,0:T(8,128)(2,1)} %get-tuple-element.191), channel_id=1, source_target_pairs={{0,8},{8,0},{16,24},{24,16},{1,9},{9,1},{17,25},{25,17},{2,10},{10... | collective-permute-start | bytes 3145736 | tf_op jit(solution)/shard_map/ppermute | solution.py:57
  458.2 24.6 %collective-permute-start.42 = (bf16[256,2048]{1,0:T(8,128)(2,1)}, bf16[256,2048]{1,0:T(8,128)(2,1)}, u32[]{:S(2)}, u32[]{:S(2)}) collective-permute-start(bf16[256,2048]{1,0:T(8,128)(2,1)} %get-tuple-element.192), channel_id=1, source_target_pairs={{0,16},{8,24},{16,0},{24,8},{1,17},{9,25},{17,1},{25,9},{2,18},{10... | collective-permute-start | bytes 3145736 | tf_op jit(solution)/shard_map/ppermute | solution.py:57
  482.8 35.4 %collective-permute-start.43 = (bf16[256,2048]{1,0:T(8,128)(2,1)}, bf16[256,2048]{1,0:T(8,128)(2,1)S(1)}, u32[]{:S(2)}, u32[]{:S(2)}) collective-permute-start(bf16[256,2048]{1,0:T(8,128)(2,1)} %get-tuple-element.201), channel_id=1, source_target_pairs={{0,8},{8,0},{16,24},{24,16},{1,9},{9,1},{17,25},{25,17},{2,10},{10... | collective-permute-start | bytes 3145736 | tf_op jit(solution)/shard_map/ppermute | solution.py:57
  484.1 34.1 %collective-permute-start.44 = (bf16[256,2048]{1,0:T(8,128)(2,1)}, bf16[256,2048]{1,0:T(8,128)(2,1)S(1)}, u32[]{:S(2)}, u32[]{:S(2)}) collective-permute-start(bf16[256,2048]{1,0:T(8,128)(2,1)} %get-tuple-element.202), channel_id=1, source_target_pairs={{0,16},{8,24},{16,0},{24,8},{1,17},{9,25},{17,1},{25,9},{2,18},{10... | collective-permute-start | bytes 3145736 | tf_op jit(solution)/shard_map/ppermute | solution.py:57
  (80 other events, 854.0 us)
Sparse Core Ops, SparseCore 0:
  9.6 31.7 all-gather.5
  46.4 69.3 all-gather.11
  117.4 80.6 all-gather.7
  199.6 80.5 all-gather.9
  282.3 75.2 reduce-scatter.6
  359.9 77.2 reduce-scatter.4
  439.5 60.7 reduce-scatter.8
  507.9 28.1 reduce-scatter.10

commit v4 on v3

--- a/solution.py
+++ b/solution.py
@@ -917,6 +917,8 @@
     packed_part = packed_kept + flip(packed_sent, "batch", 1, n_batch)
     grad_out_part = pair_product(mixed_sent, mixed_kept, d_branch_row, n_batch)
     grad_out_part = jnp.concatenate([grad_out_part, packed_part], axis=1)
+    grad_up, grad_down = grad_up.astype(WIDE), grad_down.astype(WIDE)
+    grad_out_part, grad_up, grad_down = tie(grad_out_part, grad_up, grad_down)
     grad_out_part, reduced = tie(grad_out_part, reduced)
     reduced_out = scatter_batch(grad_out_part, n_batch)
     blocks = [
@@ -930,7 +932,7 @@
     feed = scatter_end(scatter_next(feed_blocks, n_seq)) + down_bias
     layer_out = (middle_own + active * feed).astype(LOW)
     parts_one = scatter_next(blocks_one, n_seq)
-    parts_one[0][0], reduced_out = tie(parts_one[0][0], reduced_out)
+    parts_one[0][0], grad_qkv = tie(parts_one[0][0], grad_qkv)
     d_normed_one = scatter_end(parts_one)
     row_own = tokens.astype(WIDE)
     centre_own, inverse_first = norm_stats(row_own)
@@ -959,9 +961,9 @@
         g_outb,
         g_two,
         c_two,
-        grad_up.astype(WIDE),
+        grad_up,
         g_upb,
-        grad_down.astype(WIDE),
+        grad_down,
         g_downb,
     )
 

time: 565 us -> 563 us (level)
  waiting for transfers between devices: 159 us -> 148 us
  local copies, waits for them, and re-layouts: 64.9 us -> 73.5 us
    reduce_scatter x4, waiting for transfers between devices: 11.5 us -> 2.59 us  [scatter_batch(): lax.psum_scatter(total, 'batch', scatter_dimension=0, tiled=True, axis_in...]
    unnamed x102 -> x86, local copies, waits for them, and re-layouts: 12.1 us -> 16.3 us
  transfers between devices with their start and end apart: 60 -> 60, of which waited for: 31 -> 34; matrix products, arithmetic and copies ran while one was open for 23% -> 24% of each run, Pallas kernels for 36% -> 36%
where the time goes in v4:
time: 563 us; the launch traced here: 558 us
  Pallas kernels  199 us (35%)
  waiting for transfers between devices  148 us (26%)
  local copies, waits for them, and re-layouts  73.5 us (13%)
  starting transfers between devices  50.7 us (9%)
  other arithmetic  41 us (7%)
  matrix products  29.7 us (5%)
  between operations  15.4 us (3%)
    ppermute x52, waiting for transfers between devices, flip(): return lax.ppermute(values, axis, [(i, i ^ bit) for i in range(size)])  135 us
    ppermute x52, starting transfers between devices, flip(): return lax.ppermute(values, axis, [(i, i ^ bit) for i in range(size)])  50.2 us
    pallas_call x4, Pallas kernels, rows_product(): pl.pallas_call(rows_kernel, grid_spec=pltpu.PrefetchScalarGridSpec(num_sc...  36.4 us
    pallas_call x1, Pallas kernels, ffn_back(): pl.pallas_call(functools.partial(ffn_back_kernel, n_seq), grid=(n_seq,),...  28.3 us
    pallas_call x1, Pallas kernels, attend_back(): pl.pallas_call(attend_back_kernel, grid_spec=pltpu.PrefetchScalarGridSpec...  23.3 us
    pallas_call x1, Pallas kernels, attend(): pl.pallas_call(attend_kernel, grid_spec=pltpu.PrefetchScalarGridSpec(num_...  20.5 us
    pallas_call x1, Pallas kernels, ffn_up(): pl.pallas_call(ffn_up_kernel, grid=(length // FFN_ROWS,), in_specs=[pl.Bl...  19.7 us
    dot_general x4, matrix products, product_rows(): lax.dot_general(left, right, (((0,), (0,)), ((), ())), preferred_element_...  19.7 us
  transfers between devices with their start and end apart: 60, of which 34 were waited for; matrix products, arithmetic and copies ran while one was open for 24% of the time, Pallas kernels for 36%

profile of v4, /device:TPU:0, one launch (start us, length us, event | category | flops | bytes accessed | tf_op | source)
XLA Modules:
  0.0 557.9 jit_solution(2809844354063477751)
XLA Ops:
  26.4 15.0 %collective-permute-done.2 = bf16[64,1664]{1,0:T(8,128)(2,1)S(1)} collective-permute-done((bf16[64,1664]{1,0:T(8,128)(2,1)S(1)}, bf16[64,1664]{1,0:T(8,128)(2,1)S(1)}, u32[]{:S(2)}, u32[]{:S(2)}) %collective-permute-start.2) | collective-permute-done | bytes 213024 | tf_op jit(solution)/shard_map/ppermute | solution.py:57
  50.3 10.5 %collective-permute-done.6 = bf16[128,2048]{1,0:T(8,128)(2,1)S(1)} collective-permute-done((bf16[128,2048]{1,0:T(8,128)(2,1)S(1)}, bf16[128,2048]{1,0:T(8,128)(2,1)S(1)}, u32[]{:S(2)}, u32[]{:S(2)}) %collective-permute-start.6) | collective-permute-done | bytes 524320 | tf_op jit(solution)/shard_map/ppermute | solution.py:57
  69.6 18.6 %collective-permute-done.9 = bf16[256,2048]{1,0:T(8,128)(2,1)S(1)} collective-permute-done((bf16[256,2048]{1,0:T(8,128)(2,1)}, bf16[256,2048]{1,0:T(8,128)(2,1)S(1)}, u32[]{:S(2)}, u32[]{:S(2)}) %collective-permute-start.9) | collective-permute-done | bytes 1048608 | tf_op jit(solution)/shard_map/ppermute | solution.py:57
  108.1 7.7 %all-gather.12.cloned.1.call-done = bf16[2048,1664]{1,0:T(8,128)(2,1)} async-done(((bf16[256,1664]{1,0:T(8,128)(2,1)}), bf16[2048,1664]{1,0:T(8,128)(2,1)}) %all-gather.12.cloned.1.call-update) | async-done | bytes 6815760 | tf_op jit(solution)/shard_map/all_gather | solution.py:803
  115.8 6.2 %assemble.1 = (bf16[2048,1536]{1,0:T(8,128)(2,1)}, bf16[2048,128]{1,0:T(8,128)(2,1)}) custom-call(s32[1]{0:T(128)} %bitcast.me_ref, bf16[8,4,64,1664]{3,2,1,0:T(8,128)(2,1)} %bitcast.133), custom_call_target="tpu_custom_call" | custom-call | flops 2852000000 | bytes 1024 | tf_op jit(solution)/shard_map/assemble/pallas_call | solution.py:405
  135.5 10.0 %add_convert_fusion.1.q_ref.k_ref.v_ref = bf16[1024,1536]{1,0:T(8,128)(2,1)} fusion(bf16[1024,2048]{1,0:T(8,128)(2,1)S(1)} %fusion.5, bf16[2048,1536]{1,0:T(8,128)(2,1)} %get-tuple-element.137.w_ref, f32[1536]{0:T(1024)S(1)} %pad_maximum_fusion.6), kind=kOutput, calls=%fused_computation.9 | convolution fusion | flops 6445596672 | bytes 13637632 | tf_op jit(solution)/shard_map/dot_general | solution.py:31
  147.0 20.5 %attend.1 = (bf16[1024,512]{1,0:T(8,128)(2,1)}, f32[4,2,1024]{2,1,0:T(2,128)}) custom-call(s32[1]{0:T(128)} %bitcast.me_ref, bf16[1024,1536]{1,0:T(8,128)(2,1)} %add_convert_fusion.1.q_ref.k_ref.v_ref, bf16[1024,1536]{1,0:T(8,128)(2,1)} %add_convert_fusion.1.q_ref.k_ref.v_ref, bf16[1024,1536]{1,0:T(8,128)(2,1)} %add_convert_fusion.1.q_ref.k_ref.v_ref, ...), custom_call_target="tpu_custom_call" | custom-call | flops 9429999616 | bytes 1024 | tf_op jit(solution)/shard_map/attend/pallas_call | solution.py:228
  175.7 15.6 %collective-permute-done.19.refs_2_ = bf16[1024,512]{1,0:T(8,128)(2,1)} collective-permute-done((bf16[1024,512]{1,0:T(8,128)(2,1)}, bf16[1024,512]{1,0:T(8,128)(2,1)}, u32[]{:S(2)}, u32[]{:S(2)}) %collective-permute-start.19) | collective-permute-done | bytes 1048608 | tf_op jit(solution)/shard_map/ppermute | solution.py:57
  207.1 19.6 %out_norm.1 = (bf16[1024,2048]{1,0:T(8,128)(2,1)}, f32[256,2048]{1,0:T(8,128)}, f32[256,2048]{1,0:T(8,128)}, f32[256,1]{1,0:T(8,128)}) custom-call(bf16[1024,512]{1,0:T(8,128)(2,1)} %get-tuple-element.142.refs_0_, bf16[1024,512]{1,0:T(8,128)(2,1)} %collective-permute-done.18.refs_1_, bf16[1024,512]{1,0:T(8,128)(2,1)} %collective-permute-done.19.refs_2_, ...), custom_call_target="tpu_custom_call" | custom-call | flops 8924000256 | bytes 1024 | tf_op jit(solution)/shard_map/out_norm/pallas_call | solution.py:360
  226.7 19.7 %ffn_up.1 = (bf16[1024,2048]{1,0:T(8,128)(2,1)}, f32[1024,2048]{1,0:T(8,128)}) custom-call(bf16[1024,2048]{1,0:T(8,128)(2,1)} %get-tuple-element.145.n_ref.right_ref, bf16[2048,2048]{1,0:T(8,128)(2,1)} %all-gather.8.cloned.1.call-done.w_ref.up_ref, f32[1,2048]{1,0:T(1,128)} %bitcast.127), custom_call_target="tpu_custom_call" | custom-call | flops 9016000512 | bytes 1024 | tf_op jit(solution)/shard_map/ffn_up/pallas_call | solution.py:446
  246.4 8.8 %rows_product.4 = bf16[1024,2048]{1,0:T(8,128)(2,1)} custom-call(s32[1]{0:T(128)S(6)} %sub.20.side_ref, bf16[1024,2048]{1,0:T(8,128)(2,1)} %get-tuple-element.146.left_ref.hidden_ref, bf16[1024,2048]{1,0:T(8,128)(2,1)} %constant_dynamic-update-slice_fusion.7.right_ref.grad_ref), custom_call_target="tpu_custom_call" | custom-call | flops 4140000000 | bytes 1024 | tf_op jit(solution)/shard_map/rows_product/pallas_call | solution.py:135
  255.2 6.4 %copy.40 = bf16[1024,2048]{0,1:T(8,128)(2,1)} copy(bf16[1024,2048]{1,0:T(8,128)(2,1)} %copy-done.2) | data formatting | bytes 8388608 | tf_op jit(solution)/shard_map/optimization_barrier | solution.py:61
  269.4 9.4 %rows_product.5 = bf16[1024,2048]{1,0:T(8,128)(2,1)} custom-call(s32[1]{0:T(128)} %bitcast.18.side_ref, bf16[1024,2048]{1,0:T(8,128)(2,1)} %get-tuple-element.146.left_ref.hidden_ref, bf16[1024,2048]{1,0:T(8,128)(2,1)} %constant_dynamic-update-slice_fusion.7.right_ref.grad_ref, bf16[1024,2048]{1,0:T(8,128)(2,1)} %collective-permute-done.22.refs_0_), custom_call_target="tpu_custom_call" | custom-call | flops 4140000000 | bytes 1024 | tf_op jit(solution)/shard_map/rows_product/pallas_call | solution.py:135
  280.3 28.3 %ffn_back.1 = (bf16[1024,2048]{1,0:T(8,128)(2,1)}, f32[1,2048]{1,0:T(1,128)}, bf16[256,2048]{1,0:T(8,128)(2,1)}, bf16[256,2048]{1,0:T(8,128)(2,1)}, bf16[256,204...) custom-call(bf16[1024,2048]{1,0:T(8,128)(2,1)} %constant_dynamic-update-slice_fusion.7.right_ref.grad_ref, ...), custom_call_target="tpu_custom_call" | custom-call | flops 12880000000 | bytes 1024 | tf_op jit(solution)/shard_map/ffn_back/pallas_call | solution.py:535
  308.6 8.7 %rows_product.6 = bf16[1024,2048]{1,0:T(8,128)(2,1)} custom-call(s32[1]{0:T(128)S(6)} %sub.20.side_ref, bf16[1024,2048]{1,0:T(8,128)(2,1)} %get-tuple-element.155.left_ref, bf16[1024,2048]{1,0:T(8,128)(2,1)} %get-tuple-element.145.n_ref.right_ref), custom_call_target="tpu_custom_call" | custom-call | flops 4140000000 | bytes 1024 | tf_op jit(solution)/shard_map/rows_product/pallas_call | solution.py:135
  320.5 15.6 %feed_down.1 = (bf16[256,2048]{1,0:T(8,128)(2,1)}, bf16[256,2048]{1,0:T(8,128)(2,1)}, bf16[256,2048]{1,0:T(8,128)(2,1)}, bf16[128,2048]{1,0:T(8,128)(2,1)}, bf16[128,2048]{1,0:T(8,128)(2,1)}) custom-call(bf16[1024,2048]{1,0:T(8,128)(2,1)} %get-tuple-element.146.left_ref.hidden_ref, bf16[2048,2048]{1,0:T(8,128)(2,1)} %all-gather.10.cloned.1.call-done.down_ref), custom_call_target="tpu_custom_call" | custom-call | flops 7176000000 | bytes 1024 | tf_op jit(solution)/shard_map/feed_down/pallas_call | solution.py:574
  338.1 9.5 %rows_product.7 = bf16[1024,2048]{1,0:T(8,128)(2,1)} custom-call(s32[1]{0:T(128)} %bitcast.18.side_ref, bf16[1024,2048]{1,0:T(8,128)(2,1)} %get-tuple-element.155.left_ref, bf16[1024,2048]{1,0:T(8,128)(2,1)} %get-tuple-element.145.n_ref.right_ref, bf16[1024,2048]{1,0:T(8,128)(2,1)} %copy-done.4), custom_call_target="tpu_custom_call" | custom-call | flops 4140000000 | bytes 1024 | tf_op jit(solution)/shard_map/rows_product/pallas_call | solution.py:135
  353.8 10.7 %collective-permute-done.26.refs_3_ = bf16[128,2048]{1,0:T(8,128)(2,1)} collective-permute-done((bf16[128,2048]{1,0:T(8,128)(2,1)}, bf16[128,2048]{1,0:T(8,128)(2,1)}, u32[]{:S(2)}, u32[]{:S(2)}) %collective-permute-start.26) | collective-permute-done | bytes 524320 | tf_op jit(solution)/shard_map/ppermute | solution.py:57
  366.5 11.2 %norm_back.1 = (f32[256,2048]{1,0:T(8,128)}, bf16[256,2048]{1,0:T(8,128)(2,1)}, bf16[4,256,512]{2,1,0:T(8,128)(2,1)}, f32[8,2048]{1,0:T(8,128)}) custom-call(bf16[256,2048]{1,0:T(8,128)(2,1)} %get-tuple-element.161.refs_0_, bf16[256,2048]{1,0:T(8,128)(2,1)} %collective-permute-done.24.refs_1_, bf16[256,2048]{1,0:T(8,128)(2,1)} %collective-permute-done.25.refs_2_, ...), custom_call_target="tpu_custom_call" | custom-call | flops 5059999744 | bytes 1024 | tf_op jit(solution)/shard_map/norm_back/pallas_call | solution.py:669
  382.6 6.7 %collective-permute-done.30 = bf16[256,512]{1,0:T(8,128)(2,1)S(1)} collective-permute-done((bf16[256,512]{1,0:T(8,128)(2,1)S(1)}, bf16[256,512]{1,0:T(8,128)(2,1)S(1)}, u32[]{:S(2)}, u32[]{:S(2)}) %collective-permute-start.30) | collective-permute-done | bytes 262176 | tf_op jit(solution)/shard_map/ppermute | solution.py:57
  396.0 23.3 %attend_back.1.grad_ref = bf16[1024,1536]{1,0:T(8,128)(2,1)} custom-call(s32[1]{0:T(128)} %bitcast.me_ref, bf16[1024,1536]{1,0:T(8,128)(2,1)} %add_convert_fusion.1.q_ref.k_ref.v_ref, bf16[1024,1536]{1,0:T(8,128)(2,1)} %add_convert_fusion.1.q_ref.k_ref.v_ref, bf16[1024,1536]{1,0:T(8,128)(2,1)} %add_convert_fusion.1.q_ref.k_ref.v_ref, ...), custom_call_target="tpu_custom_call" | custom-call | flops 10764000256 | bytes 1024 | tf_op jit(solution)/shard_map/attend_back/pallas_call | solution.py:301
  419.4 6.4 %convolution_convert_fusion = bf16[1024,1536]{1,0:T(8,128)(2,1)S(1)} fusion(bf16[1024,1024]{0,1:T(8,128)(2,1)} %get-tuple-element.188, bf16[1024,1536]{1,0:T(8,128)(2,1)} %attend_back.1.grad_ref), kind=kOutput, calls=%fused_computation.12 | convolution fusion | flops 3222798336 | bytes 8388608 | tf_op jit(solution)/shard_map/dot_general | solution.py:39
  444.8 15.7 %qkv_back.1 = (f32[8,2048]{1,0:T(8,128)}, f32[8,1536]{1,0:T(8,128)}, bf16[256,2048]{1,0:T(8,128)(2,1)}, bf16[256,2048]{1,0:T(8,128)(2,1)}, bf16[256,2048]{1,0:T(...) custom-call(bf16[1024,1536]{1,0:T(8,128)(2,1)} %attend_back.1.grad_ref, ...), custom_call_target="tpu_custom_call" | custom-call | flops 7038000128 | bytes 1024 | tf_op jit(solution)/shard_map/qkv_back/pallas_call | solution.py:611
  477.1 8.1 %collective-permute-done.41 = bf16[256,2048]{1,0:T(8,128)(2,1)} collective-permute-done((bf16[256,2048]{1,0:T(8,128)(2,1)}, bf16[256,2048]{1,0:T(8,128)(2,1)}, u32[]{:S(2)}, u32[]{:S(2)}) %collective-permute-start.41) | collective-permute-done | bytes 1048608 | tf_op jit(solution)/shard_map/ppermute | solution.py:57
  (336 shorter events, 230.1 us)
Async XLA Ops:
  7.2 55.8 %all-gather.6.cloned.1.call-start = ((), (), s32[]{:S(2)}) async-start(), calls=%async_computation.4 | async-start | bytes 2359296 | tf_op jit(solution)/shard_map/all_gather | solution.py:802
  7.9 107.9 %all-gather.12.cloned.1.call-start = ((), (), s32[]{:S(2)}) async-start(), calls=%async_computation.11 | async-start | bytes 7667712 | tf_op jit(solution)/shard_map/all_gather | solution.py:803
  8.0 37.0 %collective-permute-start.4 = (bf16[256,2048]{1,0:T(8,128)(2,1)}, bf16[256,2048]{1,0:T(8,128)(2,1)S(1)}, u32[]{:S(2)}, u32[]{:S(2)}) collective-permute-start(bf16[256,2048]{1,0:T(8,128)(2,1)} %bitcast.105), channel_id=1, source_target_pairs={{0,16},{8,24},{16,0},{24,8},{1,17},{9,25},{17,1},{25,9},{2,18},{10... | collective-permute-start | bytes 3145736 | tf_op jit(solution)/shard_map/ppermute | solution.py:57
  11.0 34.0 %collective-permute-start.3 = (bf16[256,2048]{1,0:T(8,128)(2,1)}, bf16[256,2048]{1,0:T(8,128)(2,1)}, u32[]{:S(2)}, u32[]{:S(2)}) collective-permute-start(bf16[256,2048]{1,0:T(8,128)(2,1)} %bitcast.106), channel_id=1, source_target_pairs={{0,8},{8,0},{16,24},{24,16},{1,9},{9,1},{17,25},{25,17},{2,10},{10... | collective-permute-start | bytes 3145736 | tf_op jit(solution)/shard_map/ppermute | solution.py:57
  46.3 180.4 %all-gather.8.cloned.1.call-start = ((), (), s32[]{:S(2)}) async-start(), calls=%async_computation.5 | async-start | bytes 9437184 | tf_op jit(solution)/shard_map/all_gather | solution.py:804
  47.0 233.2 %all-gather.10.cloned.1.call-start = ((), (), s32[]{:S(2)}) async-start(), calls=%async_computation.6 | async-start | bytes 9437184 | tf_op jit(solution)/shard_map/all_gather | solution.py:805
  65.8 23.4 %collective-permute-start.7 = (bf16[256,2048]{1,0:T(8,128)(2,1)}, bf16[256,2048]{1,0:T(8,128)(2,1)}, u32[]{:S(2)}, u32[]{:S(2)}) collective-permute-start(bf16[256,2048]{1,0:T(8,128)(2,1)} %constant_dynamic-slice_fusion.10), channel_id=1, source_target_pairs={{0,8},{8,0},{16,24},{24,16},{1,9},{9,1},{17,25},{25,17},{2,10},{10... | collective-permute-start | bytes 3145736 | tf_op jit(solution)/shard_map/ppermute | solution.py:57
  66.5 369.8 %reduce-scatter.7.cloned.1.call-start = ((), (), s32[]{:S(2)}) async-start(), calls=%async_computation.8 | async-start | bytes 5242880 | tf_op jit(solution)/shard_map/reduce_scatter | solution.py:169
  104.1 25.8 %collective-permute-start.15 = (bf16[256,2048]{1,0:T(8,128)(2,1)S(1)}, bf16[256,2048]{1,0:T(8,128)(2,1)}, u32[]{:S(2)}, u32[]{:S(2)}) collective-permute-start(bf16[256,2048]{1,0:T(8,128)(2,1)S(1)} %multiply_convert_fusion), channel_id=1, source_target_pairs={{0,16},{8,24},{16,0},{24,8},{1,17},{9,25},{17,1},{25,9},{2,18},{10... | collective-permute-start | bytes 3145736 | tf_op jit(solution)/shard_map/ppermute | solution.py:57
  106.0 25.4 %collective-permute-start.14 = (bf16[256,2048]{1,0:T(8,128)(2,1)S(1)}, bf16[256,2048]{1,0:T(8,128)(2,1)}, u32[]{:S(2)}, u32[]{:S(2)}) collective-permute-start(bf16[256,2048]{1,0:T(8,128)(2,1)S(1)} %multiply_convert_fusion), channel_id=1, source_target_pairs={{0,8},{8,0},{16,24},{24,16},{1,9},{9,1},{17,25},{25,17},{2,10},{10... | collective-permute-start | bytes 3145736 | tf_op jit(solution)/shard_map/ppermute | solution.py:57
  167.5 23.8 %collective-permute-start.19 = (bf16[1024,512]{1,0:T(8,128)(2,1)}, bf16[1024,512]{1,0:T(8,128)(2,1)}, u32[]{:S(2)}, u32[]{:S(2)}) collective-permute-start(bf16[1024,512]{1,0:T(8,128)(2,1)} %get-tuple-element.142.refs_0_), channel_id=1, source_target_pairs={{0,16},{8,24},{16,0},{24,8},{1,17},{9,25},{17,1},{25,9},{2,18},{10... | collective-permute-start | bytes 3145736 | tf_op jit(solution)/shard_map/ppermute | solution.py:57
  169.0 25.0 %collective-permute-start.18 = (bf16[1024,512]{1,0:T(8,128)(2,1)}, bf16[1024,512]{1,0:T(8,128)(2,1)}, u32[]{:S(2)}, u32[]{:S(2)}) collective-permute-start(bf16[1024,512]{1,0:T(8,128)(2,1)} %get-tuple-element.142.refs_0_), channel_id=1, source_target_pairs={{0,8},{8,0},{16,24},{24,16},{1,9},{9,1},{17,25},{25,17},{2,10},{10... | collective-permute-start | bytes 3145736 | tf_op jit(solution)/shard_map/ppermute | solution.py:57
  280.2 157.0 %reduce-scatter.5.cloned.1.call-start = ((), (), s32[]{:S(2)}) async-start(), calls=%async_computation.7 | async-start | bytes 5242880 | tf_op jit(solution)/shard_map/reduce_scatter | solution.py:169
  317.5 30.2 %collective-permute-start.24 = (bf16[256,2048]{1,0:T(8,128)(2,1)}, bf16[256,2048]{1,0:T(8,128)(2,1)}, u32[]{:S(2)}, u32[]{:S(2)}) collective-permute-start(bf16[256,2048]{1,0:T(8,128)(2,1)} %get-tuple-element.162), channel_id=1, source_target_pairs={{0,8},{8,0},{16,24},{24,16},{1,9},{9,1},{17,25},{25,17},{2,10},{10... | collective-permute-start | bytes 3145736 | tf_op jit(solution)/shard_map/ppermute | solution.py:57
  319.1 32.2 %collective-permute-start.25 = (bf16[256,2048]{1,0:T(8,128)(2,1)}, bf16[256,2048]{1,0:T(8,128)(2,1)}, u32[]{:S(2)}, u32[]{:S(2)}) collective-permute-start(bf16[256,2048]{1,0:T(8,128)(2,1)} %get-tuple-element.163), channel_id=1, source_target_pairs={{0,16},{8,24},{16,0},{24,8},{1,17},{9,25},{17,1},{25,9},{2,18},{10... | collective-permute-start | bytes 3145736 | tf_op jit(solution)/shard_map/ppermute | solution.py:57
  347.7 152.7 %reduce-scatter.9.cloned.1.call-start = ((), (), s32[]{:S(2)}) async-start(), calls=%async_computation.9 | async-start | bytes 3932160 | tf_op jit(solution)/shard_map/reduce_scatter | solution.py:169
  394.1 25.3 %collective-permute-start.32 = (bf16[256,2048]{1,0:T(8,128)(2,1)S(1)}, bf16[256,2048]{1,0:T(8,128)(2,1)S(1)}, u32[]{:S(2)}, u32[]{:S(2)}) collective-permute-start(bf16[256,2048]{1,0:T(8,128)(2,1)S(1)} %copy-done.15), channel_id=1, source_target_pairs={{0,16},{8,24},{16,0},{24,8},{1,17},{9,25},{17,1},{25,9},{2,18},{10... | collective-permute-start | bytes 3145736 | tf_op jit(solution)/shard_map/ppermute | solution.py:57
  394.9 24.5 %collective-permute-start.31 = (bf16[256,2048]{1,0:T(8,128)(2,1)S(1)}, bf16[256,2048]{1,0:T(8,128)(2,1)S(1)}, u32[]{:S(2)}, u32[]{:S(2)}) collective-permute-start(bf16[256,2048]{1,0:T(8,128)(2,1)S(1)} %copy-done.15), channel_id=1, source_target_pairs={{0,8},{8,0},{16,24},{24,16},{1,9},{9,1},{17,25},{25,17},{2,10},{10... | collective-permute-start | bytes 3145736 | tf_op jit(solution)/shard_map/ppermute | solution.py:57
  437.3 105.4 %reduce-scatter.11.cloned.1.call-start = ((), (), s32[]{:S(2)}) async-start(), calls=%async_computation.10 | async-start | bytes 1392640 | tf_op jit(solution)/shard_map/reduce_scatter | solution.py:169
  441.9 26.1 %collective-permute-start.34 = (bf16[128,2048]{1,0:T(8,128)(2,1)}, bf16[128,2048]{1,0:T(8,128)(2,1)}, u32[]{:S(2)}, u32[]{:S(2)}) collective-permute-start(bf16[128,2048]{1,0:T(8,128)(2,1)} %slice.200), channel_id=1, source_target_pairs={{0,8},{8,0},{16,24},{24,16},{1,9},{9,1},{17,25},{25,17},{2,10},{10... | collective-permute-start | bytes 1572872 | tf_op jit(solution)/shard_map/ppermute | solution.py:57
  460.5 24.7 %collective-permute-start.41 = (bf16[256,2048]{1,0:T(8,128)(2,1)}, bf16[256,2048]{1,0:T(8,128)(2,1)}, u32[]{:S(2)}, u32[]{:S(2)}) collective-permute-start(bf16[256,2048]{1,0:T(8,128)(2,1)} %get-tuple-element.197), channel_id=1, source_target_pairs={{0,8},{8,0},{16,24},{24,16},{1,9},{9,1},{17,25},{25,17},{2,10},{10... | collective-permute-start | bytes 3145736 | tf_op jit(solution)/shard_map/ppermute | solution.py:57
  461.0 24.2 %collective-permute-start.42 = (bf16[256,2048]{1,0:T(8,128)(2,1)}, bf16[256,2048]{1,0:T(8,128)(2,1)}, u32[]{:S(2)}, u32[]{:S(2)}) collective-permute-start(bf16[256,2048]{1,0:T(8,128)(2,1)} %get-tuple-element.198), channel_id=1, source_target_pairs={{0,16},{8,24},{16,0},{24,8},{1,17},{9,25},{17,1},{25,9},{2,18},{10... | collective-permute-start | bytes 3145736 | tf_op jit(solution)/shard_map/ppermute | solution.py:57
  485.2 37.4 %collective-permute-start.43 = (bf16[256,2048]{1,0:T(8,128)(2,1)}, bf16[256,2048]{1,0:T(8,128)(2,1)}, u32[]{:S(2)}, u32[]{:S(2)}) collective-permute-start(bf16[256,2048]{1,0:T(8,128)(2,1)} %get-tuple-element.207), channel_id=1, source_target_pairs={{0,8},{8,0},{16,24},{24,16},{1,9},{9,1},{17,25},{25,17},{2,10},{10... | collective-permute-start | bytes 3145736 | tf_op jit(solution)/shard_map/ppermute | solution.py:57
  486.9 35.7 %collective-permute-start.44 = (bf16[256,2048]{1,0:T(8,128)(2,1)}, bf16[256,2048]{1,0:T(8,128)(2,1)S(1)}, u32[]{:S(2)}, u32[]{:S(2)}) collective-permute-start(bf16[256,2048]{1,0:T(8,128)(2,1)} %get-tuple-element.208), channel_id=1, source_target_pairs={{0,16},{8,24},{16,0},{24,8},{1,17},{9,25},{17,1},{25,9},{2,18},{10... | collective-permute-start | bytes 3145736 | tf_op jit(solution)/shard_map/ppermute | solution.py:57
  (73 other events, 803.2 us)
Sparse Core Ops, SparseCore 0:
  9.6 31.7 all-gather.5
  46.4 69.3 all-gather.11
  117.4 80.6 all-gather.7
  199.6 80.5 all-gather.9
  282.3 75.2 reduce-scatter.6
  359.9 77.2 reduce-scatter.4
  439.5 60.7 reduce-scatter.8
  510.3 28.1 reduce-scatter.10
